TPU v7x, 32 devices: a whole 2x2x4 slice. The times are simulated.
32 devices in a mesh: grp: 16 (over z, x, core), patch: 2 (over y).
Axes of the slice: x: 2, y: 2, z: 4, core: 2. Of those that a mesh axis runs over, the one named last changes fastest.
Arguments:
- tokens: bfloat16 [12288, 1152], P(('grp', 'patch')), parts along dimension 0, may hold values from -6 to 6
- projection_weight: bfloat16 [1152, 3456], replicated, may hold values from -0.1875 to 0.1875
- shift_term: float32 [1152], replicated, may hold values from -3 to 3
- scale_term: float32 [1152], replicated, may hold values from -3 to 3
- query_gain: float32 [72], replicated, may hold values from 0.1 to 1.9
- key_gain: float32 [72], replicated, may hold values from 0.1 to 1.9
- stale_keys: bfloat16 [12288, 1152], P(('grp', 'patch')), parts along dimension 0, may hold values from -6 to 6
- stale_values: bfloat16 [12288, 1152], P(('grp', 'patch')), parts along dimension 0, may hold values from -6 to 6
- stale_output: bfloat16 [12288, 1152], P(('grp', 'patch')), parts along dimension 0, may hold values from -3 to 3
- refreshed: int32 [768], P('grp'), parts along dimension 0, may hold values from 0 to 1, as said below
Outputs:
- attended: bfloat16 [12288, 1152], P(('grp', 'patch')), parts along dimension 0
There are 16 independent parts, one for each index of `grp`. A program takes and returns all parts, laid end to end along the dimension named above; an argument that names none is the same for every part. Nothing has to cross between parts.
Inputs may be any that keep to these rules, and one draw needn't show every extreme that they name: Exactly 16 of the 48 entries are 1; in every prompt some device has all 16 of its tiles refreshed.
All inputs are finite; a program needn't handle non-finite values.
Results may differ from a plain program's by a relative error of at most 0.0045.
Values may be sent and summed in bfloat16 or wider, within the bound.
No kernel may reach another device: no remote copies, remote signals or barrier semaphores. Data moves between devices by JAX's collectives and lax.ppermute only.
A program may use at most 128 MiB of HBM per device.

v0:
```python
import math

import jax
import jax.numpy as jnp
from jax import lax
from jax.sharding import PartitionSpec as P

H = 16
TILE = 16


epsilon = 1e-06


def modulate(row_block, shift_term, scale_term):
    values = row_block.astype(jnp.float32)
    center = values - jnp.mean(values, axis=-1, keepdims=True)
    spread = jnp.mean(center * center, axis=-1, keepdims=True)
    normed = center / jnp.sqrt(spread + epsilon)
    return (normed * (1.0 + scale_term) + shift_term).astype(jnp.bfloat16)


def head_norm(row_block, gain_vector, head_count):
    values = row_block.astype(jnp.float32).reshape(row_block.shape[0], head_count, -1)
    normed = values / jnp.sqrt(jnp.mean(values * values, axis=-1, keepdims=True) + epsilon)
    return (normed * gain_vector).astype(jnp.bfloat16).reshape(row_block.shape[0], -1)


def block_size(row_total, row_unit):
    multiple = row_total // row_unit
    chosen = 1
    for candidate in range(1, multiple + 1):
        if multiple % candidate == 0 and candidate * row_unit <= 1024:
            chosen = candidate
    return chosen * row_unit


def partial_terms(queries, key_rows, values, head_count):
    query_count = queries.shape[0]
    model_width = queries.shape[1]
    head_size = model_width // head_count
    factor = 1.0 / math.sqrt(head_size)
    query_heads = queries.reshape(query_count, head_count, head_size)
    key_heads = key_rows.reshape(key_rows.shape[0], head_count, head_size)
    value_heads = values.reshape(values.shape[0], head_count, head_size)
    scores = (
        jnp.einsum("qhd,khd->hqk", query_heads, key_heads, preferred_element_type=jnp.float32)
        * factor
    )
    weights = jnp.exp(scores)
    totals = jnp.sum(weights, axis=2).T
    numerator = jnp.einsum(
        "hqk,khd->qhd",
        weights.astype(jnp.bfloat16),
        value_heads,
        preferred_element_type=jnp.float32,
    )
    return (numerator.reshape(query_count, model_width), totals)


def own_terms(every_query, key_rows, values, head_count, row_unit):
    row_total = every_query.shape[0]
    stride = block_size(row_total, row_unit)

    def advance(turn_index, inner_sums):
        offset = turn_index * stride
        query_block = lax.dynamic_slice_in_dim(every_query, offset, stride, 0)
        numerator, totals = partial_terms(query_block, key_rows, values, head_count)
        return (
            lax.dynamic_update_slice_in_dim(inner_sums[0], numerator, offset, 0),
            lax.dynamic_update_slice_in_dim(inner_sums[1], totals, offset, 0),
        )

    starting = (
        jnp.zeros((row_total, key_rows.shape[1]), jnp.float32),
        jnp.zeros((row_total, head_count), jnp.float32),
    )
    return lax.fori_loop(0, row_total // stride, advance, starting)


def attend(queries, own_keys, own_values, head_count):
    query_count = queries.shape[0]
    model_width = queries.shape[1]
    every_query = lax.all_gather(queries, "patch", axis=0, tiled=True)
    numerator, totals = own_terms(every_query, own_keys, own_values, head_count, query_count)
    numerator, totals = (
        lax.psum_scatter(
            numerator.astype(jnp.bfloat16), "patch", scatter_dimension=0, tiled=True
        ).astype(jnp.float32),
        lax.psum_scatter(
            totals.astype(jnp.bfloat16), "patch", scatter_dimension=0, tiled=True
        ).astype(jnp.float32),
    )
    fresh_heads = numerator.reshape(query_count, head_count, -1) / totals[:, :, None]
    return fresh_heads.reshape(query_count, model_width).astype(jnp.bfloat16)


def body(
    tokens,
    projection_weight,
    shift_term,
    scale_term,
    query_gain,
    key_gain,
    stale_keys,
    stale_values,
    stale_output,
    refreshed,
):
    model_width = tokens.shape[1]
    head_count = H
    own_rows = tokens.shape[0]
    own_tiles = own_rows // TILE
    patch_count = lax.axis_size("patch")
    my_index = lax.axis_index("patch")
    share_tiles = own_tiles // 3
    most_tiles = min(own_tiles, share_tiles * patch_count)
    tile_grid = refreshed.reshape(patch_count, own_tiles)
    my_tiles = lax.dynamic_index_in_dim(tile_grid, my_index, 0, keepdims=False)
    picked = jnp.nonzero(my_tiles, size=most_tiles, fill_value=0)[0].astype(jnp.int32)
    token_tiles = tokens.reshape(own_tiles, TILE, model_width)
    chosen = token_tiles[picked].reshape(most_tiles * TILE, model_width)
    hidden = modulate(chosen, shift_term, scale_term)
    projected = jnp.dot(hidden, projection_weight, preferred_element_type=jnp.float32)
    query_new = projected[:, :model_width].astype(jnp.bfloat16)
    key_new = (
        projected[:, model_width : 2 * model_width]
        .astype(jnp.bfloat16)
        .reshape(most_tiles, TILE, model_width)
    )
    value_new = (
        projected[:, 2 * model_width :].astype(jnp.bfloat16).reshape(most_tiles, TILE, model_width)
    )
    position = jnp.maximum(jnp.cumsum(my_tiles) - 1, 0)
    fresh_tile = (my_tiles > 0)[:, None, None]
    keys_all = jnp.where(
        fresh_tile, key_new[position], stale_keys.reshape(own_tiles, TILE, model_width)
    ).reshape(own_rows, model_width)
    values_all = jnp.where(
        fresh_tile, value_new[position], stale_values.reshape(own_tiles, TILE, model_width)
    ).reshape(own_rows, model_width)
    own_keys = head_norm(keys_all, key_gain, head_count)
    queries = head_norm(query_new, query_gain, head_count)
    fresh_rows = attend(queries, own_keys, values_all, head_count)
    fresh_tiles = fresh_rows.reshape(most_tiles, TILE, model_width)
    merged = jnp.where(
        fresh_tile, fresh_tiles[position], stale_output.reshape(own_tiles, TILE, model_width)
    )
    return merged.reshape(own_rows, model_width)


def solution(mesh):
    in_specs = (
        P(("grp", "patch"), None),
        P(),
        P(),
        P(),
        P(),
        P(),
        P(("grp", "patch"), None),
        P(("grp", "patch"), None),
        P(("grp", "patch"), None),
        P("grp"),
    )
    out_specs = P(("grp", "patch"), None)
    return jax.shard_map(body, mesh=mesh, in_specs=in_specs, out_specs=out_specs, check_vma=False)
```

profile of v0, /device:TPU:0, one launch (start us, length us, event | category | flops | bytes accessed | tf_op | source)
XLA Modules:
  0.0 102.9 jit_solution(11285227140400040629)
XLA Ops:
  6.6 0.8 reshape.206
  7.4 0.6 fusion.25
  8.3 0.7 scatter_custom_fusion
  9.1 0.8 fusion.24
  9.9 0.6 gather_fusion
  11.2 0.3 fusion.17
  11.5 5.8 %convolution_convert_fusion = bf16[256,3456]{1,0:T(8,128)(2,1)S(1)} fusion(bf16[256,1152]{1,0:T(8,128)(2,1)S(1)} %fusion.17, bf16[1152,3456]{1,0:T(8,128)(2,1)} %param.11), kind=kOutput, calls=%fused_computation.10 | convolution fusion | flops 2039316480 | bytes 10321920 | tf_op jit(solution)/shard_map/dot_general | solution.py:124
  17.3 1.2 %copy-done.2 = bf16[256,3456]{1,0:T(8,128)(2,1)} copy-done((bf16[256,3456]{1,0:T(8,128)(2,1)}, bf16[256,3456]{1,0:T(8,128)(2,1)S(1)}, u32[]{:S(2)}) %copy-start.2) | copy-done | bytes 1769496
  18.6 0.4 copy.40
  19.2 0.4 copy.41
  19.8 2.1 %fusion.12 = bf16[256,1152]{1,0:T(8,128)(2,1)} fusion(f32[256,1152]{1,0:T(8,128)S(1)} %copy.41, f32[1152]{0:T(1024)S(1)} %mul.54, bf16[256,3456]{1,0:T(8,128)(2,1)} %copy-done.2), kind=kLoop, calls=%fused_computation.19 | loop fusion | flops 1179648 | bytes 2363904 | tf_op jit(solution)/shard_map/convert_element_type | solution.py:26
  22.0 1.3 %fusion.30 = (bf16[256,1152]{1,0:T(8,128)(2,1)S(1)}, bf16[256,1152]{1,0:T(8,128)(2,1)S(1)}) fusion(bf16[256,3456]{1,0:T(8,128)(2,1)} %copy-done.2), kind=kLoop, calls=%fused_computation.60 | loop fusion | bytes 2359296 | tf_op jit(solution)/shard_map/slice | solution.py:132
  23.6 0.7 gather_fusion.2
  24.3 2.6 %fusion.19 = f32[384,1152]{1,0:T(8,128)} fusion(bf16[384,1152]{1,0:T(8,128)(2,1)} %param.16, bf16[24,16,1152]{2,1,0:T(8,128)(2,1)S(1)} %gather_fusion.2, pred[384]{0:T(512)(128)(4,1)S(1)} %broadcast_in_dim.29), kind=kLoop, calls=%fused_computation.31 | loop fusion | flops 884736 | bytes 3539328 | tf_op jit(solution)/shard_map/reshape | solution.py:24
  26.9 2.2 %copy.43 = f32[384,1152]{0,1:T(8,128)S(1)} copy(f32[384,1152]{1,0:T(8,128)} %fusion.19) | data formatting | bytes 3538944 | tf_op jit(solution)/shard_map/reshape | solution.py:24
  29.1 1.6 %gather_fusion.1 = bf16[24,16,1152]{2,1,0:T(8,128)(2,1)} fusion(bf16[16,16,1152]{2,1,0:T(8,128)(2,1)S(1)} %bitcast.50, s32[1024]{0:T(1024)S(1)} %pad_clamp_fusion), kind=kCustom, calls=%fused_computation.1 | custom fusion | bytes 1769568 | tf_op jit(solution)/shard_map/gather | solution.py:140
  30.7 4.7 %gather.20 = bf16[384,16,72]{2,1,0:T(8,128)(2,1)} reshape(bf16[24,16,1152]{2,1,0:T(8,128)(2,1)} %gather_fusion.1) | data formatting | bytes 1769472 | tf_op jit(solution)/shard_map/gather | solution.py:140
  35.4 1.7 %copy.38 = bf16[384,1152]{0,1:T(8,128)(2,1)S(1)} copy(bf16[384,1152]{1,0:T(8,128)(2,1)} %param.17) | data formatting | bytes 1769472 | tf_op args[7]
  37.1 2.0 %copy.39 = bf16[384,16,72]{2,1,0:T(8,128)(2,1)} copy(bf16[384,16,72]{0,2,1:T(8,128)(2,1)S(1)} %bitcast.52) | data formatting | bytes 1769472 | tf_op jit(solution)/shard_map/reshape | solution.py:140
  39.3 1.2 %copy-done.1 = bf16[384,16,72]{2,1,0:T(8,128)(2,1)S(1)} copy-done((bf16[384,16,72]{2,1,0:T(8,128)(2,1)S(1)}, bf16[384,16,72]{2,1,0:T(8,128)(2,1)}, u32[]{:S(2)}) %copy-start.1) | copy-done | bytes 884760
  40.5 3.3 %broadcast_select_fusion = bf16[384,16,72]{2,1,0:T(8,128)(2,1)} fusion(bf16[384,16,72]{2,1,0:T(8,128)(2,1)S(1)} %copy-done.1, bf16[384,16,72]{2,1,0:T(8,128)(2,1)} %copy.39, pred[384]{0:T(512)(128)(4,1)S(1)} %broadcast_in_dim.29), kind=kLoop, calls=%fused_computation.14 | loop fusion | flops 442368 | bytes 2654592 | tf_op jit(solution)/shard_map/jit(_where)/select_n | solution.py:139
  43.8 3.8 %all-gather.2.cloned.1.call-done = bf16[512,1152]{1,0:T(8,128)(2,1)} async-done(((bf16[256,1152]{1,0:T(8,128)(2,1)}), bf16[512,1152]{1,0:T(8,128)(2,1)}) %all-gather.2.cloned.1.call-update) | async-done | bytes 1179664 | tf_op jit(solution)/shard_map/all_gather | solution.py:84
  47.5 2.4 %copy.42 = bf16[512,1152]{0,1:T(8,128)(2,1)} copy(bf16[512,1152]{1,0:T(8,128)(2,1)} %all-gather.2.cloned.1.call-done) | data formatting | bytes 2359296 | tf_op jit(solution)/shard_map/all_gather | solution.py:84
  49.9 8.7 %fusion = (bf16[16,512]{1,0:T(8,128)(2,1)}, f32[16,512,384]{1,2,0:T(8,128)}) fusion(bf16[512,16,72]{0,2,1:T(8,128)(2,1)} %bitcast.53, f32[384,16,72]{0,2,1:T(8,128)S(1)} %bitcast.45, f32[72]{0:T(128)S(1)} %copy-done.7, f32[384,16]{0,1:T(8,128)S(1)} %add_sqrt_fusion), kind=kOutput, calls=%fused_computation.6 | convolution fusion | flops 460595200 | bytes 15573280 | tf_op jit(solution)/shard_map/while/body/eval_jaxpr/qhd,khd->hqk/dot_general | solution.py:47
  58.9 8.5 %fusion.6 = bf16[16,72,512]{2,1,0:T(8,128)(2,1)} fusion(f32[16,512,384]{1,2,0:T(8,128)} %get-tuple-element.30, bf16[384,16,72]{2,1,0:T(8,128)(2,1)} %broadcast_select_fusion), kind=kOutput, calls=%fused_computation.15 | convolution fusion | flops 459866112 | bytes 14647296 | tf_op jit(solution)/shard_map/while/body/eval_jaxpr/hqk,khd->qhd/dot_general | solution.py:52
  67.4 1.3 %reduce-scatter.5.cloned.1.call-done = bf16[256,16]{0,1:T(8,128)(2,1)} async-done(((bf16[512,16]{0,1:T(8,128)(2,1)}), bf16[256,16]{0,1:T(8,128)(2,1)}) %reduce-scatter.5.cloned.1.call-update) | async-done | bytes 8208 | tf_op jit(solution)/shard_map/reduce_scatter | solution.py:90
  68.7 0.7 convert_element_type.86
  69.4 23.4 %reduce-scatter.3.cloned.1.call-done = bf16[256,1152]{0,1:T(8,128)(2,1)} async-done(((bf16[512,1152]{0,1:T(8,128)(2,1)}), bf16[256,1152]{0,1:T(8,128)(2,1)}) %reduce-scatter.3.cloned.1.call-update) | async-done | bytes 589840 | tf_op jit(solution)/shard_map/reduce_scatter | solution.py:87
  92.9 1.2 %fusion.13 = bf16[256,1152]{0,1:T(8,128)(2,1)S(1)} fusion(bf16[256,1152]{0,1:T(8,128)(2,1)} %reduce-scatter.3.cloned.1.call-done, f32[256,16]{0,1:T(8,128)S(1)} %convert_element_type.86), kind=kLoop, calls=%fused_computation.21 | loop fusion | flops 884736 | bytes 1196032 | tf_op jit(solution)/shard_map/convert_element_type | solution.py:95
  94.1 0.3 copy.46
  94.4 0.7 gather_fusion.3
  95.2 1.2 %bitcast_select_fusion = bf16[384,1152]{1,0:T(8,128)(2,1)} fusion(bf16[384,1152]{1,0:T(8,128)(2,1)S(1)} %copy-done.3, bf16[24,16,1152]{2,1,0:T(8,128)(2,1)S(1)} %gather_fusion.3, pred[384]{0:T(512)(128)(4,1)S(1)} %broadcast_in_dim.29), kind=kLoop, calls=%fused_computation.29 | loop fusion | flops 442368 | bytes 2654592 | tf_op jit(solution)/shard_map/jit(_where)/select_n | solution.py:146
  (49 shorter events, 2.6 us)
Async XLA Ops:
  6.5 3.3 %copy-start = (bf16[384,1152]{1,0:T(8,128)(2,1)S(1)}, bf16[384,1152]{1,0:T(8,128)(2,1)}, u32[]{:S(2)}) copy-start(bf16[384,1152]{1,0:T(8,128)(2,1)} %param.10) | copy-start | bytes 2654212
  6.5 4.6 %copy-start.5 = (f32[1152]{0:T(1024)S(1)}, f32[1152]{0:T(1024)}, u32[]{:S(2)}) copy-start(f32[1152]{0:T(1024)} %param.13) | copy-start | bytes 13828
  6.5 4.6 %copy-start.4 = (f32[1152]{0:T(1024)S(1)}, f32[1152]{0:T(1024)}, u32[]{:S(2)}) copy-start(f32[1152]{0:T(1024)} %param.12) | copy-start | bytes 13828
  6.5 41.0 %all-gather.2.cloned.1.call-start = ((), (), s32[]{:S(2)}) async-start(), calls=%async_computation.2 | async-start | bytes 1769472 | tf_op jit(solution)/shard_map/all_gather | solution.py:84
  17.3 1.2 %copy-start.2 = (bf16[256,3456]{1,0:T(8,128)(2,1)}, bf16[256,3456]{1,0:T(8,128)(2,1)S(1)}, u32[]{:S(2)}) copy-start(bf16[256,3456]{1,0:T(8,128)(2,1)S(1)} %convolution_convert_fusion) | copy-start | bytes 5308420
  19.1 0.7 copy-start.6
  21.9 46.8 %reduce-scatter.5.cloned.1.call-start = ((), (), s32[]{:S(2)}) async-start(), calls=%async_computation.4 | async-start | bytes 24576 | tf_op jit(solution)/shard_map/reduce_scatter | solution.py:90
  39.1 1.4 %copy-start.1 = (bf16[384,16,72]{2,1,0:T(8,128)(2,1)S(1)}, bf16[384,16,72]{2,1,0:T(8,128)(2,1)}, u32[]{:S(2)}) copy-start(bf16[384,16,72]{2,1,0:T(8,128)(2,1)} %gather.20) | copy-start | bytes 2654212
  43.8 6.2 %copy-start.7 = (f32[72]{0:T(128)S(1)}, f32[72]{0:T(128)}, u32[]{:S(2)}) copy-start(f32[72]{0:T(128)} %param.15) | copy-start | bytes 868
  58.6 34.2 %reduce-scatter.3.cloned.1.call-start = ((), (), s32[]{:S(2)}) async-start(), calls=%async_computation.3 | async-start | bytes 1769472 | tf_op jit(solution)/shard_map/reduce_scatter | solution.py:87
  94.0 1.2 %copy-start.3 = (bf16[384,1152]{1,0:T(8,128)(2,1)S(1)}, bf16[384,1152]{1,0:T(8,128)(2,1)}, u32[]{:S(2)}) copy-start(bf16[384,1152]{1,0:T(8,128)(2,1)} %param.18) | copy-start | bytes 2654212
Sparse Core Ops, SparseCore 0:
  22.0 25.4 all-gather.1
  58.8 9.9 reduce-scatter.4
  71.0 21.8 reduce-scatter.2
where the time goes:
time: 104 us; the launch traced here: 103 us
  waiting for transfers between devices  28.5 us (27%)
  local copies, waits for them, and re-layouts  23.2 us (22%)
  matrix products  23 us (22%)
  other arithmetic  14.6 us (14%)
  between operations  13.3 us (13%)
    reduce_scatter x1, waiting for transfers between devices, attend(): lax.psum_scatter(numerator.astype(jnp.bfloat16), 'patch', scatter_dimensi...  23.4 us
    dot_general x1, matrix products, partial_terms(): jnp.einsum('qhd,khd->hqk', query_heads, key_heads, preferred_element_type...  8.67 us
    dot_general x1, matrix products, partial_terms(): jnp.einsum('hqk,khd->qhd', weights.astype(jnp.bfloat16), value_heads, pre...  8.54 us
    gather x2, local copies, waits for them, and re-layouts, body(): value_new[position]  6.26 us
    dot_general x1, matrix products, body(): jnp.dot(hidden, projection_weight, preferred_element_type=jnp.float32)  5.78 us
    unnamed x17, local copies, waits for them, and re-layouts  4.56 us
    all_gather x1, waiting for transfers between devices, attend(): every_query = lax.all_gather(queries, 'patch', axis=0, tiled=True)  3.75 us
    select_n x1, other arithmetic, body(): jnp.where(fresh_tile, value_new[position], stale_values.reshape(own_tiles...  3.29 us
  transfers between devices with their start and end apart: 3, of which 3 were waited for; matrix products, arithmetic and copies ran while one was open for 29% of the time, Pallas kernels for 0%

commit v1 on v0

--- a/solution.py
+++ b/solution.py
@@ -1,8 +1,11 @@
+import functools
 import math
 
 import jax
 import jax.numpy as jnp
 from jax import lax
+from jax.experimental import pallas as pl
+from jax.experimental.pallas import tpu as pltpu
 from jax.sharding import PartitionSpec as P
 
 H = 16
@@ -149,6 +152,499 @@
     return merged.reshape(own_rows, model_width)
 
 
+LANES = 128
+
+
+def ceil_to(amount, unit):
+    return -(-amount // unit) * unit
+
+
+def lane_window(start, stop):
+    return start // LANES * LANES, ceil_to(stop, LANES)
+
+
+def pair_plan(head_count, own_rows, fresh_rows, chunks):
+    ratio = 2 * own_rows // fresh_rows
+    shipped = head_count // (1 + ratio)
+    asked = head_count - shipped
+    if shipped % (2 * chunks) or asked % (2 * chunks):
+        return None
+    if asked * fresh_rows != shipped * 2 * own_rows:
+        return None
+    if own_rows % LANES or fresh_rows % LANES:
+        return None
+    a, s = asked // chunks, shipped // chunks
+    return [
+        (
+            tuple(range(c * a, (c + 1) * a)),
+            tuple(range(asked + c * s, asked + (c + 1) * s)),
+        )
+        for c in range(chunks)
+    ]
+
+
+def pair_body(
+    plan,
+    tokens,
+    projection_weight,
+    shift_term,
+    scale_term,
+    query_gain,
+    key_gain,
+    stale_keys,
+    stale_values,
+    stale_output,
+    refreshed,
+):
+    N, D = tokens.shape
+    HD = query_gain.shape[0]
+    heads = D // HD
+    tiles = N // TILE
+    patch_count = lax.axis_size("patch")
+    R = tiles * patch_count // 3 * TILE
+    HP = ceil_to(HD + 1, 16)
+    f32, bf16 = jnp.float32, jnp.bfloat16
+    factor = math.log2(math.e) / math.sqrt(HD)
+    asked = [h for qs, _ in plan for h in qs]
+    shipped = [h for _, ks in plan for h in ks]
+    hq, hk = len(plan[0][0]), len(plan[0][1])
+    qrows, krows = hq * HD, 2 * hk * HD
+    xrows = qrows * (R // LANES)
+    trows = ceil_to(hq, 8)
+    rrows = xrows + ceil_to(2 * trows * (R // LANES), 16)
+    VM = pl.BlockSpec(memory_space=pltpu.VMEM)
+    ANY = pl.BlockSpec(memory_space=pl.ANY)
+    SM = pl.BlockSpec(memory_space=pltpu.SMEM)
+    params = pltpu.CompilerParams()
+    DMA = pltpu.SemaphoreType.DMA
+    vm = pltpu.VMEM
+
+    def sds(rows, cols, dtype):
+        return jax.ShapeDtypeStruct((rows, cols), dtype)
+
+    def is_fresh(flags):
+        base = lax.axis_index("patch") * tiles
+        return lax.fori_loop(0, tiles, lambda t, s: s + flags[base + t], 0) > 0
+
+    def each_tile(flags, action):
+        base = lax.axis_index("patch") * tiles
+
+        def step(t, seen):
+            flag = flags[base + t]
+
+            @pl.when(flag > 0)
+            def _():
+                action(pl.multiple_of(t * TILE, TILE), pl.multiple_of(seen * TILE, TILE))
+
+            return seen + flag
+
+        lax.fori_loop(0, tiles, step, 0)
+
+    def column(gain):
+        row = jnp.broadcast_to(gain[...].reshape(1, HD), (HD, HD))
+        eye = lax.broadcasted_iota(jnp.int32, (HD, HD), 0) == lax.broadcasted_iota(
+            jnp.int32, (HD, HD), 1
+        )
+        return jnp.sum(jnp.where(eye, row, 0.0), axis=1, keepdims=True)
+
+    def turn(source, width, target):
+        for j in range(width // LANES):
+            target[LANES * j : LANES * (j + 1), :] = source[:, LANES * j : LANES * (j + 1)].astype(f32).T
+
+    def normed(part, gain):
+        spread = jnp.mean(part * part, axis=0, keepdims=True)
+        return part * lax.rsqrt(spread + epsilon) * gain
+
+    def padded(part, fill):
+        extra = jnp.full((HP - HD, part.shape[1]), fill, f32)
+        return jnp.concatenate([part, extra], axis=0).astype(bf16)
+
+    def put(target, row, stride, value):
+        for b in range(value.shape[1] // LANES):
+            target[stride * b + row : stride * b + row + value.shape[0], :] = value[
+                :, LANES * b : LANES * (b + 1)
+            ]
+
+    def take(source, row, stride, count, width):
+        return jnp.concatenate(
+            [source[stride * b + row : stride * b + row + count, :] for b in range(width // LANES)],
+            axis=1,
+        ).astype(f32)
+
+    def pack_queries(projected_turned, low, qs, gain, target):
+        for i in range(0, len(qs), 2):
+            two = [
+                normed(projected_turned[HD * h - low : HD * (h + 1) - low, :], gain)
+                for h in qs[i : i + 2]
+            ]
+            put(target, HD * i, qrows, jnp.concatenate(two, axis=0).astype(bf16))
+
+    def pack_shipped(kbuf, vbuf, turned, low, ks, gain, target):
+        width = kbuf.shape[1]
+        turn(kbuf, width, turned)
+        for i in range(0, len(ks), 2):
+            two = [normed(turned[HD * h - low : HD * (h + 1) - low, :], gain) for h in ks[i : i + 2]]
+            put(target, HD * i, krows, jnp.concatenate(two, axis=0).astype(bf16))
+        turn(vbuf, width, turned)
+        for i in range(0, len(ks), 2):
+            two = [turned[HD * h - low : HD * (h + 1) - low, :] for h in ks[i : i + 2]]
+            put(target, HD * (len(ks) + i), krows, jnp.concatenate(two, axis=0).astype(bf16))
+
+    def score(queries, keys, values):
+        scores = lax.dot_general(
+            keys, queries, (((0,), (0,)), ((), ())), preferred_element_type=f32
+        )
+        weights = jnp.exp2(scores * factor).astype(bf16)
+        return jnp.dot(values, weights, preferred_element_type=f32)
+
+    qlow0, qhigh0 = lane_window(HD * plan[0][0][0], HD * (plan[0][0][-1] + 1))
+    qlow1, qhigh1 = lane_window(HD * (hq if len(plan) > 1 else shipped[0]), D)
+    swindow = [lane_window(HD * ks[0], HD * (ks[-1] + 1)) for _, ks in plan]
+    swidth = max(b - a for a, b in swindow)
+
+    def front(flags, tok, w, shift, scale, gq, gk, sk, sv, x0, hid, xbuf, wbuf, qt, kbuf, vbuf, st, sems):
+        fresh = is_fresh(flags)
+
+        @pl.when(fresh)
+        def _():
+            wcopy = pltpu.make_async_copy(w.at[:, qlow0:qhigh0], wbuf, sems.at[0])
+            each_tile(
+                flags,
+                lambda t, s: pltpu.make_async_copy(
+                    tok.at[pl.ds(t, TILE), :], xbuf.at[pl.ds(s, TILE), :], sems.at[1]
+                ).start(),
+            )
+            wcopy.start()
+            pltpu.make_async_copy(tok.at[0:R, :], xbuf, sems.at[1]).wait()
+            up = 1.0 + scale[...].reshape(1, D)
+            down = shift[...].reshape(1, D)
+            for i in range(0, R, 64):
+                x = xbuf[i : i + 64, :].astype(f32)
+                center = x - jnp.mean(x, axis=1, keepdims=True)
+                spread = jnp.mean(center * center, axis=1, keepdims=True)
+                hid[i : i + 64, :] = (center * lax.rsqrt(spread + epsilon) * up + down).astype(bf16)
+            wcopy.wait()
+            projected = jnp.dot(hid[...], wbuf[...], preferred_element_type=f32).astype(bf16)
+            turn(projected, qhigh0 - qlow0, qt)
+            pack_queries(qt, qlow0, plan[0][0], column(gq), x0)
+
+        @pl.when(jnp.logical_not(fresh))
+        def _():
+            low, high = swindow[0]
+            kcopy = pltpu.make_async_copy(sk.at[:, low:high], kbuf, sems.at[0])
+            vcopy = pltpu.make_async_copy(sv.at[:, low:high], vbuf, sems.at[1])
+            kcopy.start()
+            vcopy.start()
+            kcopy.wait()
+            vcopy.wait()
+            pack_shipped(kbuf, vbuf, st, low, plan[0][1], column(gk), x0)
+
+    width0 = swindow[0][1] - swindow[0][0]
+    x0, hidden = pl.pallas_call(
+        front,
+        out_shape=(sds(xrows, LANES, bf16), sds(R, D, bf16)),
+        in_specs=[SM, ANY, ANY, VM, VM, VM, VM, ANY, ANY],
+        out_specs=(VM, VM),
+        scratch_shapes=[
+            vm((R, D), bf16),
+            vm((D, qhigh0 - qlow0), bf16),
+            vm((qhigh0 - qlow0, R), f32),
+            vm((N, width0), bf16),
+            vm((N, width0), bf16),
+            vm((width0, N), f32),
+            DMA((2,)),
+        ],
+        compiler_params=params,
+        name="front",
+    )(refreshed, tokens, projection_weight, shift_term, scale_term, query_gain, key_gain, stale_keys, stale_values)
+
+    swap = [(0, 1), (1, 0)]
+    sent = [x0]
+    got = [lax.ppermute(x0, "patch", swap)]
+
+    more = len(plan) > 1
+
+    def second(flags, hid, w, gq, gk, sk, sv, *rest):
+        x1 = rest[0] if more else None
+        qx, wbuf, qt, kbuf, vbuf, st, sems = rest[1:] if more else rest
+        fresh = is_fresh(flags)
+
+        @pl.when(fresh)
+        def _():
+            wcopy = pltpu.make_async_copy(w.at[:, qlow1:qhigh1], wbuf, sems.at[0])
+            wcopy.start()
+            wcopy.wait()
+            projected = jnp.dot(hid[...], wbuf[...], preferred_element_type=f32).astype(bf16)
+            turn(projected, qhigh1 - qlow1, qt)
+            gain = column(gq)
+            if more:
+                pack_queries(qt, qlow1, plan[1][0], gain, x1)
+            for i, h in enumerate(shipped):
+                part = normed(qt[HD * h - qlow1 : HD * (h + 1) - qlow1, :], gain)
+                qx[HP * i : HP * (i + 1), :] = padded(part, 0.0)
+
+        if more:
+
+            @pl.when(jnp.logical_not(fresh))
+            def _():
+                low, high = swindow[1]
+                kcopy = pltpu.make_async_copy(sk.at[:, low:high], kbuf, sems.at[0])
+                vcopy = pltpu.make_async_copy(sv.at[:, low:high], vbuf, sems.at[1])
+                kcopy.start()
+                vcopy.start()
+                kcopy.wait()
+                vcopy.wait()
+                pack_shipped(kbuf, vbuf, st, low, plan[1][1], column(gk), x1)
+
+    width1 = swindow[-1][1] - swindow[-1][0]
+    outs = [sds(len(shipped) * HP, R, bf16)]
+    if more:
+        outs = [sds(xrows, LANES, bf16)] + outs
+    outs = pl.pallas_call(
+        second,
+        out_shape=tuple(outs),
+        in_specs=[SM, VM, ANY, VM, VM, ANY, ANY],
+        out_specs=(VM,) * len(outs),
+        scratch_shapes=[
+            vm((D, qhigh1 - qlow1), bf16),
+            vm((qhigh1 - qlow1, R), f32),
+            vm((N, width1), bf16),
+            vm((N, width1), bf16),
+            vm((width1, N), f32),
+            DMA((2,)),
+        ],
+        compiler_params=params,
+        name="second",
+    )(refreshed, hidden, projection_weight, query_gain, key_gain, stale_keys, stale_values)
+    if more:
+        sent.append(outs[0])
+        got.append(lax.ppermute(outs[0], "patch", swap))
+    qx = outs[-1]
+
+    def third(flags, hid, w, gk, sk, sv, so, kt, vt, out, kall, vall, new, wk, wv, turned, sems):
+        fresh = is_fresh(flags)
+        ocopy = pltpu.make_async_copy(so, out, sems.at[0])
+        kcopy = pltpu.make_async_copy(sk, kall, sems.at[1])
+        vcopy = pltpu.make_async_copy(sv, vall, sems.at[2])
+        kcopy.start()
+        vcopy.start()
+
+        @pl.when(fresh)
+        def _():
+            wkcopy = pltpu.make_async_copy(w.at[:, D : 2 * D], wk, sems.at[3])
+            wvcopy = pltpu.make_async_copy(w.at[:, 2 * D : 3 * D], wv, sems.at[4])
+            wkcopy.start()
+            wvcopy.start()
+            kcopy.wait()
+            wkcopy.wait()
+            new[...] = jnp.dot(hid[...], wk[...], preferred_element_type=f32).astype(bf16)
+
+            def merge_keys(t, s):
+                kall[pl.ds(t, TILE), :] = new[pl.ds(s, TILE), :]
+
+            each_tile(flags, merge_keys)
+            vcopy.wait()
+            wvcopy.wait()
+            new[...] = jnp.dot(hid[...], wv[...], preferred_element_type=f32).astype(bf16)
+
+            def merge_values(t, s):
+                vall[pl.ds(t, TILE), :] = new[pl.ds(s, TILE), :]
+
+            each_tile(flags, merge_values)
+
+        @pl.when(jnp.logical_not(fresh))
+        def _():
+            kcopy.wait()
+            vcopy.wait()
+
+        ocopy.start()
+        gain = column(gk)
+        turn(kall, D, turned)
+        for h in range(heads):
+            kt[HP * h : HP * (h + 1), :] = padded(normed(turned[HD * h : HD * (h + 1), :], gain), 0.0)
+        turn(vall, D, turned)
+        for h in range(heads):
+            vt[HP * h : HP * (h + 1), :] = padded(turned[HD * h : HD * (h + 1), :], 1.0)
+        ocopy.wait()
+
+    kt, vt, held = pl.pallas_call(
+        third,
+        out_shape=(sds(heads * HP, N, bf16), sds(heads * HP, N, bf16), sds(N, D, bf16)),
+        in_specs=[SM, VM, ANY, VM, ANY, ANY, ANY],
+        out_specs=(VM, VM, ANY),
+        scratch_shapes=[
+            vm((N, D), bf16),
+            vm((N, D), bf16),
+            vm((R, D), bf16),
+            vm((D, D), bf16),
+            vm((D, D), bf16),
+            vm((D, N), f32),
+            DMA((5,)),
+        ],
+        compiler_params=params,
+        name="third",
+    )(refreshed, hidden, projection_weight, key_gain, stale_keys, stale_values, stale_output)
+
+    def query_pair(x, i):
+        two = take(x, HD * i, qrows, 2 * HD, R)
+        return [padded(two[:HD], 0.0), padded(two[HD:], 0.0)]
+
+    def keys_of(kt, h):
+        return kt[HP * h : HP * (h + 1), :]
+
+    def answer(x, kt, vt, qs, target):
+        totals = []
+        for i in range(0, hq, 2):
+            both = []
+            for q, h in zip(query_pair(x, i), qs[i : i + 2]):
+                terms = score(q, keys_of(kt, h), keys_of(vt, h))
+                both.append(terms[:HD])
+                totals.append(terms[HD : HD + 1])
+            put(target, HD * i, qrows, jnp.concatenate(both, axis=0).astype(bf16))
+        if trows > hq:
+            totals.append(jnp.zeros((trows - hq, R), f32))
+        total = jnp.concatenate(totals, axis=0)
+        high = total.astype(bf16)
+        low = (total - high.astype(f32)).astype(bf16)
+        pieces = [
+            piece[:, LANES * b : LANES * (b + 1)].astype(f32)
+            for piece in (high, low)
+            for b in range(R // LANES)
+        ]
+        spare = rrows - xrows - len(pieces) * trows
+        if spare:
+            pieces.append(jnp.zeros((spare, LANES), f32))
+        target[xrows:, :] = jnp.concatenate(pieces, axis=0).astype(bf16)
+
+    def own_terms_of(x, kt, vt, qs, target):
+        for i in range(0, hq, 2):
+            for k, (q, h) in enumerate(zip(query_pair(x, i), qs[i : i + 2])):
+                target[HP * (i + k) : HP * (i + k + 1), :] = score(q, keys_of(kt, h), keys_of(vt, h))
+
+    answers, own = [], []
+    for c, (qs, _) in enumerate(plan):
+
+        def reply(flags, xr, kt, vt, *rest, c=c, qs=qs):
+            fresh = is_fresh(flags)
+            if c:
+                xs, r, mine = rest
+            else:
+                (r,) = rest
+
+            @pl.when(jnp.logical_not(fresh))
+            def _():
+                answer(xr, kt, vt, qs, r)
+
+            if c:
+
+                @pl.when(fresh)
+                def _():
+                    own_terms_of(xs, kt, vt, plan[c - 1][0], mine)
+
+        extra = [sent[c - 1]] if c else []
+        res = pl.pallas_call(
+            reply,
+            out_shape=(sds(rrows, LANES, bf16),) + ((sds(hq * HP, R, f32),) if c else ()),
+            in_specs=[SM, VM, VM, VM] + [VM] * len(extra),
+            out_specs=(VM,) * (1 + len(extra)),
+            compiler_params=params,
+            name="reply",
+        )(refreshed, got[c], kt, vt, *extra)
+        answers.append(lax.ppermute(res[0], "patch", swap))
+        if c:
+            own.append(res[1])
+
+    def rest_of(flags, xs, kt, vt, qx, *rest):
+        xr = rest[: len(plan)]
+        mine, full = rest[len(plan) :]
+
+        @pl.when(is_fresh(flags))
+        def _():
+            own_terms_of(xs, kt, vt, plan[-1][0], mine)
+            for c, (_, ks) in enumerate(plan):
+                for i in range(0, hk, 2):
+                    ktwo = take(xr[c], HD * i, krows, 2 * HD, N)
+                    vtwo = take(xr[c], HD * (hk + i), krows, 2 * HD, N)
+                    for k in range(2):
+                        h = ks[i + k]
+                        at = shipped.index(h)
+                        q = qx[HP * at : HP * (at + 1), :]
+                        terms = score(q, keys_of(kt, h), keys_of(vt, h)) + score(
+                            q,
+                            padded(ktwo[HD * k : HD * (k + 1)], 0.0),
+                            padded(vtwo[HD * k : HD * (k + 1)], 1.0),
+                        )
+                        full[HD * at : HD * (at + 1), :] = terms[:HD] / terms[HD : HD + 1]
+
+    mine, full = pl.pallas_call(
+        rest_of,
+        out_shape=(sds(hq * HP, R, f32), sds(len(shipped) * HD, R, f32)),
+        in_specs=[SM, VM, VM, VM, VM] + [VM] * len(plan),
+        out_specs=(VM, VM),
+        compiler_params=params,
+        name="rest",
+    )(refreshed, sent[-1], kt, vt, qx, *got)
+    own.append(mine)
+
+    def last(flags, full, *rest):
+        mine = rest[: len(plan)]
+        theirs = rest[len(plan) : 2 * len(plan)]
+        _, out, turned, rows, sem = rest[2 * len(plan) :]
+
+        @pl.when(is_fresh(flags))
+        def _():
+            turned[HD * shipped[0] :, :] = full[...]
+            blocks = R // LANES
+            for c, (qs, _) in enumerate(plan):
+                tail = theirs[c][xrows:, :].astype(f32)
+                parts = [tail[trows * k : trows * (k + 1)] for k in range(2 * blocks)]
+                total = jnp.concatenate(
+                    [parts[b] + parts[blocks + b] for b in range(blocks)], axis=1
+                )
+                for i in range(0, hq, 2):
+                    two = take(theirs[c], HD * i, qrows, 2 * HD, R)
+                    for k in range(2):
+                        h = i + k
+                        terms = mine[c][HP * h : HP * (h + 1), :]
+                        top = terms[:HD] + two[HD * k : HD * (k + 1)]
+                        bottom = terms[HD : HD + 1] + total[h : h + 1]
+                        turned[HD * qs[h] : HD * (qs[h] + 1), :] = top / bottom
+            for j in range(D // LANES):
+                rows[:, LANES * j : LANES * (j + 1)] = turned[LANES * j : LANES * (j + 1), :].T.astype(bf16)
+            each_tile(
+                flags,
+                lambda t, s: pltpu.make_async_copy(
+                    rows.at[pl.ds(s, TILE), :], out.at[pl.ds(t, TILE), :], sem
+                ).start(),
+            )
+            pltpu.make_async_copy(rows, out.at[0:R, :], sem).wait()
+
+    operands = (refreshed, full, *own, *answers, held)
+    return pl.pallas_call(
+        last,
+        out_shape=sds(N, D, bf16),
+        in_specs=[SM] + [VM] * (1 + 2 * len(plan)) + [ANY],
+        out_specs=ANY,
+        input_output_aliases={len(operands) - 1: 0},
+        scratch_shapes=[vm((D, R), f32), vm((R, D), bf16), DMA],
+        compiler_params=params,
+        name="last",
+    )(*operands)
+
+
+def pick_plan(mesh, tokens_shape, width):
+    patch = mesh.shape["patch"]
+    own_rows = tokens_shape // (mesh.shape["grp"] * patch)
+    own_tiles = own_rows // TILE
+    fresh_tiles = own_tiles * patch // 3
+    if patch != 2 or fresh_tiles > own_tiles:
+        return None
+    return pair_plan(H, own_rows, fresh_tiles * TILE, CHUNKS)
+
+
+CHUNKS = 2
+
+
 def solution(mesh):
     in_specs = (
         P(("grp", "patch"), None),
@@ -163,4 +659,12 @@
         P("grp"),
     )
     out_specs = P(("grp", "patch"), None)
-    return jax.shard_map(body, mesh=mesh, in_specs=in_specs, out_specs=out_specs, check_vma=False)
+
+    def whole(*arrays):
+        plan = pick_plan(mesh, arrays[0].shape[0], arrays[0].shape[1])
+        inner = body if plan is None else functools.partial(pair_body, plan)
+        return jax.shard_map(
+            inner, mesh=mesh, in_specs=in_specs, out_specs=out_specs, check_vma=False
+        )(*arrays)
+
+    return whole

time: 104 us -> 67.8 us (0.65)
  Pallas kernels: 0 us -> 59 us
  waiting for transfers between devices: 28.5 us -> 0.05 us
  matrix products: 23 us -> 0 us
  local copies, waits for them, and re-layouts: 23.2 us -> 2.07 us
  other arithmetic: 14.6 us -> 0 us
  between operations: 13.3 us -> 0.07 us
  starting transfers between devices: 0.27 us -> 5.78 us
    pallas_call x0 -> x7, Pallas kernels: none -> 59 us  [the longest x1 35.5 us: pair_body(): pl.pallas_call(third, out_shape=(sds(heads * HP, N, bf16), sds(heads * HP...]
    reduce_scatter x2 -> x0, waiting for transfers between devices: 24.7 us -> none  [the longest x1 23.4 us: attend(): lax.psum_scatter(numerator.astype(jnp.bfloat16), 'patch', scatter_dimensi...]
    dot_general x3 -> x0, matrix products: 23 us -> none  [the longest x1 8.67 us: partial_terms(): jnp.einsum('qhd,khd->hqk', query_heads, key_heads, preferred_element_type...]
    gather x5 -> x0, local copies, waits for them, and re-layouts: 8.27 us -> none  [the longest x2 6.26 us: body(): value_new[position]]
    ppermute x0 -> x4, starting transfers between devices: none -> 5.78 us  [the longest x2 3.69 us: pair_body(): answers.append(lax.ppermute(res[0], 'patch', swap))]
    select_n x5 -> x0, other arithmetic: 5.37 us -> none  [the longest x1 3.29 us: body(): jnp.where(fresh_tile, value_new[position], stale_values.reshape(own_tiles...]
    reshape x3 -> x0, local copies, waits for them, and re-layouts: 4.97 us -> none  [the longest x1 2.19 us: head_norm(): row_block.astype(jnp.float32).reshape(row_block.shape[0], head_count, -1)]
    convert_element_type x5 -> x0, other arithmetic: 4.23 us -> none  [the longest x1 2.06 us: head_norm(): (normed * gain_vector).astype(jnp.bfloat16).reshape(row_block.shape[0], -1)]
  transfers between devices with their start and end apart: 3 -> 4, of which waited for: 3 -> 0; matrix products, arithmetic and copies ran while one was open for 29% -> 0% of each run, Pallas kernels for 0% -> 71%
where the time goes in v1:
time: 67.8 us; the launch traced here: 67 us
  Pallas kernels  59 us (87%)
  starting transfers between devices  5.78 us (9%)
  local copies, waits for them, and re-layouts  2.07 us (3%)
    pallas_call x1, Pallas kernels, pair_body(): pl.pallas_call(third, out_shape=(sds(heads * HP, N, bf16), sds(heads * HP...  35.5 us
    pallas_call x2, Pallas kernels, pair_body(): pl.pallas_call(reply, out_shape=(sds(rrows, LANES, bf16),) + ((sds(hq * H...  6.67 us
    pallas_call x1, Pallas kernels, pair_body(): pl.pallas_call(rest_of, out_shape=(sds(hq * HP, R, f32), sds(len(shipped)...  5.61 us
    pallas_call x1, Pallas kernels, pair_body(): pl.pallas_call(second, out_shape=tuple(outs), in_specs=[SM, VM, ANY, VM,...  4.37 us
    pallas_call x1, Pallas kernels, pair_body(): pl.pallas_call(front, out_shape=(sds(xrows, LANES, bf16), sds(R, D, bf16)...  4.16 us
    ppermute x2, starting transfers between devices, pair_body(): answers.append(lax.ppermute(res[0], 'patch', swap))  3.69 us
    pallas_call x1, Pallas kernels, pair_body(): pl.pallas_call(last, out_shape=sds(N, D, bf16), in_specs=[SM] + [VM] * (1...  2.67 us
    unnamed x10, local copies, waits for them, and re-layouts  2.07 us
  transfers between devices with their start and end apart: 4, of which 0 were waited for; matrix products, arithmetic and copies ran while one was open for 0% of the time, Pallas kernels for 71%

profile of v1, /device:TPU:0, one launch (start us, length us, event | category | flops | bytes accessed | tf_op | source)
XLA Modules:
  0.0 67.0 jit_solution(4198957086223167456)
XLA Ops:
  0.0 4.2 %front.1 = (bf16[864,128]{1,0:T(8,128)(2,1)}, bf16[256,1152]{1,0:T(8,128)(2,1)}) custom-call(s32[48]{0:T(128)} %flags.13, bf16[384,1152]{1,0:T(8,128)(2,1)} %tok.1, bf16[1152,3456]{1,0:T(8,128)(2,1)} %w.5, f32[1152]{0:T(1024)} %shift.1, f32[1152]{0:T(1024)} %scale.1, f32[72]{0:T(128)} %gq.3, f32[72]{0:T(128)} %gk.5, bf16[384,1152]{1,0:T(8,128)(2,1)} %sk.5, ...), custom_call_target="tpu_custom_call" | custom-call | tf_op jit(solution)/shard_map/front/pallas_call | solution.py:343
  4.2 0.0 copy-start.4
  4.2 4.4 %second.1 = (bf16[864,128]{1,0:T(8,128)(2,1)}, bf16[320,256]{1,0:T(8,128)(2,1)}) custom-call(s32[48]{0:T(128)} %flags.13, bf16[256,1152]{1,0:T(8,128)(2,1)} %get-tuple-element.16.hid, bf16[1152,3456]{1,0:T(8,128)(2,1)} %w.5, f32[72]{0:T(128)} %gq.3, f32[72]{0:T(128)} %gk.5, bf16[384,1152]{1,0:T(8,128)(2,1)} %sk.5, bf16[384,1152]{1,0:T(8,128)(2,1)} %sv.5), custom_call_target="tpu_custom_call" | custom-call | tf_op jit(solution)/shard_map/second/pallas_call | solution.py:403
  8.6 0.9 %collective-permute-start.1 = (bf16[864,128]{1,0:T(8,128)(2,1)}, bf16[864,128]{1,0:T(8,128)(2,1)S(1)}, u32[]{:S(2)}, u32[]{:S(2)}) collective-permute-start(bf16[864,128]{1,0:T(8,128)(2,1)} %get-tuple-element.17.xs), channel_id=1, source_target_pairs={{0,1},{1,0},{2,3},{3,2},{4,5},{5,4},{6,7},{7,6},{8,9},{9,8},{10,11... | collective-permute-start | bytes 663560 | tf_op jit(solution)/shard_map/ppermute | solution.py:421
  9.5 0.0 copy-done.4
  9.5 1.2 %collective-permute-start = (bf16[864,128]{1,0:T(8,128)(2,1)S(1)}, bf16[864,128]{1,0:T(8,128)(2,1)S(1)}, u32[]{:S(2)}, u32[]{:S(2)}) collective-permute-start(bf16[864,128]{1,0:T(8,128)(2,1)S(1)} %copy-done.4), channel_id=1, source_target_pairs={{0,1},{1,0},{2,3},{3,2},{4,5},{5,4},{6,7},{7,6},{8,9},{9,8},{10,11... | collective-permute-start | bytes 663560 | tf_op jit(solution)/shard_map/ppermute | solution.py:363
  10.6 35.5 %third.1 = (bf16[1280,384]{1,0:T(8,128)(2,1)}, bf16[1280,384]{1,0:T(8,128)(2,1)}, bf16[384,1152]{1,0:T(8,128)(2,1)}) custom-call(s32[48]{0:T(128)} %flags.13, bf16[256,1152]{1,0:T(8,128)(2,1)} %get-tuple-element.16.hid, bf16[1152,3456]{1,0:T(8,128)(2,1)} %w.5, f32[72]{0:T(128)} %gk.5, bf16[384,1152]{1,0:T(8,128)(2,1)} %sk.5, bf16[384,1152]{1,0:T(8,128)(2,1)} %sv.5, ...), custom_call_target="tpu_custom_call" | custom-call | tf_op jit(solution)/shard_map/third/pallas_call | solution.py:470
  46.2 0.0 collective-permute-done.1.rest_1_.xr
  46.2 0.0 copy-start
  46.2 0.7 copy-done
  46.9 4.3 %reply.2 = (bf16[896,128]{1,0:T(8,128)(2,1)}, f32[480,256]{1,0:T(8,128)}) custom-call(s32[48]{0:T(128)} %flags.13, bf16[864,128]{1,0:T(8,128)(2,1)} %copy-done, bf16[1280,384]{1,0:T(8,128)(2,1)} %get-tuple-element.18.kt, bf16[1280,384]{1,0:T(8,128)(2,1)} %get-tuple-element.19.vt, bf16[864,128]{1,0:T(8,128)(2,1)} %get-tuple-element.21.rest_0_), custom_call_target="tpu_custom_call" | custom-call | tf_op jit(solution)/shard_map/reply/pallas_call | solution.py:545
  51.1 0.0 collective-permute-start.3
  51.1 0.0 collective-permute-done.rest_0_.xr
  51.1 0.0 copy-start.1
  51.2 0.7 %copy-done.1 = bf16[864,128]{1,0:T(8,128)(2,1)} copy-done((bf16[864,128]{1,0:T(8,128)(2,1)}, bf16[864,128]{1,0:T(8,128)(2,1)S(1)}, u32[]{:S(2)}) %copy-start.1) | copy-done | bytes 221208
  51.8 2.4 %reply.3 = bf16[896,128]{1,0:T(8,128)(2,1)} custom-call(s32[48]{0:T(128)} %flags.13, bf16[864,128]{1,0:T(8,128)(2,1)} %copy-done.1, bf16[1280,384]{1,0:T(8,128)(2,1)} %get-tuple-element.18.kt, bf16[1280,384]{1,0:T(8,128)(2,1)} %get-tuple-element.19.vt), custom_call_target="tpu_custom_call" | custom-call | tf_op jit(solution)/shard_map/reply/pallas_call | solution.py:545
  54.2 3.7 %collective-permute-start.2 = (bf16[896,128]{1,0:T(8,128)(2,1)}, bf16[896,128]{1,0:T(8,128)(2,1)S(1)}, u32[]{:S(2)}, u32[]{:S(2)}) collective-permute-start(bf16[896,128]{1,0:T(8,128)(2,1)} %reply.3), channel_id=1, source_target_pairs={{0,1},{1,0},{2,3},{3,2},{4,5},{5,4},{6,7},{7,6},{8,9},{9,8},{10,11... | collective-permute-start | bytes 688136 | tf_op jit(solution)/shard_map/ppermute | solution.py:553
  57.9 5.6 %rest.1 = (f32[480,256]{1,0:T(8,128)}, f32[288,256]{1,0:T(8,128)}) custom-call(s32[48]{0:T(128)} %flags.13, bf16[864,128]{1,0:T(8,128)(2,1)} %get-tuple-element.17.xs, bf16[1280,384]{1,0:T(8,128)(2,1)} %get-tuple-element.18.kt, bf16[1280,384]{1,0:T(8,128)(2,1)} %get-tuple-element.19.vt, bf16[320,256]{1,0:T(8,128)(2,1)} %get-tuple-element.20.qx, ...), custom_call_target="tpu_custom_call" | custom-call | tf_op jit(solution)/shard_map/rest/pallas_call | solution.py:579
  63.5 0.0 collective-permute-done.3.rest_3_
  63.5 0.0 copy-start.2
  63.5 0.0 collective-permute-done.2.rest_2_
  63.6 0.0 copy-start.3
  63.6 0.6 copy-done.2
  64.2 0.1 copy-done.3
  64.3 2.7 %last.1 = bf16[384,1152]{1,0:T(8,128)(2,1)} custom-call(s32[48]{0:T(128)} %flags.13, f32[288,256]{1,0:T(8,128)} %get-tuple-element.22.full, f32[480,256]{1,0:T(8,128)} %get-tuple-element.23.rest_0_, f32[480,256]{1,0:T(8,128)} %get-tuple-element.24.rest_1_, bf16[896,128]{1,0:T(8,128)(2,1)} %copy-done.3, ...), custom_call_target="tpu_custom_call", output_to_operand_aliasing={{}: (6, {})} | custom-call | tf_op jit(solution)/shard_map/last/pallas_call | solution.py:623
Async XLA Ops:
  4.2 5.3 %copy-start.4 = (bf16[864,128]{1,0:T(8,128)(2,1)S(1)}, bf16[864,128]{1,0:T(8,128)(2,1)}, u32[]{:S(2)}) copy-start(bf16[864,128]{1,0:T(8,128)(2,1)} %get-tuple-element.21.rest_0_) | copy-start | bytes 663556
  8.6 37.6 %collective-permute-start.1 = (bf16[864,128]{1,0:T(8,128)(2,1)}, bf16[864,128]{1,0:T(8,128)(2,1)S(1)}, u32[]{:S(2)}, u32[]{:S(2)}) collective-permute-start(bf16[864,128]{1,0:T(8,128)(2,1)} %get-tuple-element.17.xs), channel_id=1, source_target_pairs={{0,1},{1,0},{2,3},{3,2},{4,5},{5,4},{6,7},{7,6},{8,9},{9,8},{10,11... | collective-permute-start | bytes 663560 | tf_op jit(solution)/shard_map/ppermute | solution.py:421
  9.5 41.7 %collective-permute-start = (bf16[864,128]{1,0:T(8,128)(2,1)S(1)}, bf16[864,128]{1,0:T(8,128)(2,1)S(1)}, u32[]{:S(2)}, u32[]{:S(2)}) collective-permute-start(bf16[864,128]{1,0:T(8,128)(2,1)S(1)} %copy-done.4), channel_id=1, source_target_pairs={{0,1},{1,0},{2,3},{3,2},{4,5},{5,4},{6,7},{7,6},{8,9},{9,8},{10,11... | collective-permute-start | bytes 663560 | tf_op jit(solution)/shard_map/ppermute | solution.py:363
  46.2 0.7 %copy-start = (bf16[864,128]{1,0:T(8,128)(2,1)}, bf16[864,128]{1,0:T(8,128)(2,1)S(1)}, u32[]{:S(2)}) copy-start(bf16[864,128]{1,0:T(8,128)(2,1)S(1)} %collective-permute-done.1.rest_1_.xr) | copy-start | bytes 663556
  51.1 12.4 %collective-permute-start.3 = (bf16[896,128]{1,0:T(8,128)(2,1)}, bf16[896,128]{1,0:T(8,128)(2,1)S(1)}, u32[]{:S(2)}, u32[]{:S(2)}) collective-permute-start(bf16[896,128]{1,0:T(8,128)(2,1)} %get-tuple-element.25), channel_id=1, source_target_pairs={{0,1},{1,0},{2,3},{3,2},{4,5},{5,4},{6,7},{7,6},{8,9},{9,8},{10,11... | collective-permute-start | bytes 688136 | tf_op jit(solution)/shard_map/ppermute | solution.py:553
  51.1 0.7 %copy-start.1 = (bf16[864,128]{1,0:T(8,128)(2,1)}, bf16[864,128]{1,0:T(8,128)(2,1)S(1)}, u32[]{:S(2)}) copy-start(bf16[864,128]{1,0:T(8,128)(2,1)S(1)} %collective-permute-done.rest_0_.xr) | copy-start | bytes 663556
  54.2 9.3 %collective-permute-start.2 = (bf16[896,128]{1,0:T(8,128)(2,1)}, bf16[896,128]{1,0:T(8,128)(2,1)S(1)}, u32[]{:S(2)}, u32[]{:S(2)}) collective-permute-start(bf16[896,128]{1,0:T(8,128)(2,1)} %reply.3), channel_id=1, source_target_pairs={{0,1},{1,0},{2,3},{3,2},{4,5},{5,4},{6,7},{7,6},{8,9},{9,8},{10,11... | collective-permute-start | bytes 688136 | tf_op jit(solution)/shard_map/ppermute | solution.py:553
  63.5 0.7 %copy-start.2 = (bf16[896,128]{1,0:T(8,128)(2,1)}, bf16[896,128]{1,0:T(8,128)(2,1)S(1)}, u32[]{:S(2)}) copy-start(bf16[896,128]{1,0:T(8,128)(2,1)S(1)} %collective-permute-done.3.rest_3_) | copy-start | bytes 688132
  63.6 0.7 %copy-start.3 = (bf16[896,128]{1,0:T(8,128)(2,1)}, bf16[896,128]{1,0:T(8,128)(2,1)S(1)}, u32[]{:S(2)}) copy-start(bf16[896,128]{1,0:T(8,128)(2,1)S(1)} %collective-permute-done.2.rest_2_) | copy-start | bytes 688132

commit v2 on v1

--- a/solution.py
+++ b/solution.py
@@ -1,4 +1,3 @@
-import functools
 import math
 
 import jax
@@ -7,6 +6,7 @@
 from jax.experimental import pallas as pl
 from jax.experimental.pallas import tpu as pltpu
 from jax.sharding import PartitionSpec as P
+
 
 H = 16
 TILE = 16
@@ -196,6 +196,32 @@
     stale_output,
     refreshed,
 ):
+    (
+        tokens,
+        projection_weight,
+        shift_term,
+        scale_term,
+        query_gain,
+        key_gain,
+        stale_keys,
+        stale_values,
+        stale_output,
+        refreshed,
+    ) = (
+        pltpu.with_memory_space_constraint(array, pltpu.HBM)
+        for array in (
+            tokens,
+            projection_weight,
+            shift_term,
+            scale_term,
+            query_gain,
+            key_gain,
+            stale_keys,
+            stale_values,
+            stale_output,
+            refreshed,
+        )
+    )
     N, D = tokens.shape
     HD = query_gain.shape[0]
     heads = D // HD
@@ -215,12 +241,18 @@
     VM = pl.BlockSpec(memory_space=pltpu.VMEM)
     ANY = pl.BlockSpec(memory_space=pl.ANY)
     SM = pl.BlockSpec(memory_space=pltpu.SMEM)
-    params = pltpu.CompilerParams()
+    params = pltpu.CompilerParams(vmem_limit_bytes=28 * 1024 * 1024)
     DMA = pltpu.SemaphoreType.DMA
     vm = pltpu.VMEM
 
     def sds(rows, cols, dtype):
         return jax.ShapeDtypeStruct((rows, cols), dtype)
+
+    def near(rows, cols, dtype):
+        return pltpu.VMEM((rows, cols), dtype)
+
+    def here(array):
+        return pltpu.with_memory_space_constraint(array, pltpu.VMEM)
 
     def is_fresh(flags):
         base = lax.axis_index("patch") * tiles
@@ -342,7 +374,7 @@
     width0 = swindow[0][1] - swindow[0][0]
     x0, hidden = pl.pallas_call(
         front,
-        out_shape=(sds(xrows, LANES, bf16), sds(R, D, bf16)),
+        out_shape=(near(xrows, LANES, bf16), near(R, D, bf16)),
         in_specs=[SM, ANY, ANY, VM, VM, VM, VM, ANY, ANY],
         out_specs=(VM, VM),
         scratch_shapes=[
@@ -359,8 +391,12 @@
     )(refreshed, tokens, projection_weight, shift_term, scale_term, query_gain, key_gain, stale_keys, stale_values)
 
     swap = [(0, 1), (1, 0)]
+
+    def send(array):
+        return lax.ppermute(array, "patch", swap)
+
     sent = [x0]
-    got = [lax.ppermute(x0, "patch", swap)]
+    got = [send(x0)]
 
     more = len(plan) > 1
 
@@ -397,9 +433,9 @@
                 pack_shipped(kbuf, vbuf, st, low, plan[1][1], column(gk), x1)
 
     width1 = swindow[-1][1] - swindow[-1][0]
-    outs = [sds(len(shipped) * HP, R, bf16)]
+    outs = [near(len(shipped) * HP, R, bf16)]
     if more:
-        outs = [sds(xrows, LANES, bf16)] + outs
+        outs = [near(xrows, LANES, bf16)] + outs
     outs = pl.pallas_call(
         second,
         out_shape=tuple(outs),
@@ -415,15 +451,16 @@
         ],
         compiler_params=params,
         name="second",
-    )(refreshed, hidden, projection_weight, query_gain, key_gain, stale_keys, stale_values)
+    )(refreshed, here(hidden), projection_weight, query_gain, key_gain, stale_keys, stale_values)
     if more:
         sent.append(outs[0])
-        got.append(lax.ppermute(outs[0], "patch", swap))
+        got.append(send(outs[0]))
     qx = outs[-1]
 
-    def third(flags, hid, w, gk, sk, sv, so, kt, vt, out, kall, vall, new, wk, wv, turned, sems):
+    def third(flags, hid, w, gk, sk, sv, so, kt, vt, out, kall, vall, new, wk, wv, turned, held, sems):
         fresh = is_fresh(flags)
-        ocopy = pltpu.make_async_copy(so, out, sems.at[0])
+        incopy = pltpu.make_async_copy(so, held, sems.at[0])
+        ocopy = pltpu.make_async_copy(held, out, sems.at[0])
         kcopy = pltpu.make_async_copy(sk, kall, sems.at[1])
         vcopy = pltpu.make_async_copy(sv, vall, sems.at[2])
         kcopy.start()
@@ -457,11 +494,13 @@
             kcopy.wait()
             vcopy.wait()
 
-        ocopy.start()
+        incopy.start()
         gain = column(gk)
         turn(kall, D, turned)
         for h in range(heads):
             kt[HP * h : HP * (h + 1), :] = padded(normed(turned[HD * h : HD * (h + 1), :], gain), 0.0)
+        incopy.wait()
+        ocopy.start()
         turn(vall, D, turned)
         for h in range(heads):
             vt[HP * h : HP * (h + 1), :] = padded(turned[HD * h : HD * (h + 1), :], 1.0)
@@ -469,7 +508,7 @@
 
     kt, vt, held = pl.pallas_call(
         third,
-        out_shape=(sds(heads * HP, N, bf16), sds(heads * HP, N, bf16), sds(N, D, bf16)),
+        out_shape=(near(heads * HP, N, bf16), near(heads * HP, N, bf16), sds(N, D, bf16)),
         in_specs=[SM, VM, ANY, VM, ANY, ANY, ANY],
         out_specs=(VM, VM, ANY),
         scratch_shapes=[
@@ -479,11 +518,12 @@
             vm((D, D), bf16),
             vm((D, D), bf16),
             vm((D, N), f32),
+            vm((N, D), bf16),
             DMA((5,)),
         ],
         compiler_params=params,
         name="third",
-    )(refreshed, hidden, projection_weight, key_gain, stale_keys, stale_values, stale_output)
+    )(refreshed, here(hidden), projection_weight, key_gain, stale_keys, stale_values, stale_output)
 
     def query_pair(x, i):
         two = take(x, HD * i, qrows, 2 * HD, R)
@@ -544,13 +584,12 @@
         extra = [sent[c - 1]] if c else []
         res = pl.pallas_call(
             reply,
-            out_shape=(sds(rrows, LANES, bf16),) + ((sds(hq * HP, R, f32),) if c else ()),
+            out_shape=(near(rrows, LANES, bf16),) + ((near(hq * HP, R, f32),) if c else ()),
             in_specs=[SM, VM, VM, VM] + [VM] * len(extra),
             out_specs=(VM,) * (1 + len(extra)),
             compiler_params=params,
-            name="reply",
-        )(refreshed, got[c], kt, vt, *extra)
-        answers.append(lax.ppermute(res[0], "patch", swap))
+        )(refreshed, here(got[c]), here(kt), here(vt), *map(here, extra))
+        answers.append(send(res[0]))
         if c:
             own.append(res[1])
 
@@ -578,12 +617,12 @@
 
     mine, full = pl.pallas_call(
         rest_of,
-        out_shape=(sds(hq * HP, R, f32), sds(len(shipped) * HD, R, f32)),
+        out_shape=(near(hq * HP, R, f32), near(len(shipped) * HD, R, f32)),
         in_specs=[SM, VM, VM, VM, VM] + [VM] * len(plan),
         out_specs=(VM, VM),
         compiler_params=params,
         name="rest",
-    )(refreshed, sent[-1], kt, vt, qx, *got)
+    )(refreshed, here(sent[-1]), here(kt), here(vt), here(qx), *map(here, got))
     own.append(mine)
 
     def last(flags, full, *rest):
@@ -619,7 +658,7 @@
             )
             pltpu.make_async_copy(rows, out.at[0:R, :], sem).wait()
 
-    operands = (refreshed, full, *own, *answers, held)
+    operands = (refreshed, *map(here, (full, *own, *answers)), held)
     return pl.pallas_call(
         last,
         out_shape=sds(N, D, bf16),
@@ -632,7 +671,7 @@
     )(*operands)
 
 
-def pick_plan(mesh, tokens_shape, width):
+def pick_plan(mesh, tokens_shape):
     patch = mesh.shape["patch"]
     own_rows = tokens_shape // (mesh.shape["grp"] * patch)
     own_tiles = own_rows // TILE
@@ -661,10 +700,17 @@
     out_specs = P(("grp", "patch"), None)
 
     def whole(*arrays):
-        plan = pick_plan(mesh, arrays[0].shape[0], arrays[0].shape[1])
-        inner = body if plan is None else functools.partial(pair_body, plan)
-        return jax.shard_map(
+        plan = pick_plan(mesh, arrays[0].shape[0])
+        if plan is None:
+            inner = body
+        else:
+
+            def inner(*blocks):
+                return pair_body(plan, *blocks)
+
+        step = jax.shard_map(
             inner, mesh=mesh, in_specs=in_specs, out_specs=out_specs, check_vma=False
-        )(*arrays)
+        )
+        return step(*arrays)
 
     return whole

time: 67.8 us -> 33.7 us (0.50)
  Pallas kernels: 59 us -> 23.3 us
  waiting for transfers between devices: 0.05 us -> 4.1 us
  local copies, waits for them, and re-layouts: 2.07 us -> 0 us
    pallas_call x5, Pallas kernels: 52 us -> 18.2 us  [the longest x1 8.02 us: pair_body(): pl.pallas_call(third, out_shape=(near(heads * HP, N, bf16), near(heads *...]
    ppermute x4, waiting for transfers between devices: 0.05 us -> 4.1 us  [send(): return lax.ppermute(array, 'patch', swap)]
    unnamed x10 -> x0, local copies, waits for them, and re-layouts: 2.07 us -> none
    pallas_call x1, Pallas kernels: 4.37 us -> 3.2 us  [pair_body(): pl.pallas_call(second, out_shape=tuple(outs), in_specs=[SM, VM, ANY, VM,...]
    pallas_call x1, Pallas kernels: 2.67 us -> 1.88 us  [pair_body(): pl.pallas_call(last, out_shape=sds(N, D, bf16), in_specs=[SM] + [VM] * (1...]
  transfers between devices with their start and end apart: 4 -> 4, of which waited for: 0 -> 2; matrix products, arithmetic and copies ran while one was open for 0% -> 0% of each run, Pallas kernels for 71% -> 45%
where the time goes in v2:
time: 33.7 us; the launch traced here: 33.4 us
  Pallas kernels  23.3 us (69%)
  starting transfers between devices  5.89 us (17%)
  waiting for transfers between devices  4.1 us (12%)
    pallas_call x1, Pallas kernels, pair_body(): pl.pallas_call(third, out_shape=(near(heads * HP, N, bf16), near(heads *...  8.02 us
    ppermute x4, starting transfers between devices, send(): return lax.ppermute(array, 'patch', swap)  5.89 us
    ppermute x4, waiting for transfers between devices, send(): return lax.ppermute(array, 'patch', swap)  4.1 us
    pallas_call x1, Pallas kernels, pair_body(): pl.pallas_call(rest_of, out_shape=(near(hq * HP, R, f32), near(len(shippe...  3.68 us
    pallas_call x2, Pallas kernels, pair_body(): pl.pallas_call(reply, out_shape=(near(rrows, LANES, bf16),) + ((near(hq *...  3.29 us
    pallas_call x1, Pallas kernels, pair_body(): pl.pallas_call(front, out_shape=(near(xrows, LANES, bf16), near(R, D, bf1...  3.25 us
    pallas_call x1, Pallas kernels, pair_body(): pl.pallas_call(second, out_shape=tuple(outs), in_specs=[SM, VM, ANY, VM,...  3.2 us
    pallas_call x1, Pallas kernels, pair_body(): pl.pallas_call(last, out_shape=sds(N, D, bf16), in_specs=[SM] + [VM] * (1...  1.88 us
  transfers between devices with their start and end apart: 4, of which 2 were waited for; matrix products, arithmetic and copies ran while one was open for 0% of the time, Pallas kernels for 45%

profile of v2, /device:TPU:0, one launch (start us, length us, event | category | flops | bytes accessed | tf_op | source)
XLA Modules:
  0.0 33.4 jit_solution(15835710528850396944)
XLA Ops:
  0.0 3.2 %front.1 = (bf16[864,128]{1,0:T(8,128)(2,1)S(1)}, bf16[256,1152]{1,0:T(8,128)(2,1)S(1)}) custom-call(s32[48]{0:T(128)} %flags.13, bf16[384,1152]{1,0:T(8,128)(2,1)} %tok.1, bf16[1152,3456]{1,0:T(8,128)(2,1)} %w.5, f32[1152]{0:T(1024)} %shift.1, f32[1152]{0:T(1024)} %scale.1, f32[72]{0:T(128)} %gq.3, f32[72]{0:T(128)} %gk.5, bf16[384,1152]{1,0:T(8,128)(2,1)} %sk.5, ...), custom_call_target="tpu_custom_call" | custom-call | tf_op jit(solution)/shard_map/front/pallas_call | solution.py:375
  3.3 3.2 %second.1 = (bf16[864,128]{1,0:T(8,128)(2,1)S(1)}, bf16[320,256]{1,0:T(8,128)(2,1)S(1)}) custom-call(s32[48]{0:T(128)} %flags.13, bf16[256,1152]{1,0:T(8,128)(2,1)S(1)} %get-tuple-element.16.hid, bf16[1152,3456]{1,0:T(8,128)(2,1)} %w.5, f32[72]{0:T(128)} %gq.3, f32[72]{0:T(128)} %gk.5, bf16[384,1152]{1,0:T(8,128)(2,1)} %sk.5, bf16[384,1152]{1,0:T(8,128)(2,1)} %sv.5), custom_call_target="tpu_custom_call" | custom-call | tf_op jit(solution)/shard_map/second/pallas_call | solution.py:439
  6.5 0.9 %collective-permute-start.1 = (bf16[864,128]{1,0:T(8,128)(2,1)S(1)}, bf16[864,128]{1,0:T(8,128)(2,1)S(1)}, u32[]{:S(2)}, u32[]{:S(2)}) collective-permute-start(bf16[864,128]{1,0:T(8,128)(2,1)S(1)} %get-tuple-element.17.xs), channel_id=1, source_target_pairs={{0,1},{1,0},{2,3},{3,2},{4,5},{5,4},{6,7},{7,6},{8,9},{9,8},{10,11... | collective-permute-start | bytes 663560 | tf_op jit(solution)/shard_map/ppermute | solution.py:396
  7.4 1.2 %collective-permute-start = (bf16[864,128]{1,0:T(8,128)(2,1)S(1)}, bf16[864,128]{1,0:T(8,128)(2,1)S(1)}, u32[]{:S(2)}, u32[]{:S(2)}) collective-permute-start(bf16[864,128]{1,0:T(8,128)(2,1)S(1)} %get-tuple-element.21.rest_0_), channel_id=1, source_target_pairs={{0,1},{1,0},{2,3},{3,2},{4,5},{5,4},{6,7},{7,6},{8,9},{9,8},{10,11... | collective-permute-start | bytes 663560 | tf_op jit(solution)/shard_map/ppermute | solution.py:396
  8.6 8.0 %third.1 = (bf16[1280,384]{1,0:T(8,128)(2,1)S(1)}, bf16[1280,384]{1,0:T(8,128)(2,1)S(1)}, bf16[384,1152]{1,0:T(8,128)(2,1)}) custom-call(s32[48]{0:T(128)} %flags.13, bf16[256,1152]{1,0:T(8,128)(2,1)S(1)} %get-tuple-element.16.hid, bf16[1152,3456]{1,0:T(8,128)(2,1)} %w.5, f32[72]{0:T(128)} %gk.5, bf16[384,1152]{1,0:T(8,128)(2,1)} %sk.5, ...), custom_call_target="tpu_custom_call" | custom-call | tf_op jit(solution)/shard_map/third/pallas_call | solution.py:509
  16.6 0.0 collective-permute-done.1.rest_1_.xr
  16.6 2.5 %shard_map.100 = (bf16[896,128]{1,0:T(8,128)(2,1)S(1)}, f32[480,256]{1,0:T(8,128)S(1)}) custom-call(s32[48]{0:T(128)} %flags.13, bf16[864,128]{1,0:T(8,128)(2,1)S(1)} %collective-permute-done.1.rest_1_.xr, bf16[1280,384]{1,0:T(8,128)(2,1)S(1)} %get-tuple-element.18.kt, bf16[1280,384]{1,0:T(8,128)(2,1)S(1)} %get-tuple-element.19.vt, ...), custom_call_target="tpu_custom_call" | custom-call | tf_op jit(solution)/shard_map/pallas_call | solution.py:585
  19.1 0.1 collective-permute-start.3
  19.2 0.0 collective-permute-done.rest_0_.xr
  19.2 0.8 %shard_map.101 = bf16[896,128]{1,0:T(8,128)(2,1)S(1)} custom-call(s32[48]{0:T(128)} %flags.13, bf16[864,128]{1,0:T(8,128)(2,1)S(1)} %collective-permute-done.rest_0_.xr, bf16[1280,384]{1,0:T(8,128)(2,1)S(1)} %get-tuple-element.18.kt, bf16[1280,384]{1,0:T(8,128)(2,1)S(1)} %get-tuple-element.19.vt), custom_call_target="tpu_custom_call" | custom-call | tf_op jit(solution)/shard_map/pallas_call | solution.py:585
  20.0 3.7 %collective-permute-start.2 = (bf16[896,128]{1,0:T(8,128)(2,1)S(1)}, bf16[896,128]{1,0:T(8,128)(2,1)S(1)}, u32[]{:S(2)}, u32[]{:S(2)}) collective-permute-start(bf16[896,128]{1,0:T(8,128)(2,1)S(1)} %shard_map.101), channel_id=1, source_target_pairs={{0,1},{1,0},{2,3},{3,2},{4,5},{5,4},{6,7},{7,6},{8,9},{9,8},{10,11... | collective-permute-start | bytes 688136 | tf_op jit(solution)/shard_map/ppermute | solution.py:396
  23.7 3.7 %rest.1 = (f32[480,256]{1,0:T(8,128)S(1)}, f32[288,256]{1,0:T(8,128)S(1)}) custom-call(s32[48]{0:T(128)} %flags.13, bf16[864,128]{1,0:T(8,128)(2,1)S(1)} %get-tuple-element.17.xs, bf16[1280,384]{1,0:T(8,128)(2,1)S(1)} %get-tuple-element.18.kt, bf16[1280,384]{1,0:T(8,128)(2,1)S(1)} %get-tuple-element.19.vt, bf16[320,256]{1,0:T(8,128)(2,1)S(1)} %get-tuple-element.20.qx, ...), custom_call_target="tpu_custom_call" | custom-call | tf_op jit(solution)/shard_map/rest/pallas_call | solution.py:618
  27.4 0.2 collective-permute-done.3.rest_3_
  27.6 3.9 %collective-permute-done.2.rest_2_ = bf16[896,128]{1,0:T(8,128)(2,1)S(1)} collective-permute-done((bf16[896,128]{1,0:T(8,128)(2,1)S(1)}, bf16[896,128]{1,0:T(8,128)(2,1)S(1)}, u32[]{:S(2)}, u32[]{:S(2)}) %collective-permute-start.2) | collective-permute-done | bytes 229408 | tf_op jit(solution)/shard_map/ppermute | solution.py:396
  31.5 1.9 %last.1 = bf16[384,1152]{1,0:T(8,128)(2,1)} custom-call(s32[48]{0:T(128)} %flags.13, f32[288,256]{1,0:T(8,128)S(1)} %get-tuple-element.22.full, f32[480,256]{1,0:T(8,128)S(1)} %get-tuple-element.23.rest_0_, f32[480,256]{1,0:T(8,128)S(1)} %get-tuple-element.24.rest_1_, ...), custom_call_target="tpu_custom_call", output_to_operand_aliasing={{}: (6, {})} | custom-call | tf_op jit(solution)/shard_map/last/pallas_call | solution.py:662
Async XLA Ops:
  6.5 10.1 %collective-permute-start.1 = (bf16[864,128]{1,0:T(8,128)(2,1)S(1)}, bf16[864,128]{1,0:T(8,128)(2,1)S(1)}, u32[]{:S(2)}, u32[]{:S(2)}) collective-permute-start(bf16[864,128]{1,0:T(8,128)(2,1)S(1)} %get-tuple-element.17.xs), channel_id=1, source_target_pairs={{0,1},{1,0},{2,3},{3,2},{4,5},{5,4},{6,7},{7,6},{8,9},{9,8},{10,11... | collective-permute-start | bytes 663560 | tf_op jit(solution)/shard_map/ppermute | solution.py:396
  7.4 11.8 %collective-permute-start = (bf16[864,128]{1,0:T(8,128)(2,1)S(1)}, bf16[864,128]{1,0:T(8,128)(2,1)S(1)}, u32[]{:S(2)}, u32[]{:S(2)}) collective-permute-start(bf16[864,128]{1,0:T(8,128)(2,1)S(1)} %get-tuple-element.21.rest_0_), channel_id=1, source_target_pairs={{0,1},{1,0},{2,3},{3,2},{4,5},{5,4},{6,7},{7,6},{8,9},{9,8},{10,11... | collective-permute-start | bytes 663560 | tf_op jit(solution)/shard_map/ppermute | solution.py:396
  19.1 8.5 %collective-permute-start.3 = (bf16[896,128]{1,0:T(8,128)(2,1)S(1)}, bf16[896,128]{1,0:T(8,128)(2,1)S(1)}, u32[]{:S(2)}, u32[]{:S(2)}) collective-permute-start(bf16[896,128]{1,0:T(8,128)(2,1)S(1)} %get-tuple-element.25), channel_id=1, source_target_pairs={{0,1},{1,0},{2,3},{3,2},{4,5},{5,4},{6,7},{7,6},{8,9},{9,8},{10,11... | collective-permute-start | bytes 688136 | tf_op jit(solution)/shard_map/ppermute | solution.py:396
  20.0 11.5 %collective-permute-start.2 = (bf16[896,128]{1,0:T(8,128)(2,1)S(1)}, bf16[896,128]{1,0:T(8,128)(2,1)S(1)}, u32[]{:S(2)}, u32[]{:S(2)}) collective-permute-start(bf16[896,128]{1,0:T(8,128)(2,1)S(1)} %shard_map.101), channel_id=1, source_target_pairs={{0,1},{1,0},{2,3},{3,2},{4,5},{5,4},{6,7},{7,6},{8,9},{9,8},{10,11... | collective-permute-start | bytes 688136 | tf_op jit(solution)/shard_map/ppermute | solution.py:396

commit v3 on v0

--- a/solution.py
+++ b/solution.py
@@ -3,7 +3,10 @@
 import jax
 import jax.numpy as jnp
 from jax import lax
+from jax.experimental import pallas as pl
+from jax.experimental.pallas import tpu as pltpu
 from jax.sharding import PartitionSpec as P
+
 
 H = 16
 TILE = 16
@@ -149,6 +152,594 @@
     return merged.reshape(own_rows, model_width)
 
 
+LANES = 128
+SENDS = 2
+
+
+def ceil_to(amount, unit):
+    return -(-amount // unit) * unit
+
+
+def pair_plan(head_count, model_width, own_rows, fresh_rows):
+    head_size = model_width // head_count
+    ratio = 2 * own_rows // fresh_rows
+    if 2 * own_rows % fresh_rows or own_rows % LANES or fresh_rows % LANES:
+        return None
+    if head_count % (SENDS * (1 + ratio)):
+        return None
+    if head_size % 8 or fresh_rows // LANES * head_size % 16 or 2 * own_rows // LANES * head_size % 16:
+        return None
+    parts = head_count // (SENDS * (1 + ratio))
+    asked = SENDS * parts * ratio
+    chunks = [tuple(range(h, h + parts * ratio)) for h in range(0, asked, parts * ratio)]
+    shipped = [tuple(range(h, h + parts)) for h in range(asked, head_count, parts)]
+    cut = -(-2 * len(chunks[-1]) // 3)
+    answers = [(c, qs) for c, qs in enumerate(chunks[:-1])]
+    answers += [(SENDS - 1, chunks[-1][:cut]), (SENDS - 1, chunks[-1][cut:])]
+    return chunks, shipped, answers
+
+
+def pair_body(
+    plan,
+    tokens,
+    projection_weight,
+    shift_term,
+    scale_term,
+    query_gain,
+    key_gain,
+    stale_keys,
+    stale_values,
+    stale_output,
+    refreshed,
+):
+    chunks, parcels, answers = plan
+    shipped = [h for ks in parcels for h in ks]
+    N, D = tokens.shape
+    HD = query_gain.shape[0]
+    heads = D // HD
+    tiles = N // TILE
+    R = tiles * lax.axis_size("patch") // 3 * TILE
+    fresh_tiles = R // TILE
+    HP = ceil_to(HD + 1, 16)
+    QB, KB = R // LANES, N // LANES
+    QR = QB * HD
+    f32, bf16 = jnp.float32, jnp.bfloat16
+    factor = math.log2(math.e) / math.sqrt(HD)
+    asked = shipped[0]
+    DMA = pltpu.SemaphoreType.DMA
+    vm = pltpu.VMEM
+    VM = pl.BlockSpec(memory_space=pltpu.VMEM)
+    SM = pl.BlockSpec(memory_space=pltpu.SMEM)
+    ANY = pl.BlockSpec(memory_space=pl.ANY)
+    params = pltpu.CompilerParams(vmem_limit_bytes=28 * 1024 * 1024)
+
+    def far(array):
+        return pltpu.with_memory_space_constraint(array, pltpu.HBM)
+
+    def here(array):
+        return pltpu.with_memory_space_constraint(array, pltpu.VMEM)
+
+    def near(rows, cols, dtype):
+        return pltpu.VMEM((rows, cols), dtype)
+
+    def call(kernel, outs, out_specs, ins, in_specs, scratch=(), aliases=None):
+        return pl.pallas_call(
+            kernel,
+            out_shape=tuple(outs),
+            in_specs=list(in_specs),
+            out_specs=tuple(out_specs),
+            scratch_shapes=list(scratch),
+            input_output_aliases=aliases or {},
+            compiler_params=params,
+        )(*ins)
+
+    def tail_rows(n):
+        return ceil_to(2 * QB * n, 16)
+
+    def wide(column, width):
+        return jnp.concatenate([column] * (width // LANES), axis=1)
+
+    def normed(part, gain):
+        spread = jnp.mean(part * part, axis=0, keepdims=True)
+        return part * lax.rsqrt(spread + epsilon) * wide(gain, part.shape[1])
+
+    def padded(part, fill):
+        extra = jnp.full((HP - HD, part.shape[1]), fill, f32)
+        return jnp.concatenate([part, extra], axis=0).astype(bf16)
+
+    def turn(source, low, high, target):
+        for j in range(low, high, LANES):
+            target[j - low : j - low + LANES, :] = source[:, j : j + LANES].astype(f32).T
+
+    def pieces(parts):
+        return jnp.concatenate(
+            [p[:, b : b + LANES] for p in parts for b in range(0, p.shape[1], LANES)], axis=0
+        ).astype(bf16)
+
+    def widen(block, first, count):
+        return jnp.concatenate(
+            [block[HD * (first + b) : HD * (first + b + 1), :] for b in range(count)], axis=1
+        )
+
+    def query_of(x, i):
+        return padded(widen(x[QR * i : QR * (i + 1), :].astype(f32), 0, QB), 0.0)
+
+    def score(queries, keys, values):
+        scores = lax.dot_general(
+            queries, keys, (((0,), (0,)), ((), ())), preferred_element_type=f32
+        )
+        weights = jnp.exp2(scores * factor).astype(bf16)
+        return lax.dot_general(
+            values, weights, (((1,), (1,)), ((), ())), preferred_element_type=f32
+        )
+
+    def head_of(ref, h):
+        return ref[HP * h : HP * (h + 1), :]
+
+    high0 = ceil_to(HD * (chunks[0][-1] + 1), LANES)
+    low1 = HD * chunks[1][0] // LANES * LANES
+    lows = HD * shipped[0] // LANES * LANES
+
+    def answer(x, skip, kt, vt, qs, target):
+        n = len(qs)
+        count = tail_rows(n)
+        place = lax.broadcasted_iota(jnp.int32, (count, LANES), 0)
+        tail = jnp.zeros((count, LANES), f32)
+        for i, h in enumerate(qs):
+            terms = score(query_of(x, skip + i), head_of(kt, h), head_of(vt, h))
+            target[QR * i : QR * (i + 1), :] = pieces([terms[:HD]])
+            total = terms[HD : HD + 1]
+            top = total.astype(bf16).astype(f32)
+            for k, piece in enumerate((top, total - top)):
+                for b in range(QB):
+                    row = (2 * i + k) * QB + b
+                    tail = jnp.where(place == row, piece[:, LANES * b : LANES * (b + 1)], tail)
+        target[QR * n : QR * n + count, :] = tail.astype(bf16)
+
+    def total_of(tail, i):
+        parts = [
+            tail[(2 * i) * QB + b : (2 * i) * QB + b + 1, :]
+            + tail[(2 * i + 1) * QB + b : (2 * i + 1) * QB + b + 1, :]
+            for b in range(QB)
+        ]
+        return jnp.concatenate(parts, axis=1)
+
+    groups = [tuple(range(heads // 2)), tuple(range(heads // 2, heads))]
+
+    def own_terms(own, h):
+        g = 0 if h in groups[0] else 1
+        i = h - groups[g][0]
+        return own[g][HP * i : HP * (i + 1), :]
+
+    def own_query(h, sent, qx):
+        if h >= asked:
+            return qx[HP * (h - asked) : HP * (h - asked + 1), :]
+        c = [h in qs for qs in chunks].index(True)
+        return query_of(sent[c], h - chunks[c][0])
+
+    def settle(info, new, mix):
+        for i in range(fresh_tiles):
+            mix[pl.ds(pl.multiple_of(info[1 + i], TILE), TILE), :] = new[TILE * i : TILE * (i + 1), :]
+
+    def merge(own_terms, x, qs, target, low):
+        tail = x[QR * len(qs) : QR * len(qs) + tail_rows(len(qs)), :].astype(f32)
+        for i, h in enumerate(qs):
+            terms = own_terms(h)
+            theirs = widen(x[QR * i : QR * (i + 1), :].astype(f32), 0, QB)
+            target[HD * h - low : HD * (h + 1) - low, :] = (terms[:HD] + theirs) / (
+                terms[HD : HD + 1] + total_of(tail, i)
+            )
+
+    def write_rows(info, rows, out, low, high, sem):
+        if low == high:
+            return
+        for i in range(fresh_tiles):
+            pltpu.make_async_copy(
+                rows.at[TILE * i : TILE * (i + 1), low:high],
+                out.at[pl.ds(pl.multiple_of(info[1 + i], TILE), TILE), low:high],
+                sem,
+            ).start()
+
+    def wait_rows(rows, out, low, high, sem):
+        if low == high:
+            return
+        pltpu.make_async_copy(rows.at[:, low:high], out.at[0:R, low:high], sem).wait()
+
+    def turn_back(turned, low, rows, j):
+        rows[:, j : j + LANES] = turned[j - low : j - low + LANES, :].T.astype(bf16)
+
+    block_rows = 2 * KB * HD
+
+    def front(
+        flags, tok, w, shift, scale, gq, gk, sk, sv,
+        info, gains, hid, wq, x0, kv,
+        fl, sh, sc, g0, g1, tbuf, wbuf, kbuf, vbuf, qt, st, sems,
+    ):
+        def load(source, target, k):
+            copy = pltpu.make_async_copy(source, target, sems.at[k])
+            copy.start()
+            return copy
+
+        cflags = load(flags, fl, 0)
+        cg0 = load(gq, g0, 1)
+        cg1 = load(gk, g1, 2)
+        ck = load(sk.at[:, lows:D], kbuf, 3)
+        cv = load(sv.at[:, lows:D], vbuf, 4)
+        ctok = load(tok, tbuf, 5)
+        cshift = load(shift, sh, 6)
+        cscale = load(scale, sc, 7)
+        cw = load(w.at[:, 0:high0], wbuf, 8)
+        cflags.wait()
+        me = lax.axis_index("patch")
+        base = me * tiles
+
+        def note(t, seen):
+            info[1 + seen] = t * TILE
+            return seen + fl[base + t]
+
+        count = lax.fori_loop(0, tiles, note, 0)
+        info[0] = count
+        rest = pltpu.make_async_copy(w.at[:, low1:D], wq, sems.at[9])
+
+        @pl.when(count > 0)
+        def _():
+            rest.start()
+
+        cg0.wait()
+        cg1.wait()
+        eye = lax.broadcasted_iota(jnp.int32, (HD, HD), 0) == lax.broadcasted_iota(
+            jnp.int32, (HD, HD), 1
+        )
+        for k, g in enumerate((g0, g1)):
+            row = jnp.broadcast_to(g[...].reshape(1, HD), (HD, HD))
+            column = jnp.sum(jnp.where(eye, row, 0.0), axis=1, keepdims=True)
+            gains[HD * k : HD * (k + 1), :] = jnp.broadcast_to(column, (HD, LANES))
+        ck.wait()
+        cv.wait()
+
+        @pl.when(count == 0)
+        def _():
+            turn(kbuf, 0, D - lows, st.at[0])
+            turn(vbuf, 0, D - lows, st.at[1])
+            gain = gains[HD : 2 * HD, :]
+            for c, ks in enumerate(parcels):
+                for i, h in enumerate(ks):
+                    at = HD * h - lows
+                    block = pieces([normed(st[0, at : at + HD, :], gain), st[1, at : at + HD, :]])
+                    if c == 0:
+                        x0[block_rows * i : block_rows * (i + 1), :] = block
+                    else:
+                        row = block_rows * ((c - 1) * len(ks) + i)
+                        kv[row : row + block_rows, :] = block
+
+        cshift.wait()
+        cscale.wait()
+        ctok.wait()
+
+        @pl.when(count > 0)
+        def _():
+            up = 1.0 + sc[...].reshape(1, D)
+            down = sh[...].reshape(1, D)
+            for i in range(fresh_tiles):
+                x = tbuf[pl.ds(pl.multiple_of(info[1 + i], TILE), TILE), :].astype(f32)
+                center = x - jnp.mean(x, axis=1, keepdims=True)
+                spread = jnp.mean(center * center, axis=1, keepdims=True)
+                hid[TILE * i : TILE * (i + 1), :] = (
+                    center * lax.rsqrt(spread + epsilon) * up + down
+                ).astype(bf16)
+
+        cw.wait()
+
+        @pl.when(count > 0)
+        def _():
+            projected = jnp.dot(hid[...], wbuf[...], preferred_element_type=f32).astype(bf16)
+            turn(projected, 0, high0, qt)
+            gain = gains[0:HD, :]
+            for i, h in enumerate(chunks[0]):
+                x0[QR * i : QR * (i + 1), :] = pieces([normed(qt[HD * h : HD * (h + 1), :], gain)])
+            rest.wait()
+
+    info, gains, hidden, wq, x0, kv = call(
+        front,
+        [
+            pltpu.SMEM((fresh_tiles + 2,), jnp.int32),
+            near(2 * HD, LANES, f32),
+            near(R, D, bf16),
+            near(D, D - low1, bf16),
+            near(QR * len(chunks[0]), LANES, bf16),
+            near(block_rows * (len(shipped) - len(parcels[0])), LANES, bf16),
+        ],
+        [SM] + [VM] * 5,
+        [
+            far(a)
+            for a in (
+                refreshed, tokens, projection_weight, shift_term, scale_term,
+                query_gain, key_gain, stale_keys, stale_values,
+            )
+        ],
+        [ANY] * 9,
+        [
+            pltpu.SMEM(refreshed.shape, jnp.int32),
+            vm(shift_term.shape, f32),
+            vm(scale_term.shape, f32),
+            vm(query_gain.shape, f32),
+            vm(key_gain.shape, f32),
+            vm((N, D), bf16),
+            vm((D, high0), bf16),
+            vm((N, D - lows), bf16),
+            vm((N, D - lows), bf16),
+            vm((high0, R), f32),
+            vm((2, D - lows, N), f32),
+            DMA((10,)),
+        ],
+    )
+
+    info = pltpu.with_memory_space_constraint(info, pltpu.SMEM)
+    gains, hidden, wq = here(gains), here(hidden), here(wq)
+    got = []
+
+    def send(array):
+        got.append(lax.ppermute(array, "patch", [(0, 1), (1, 0)]))
+
+    send(x0)
+
+    def second(
+        info, gains, hid, wq, w, sk, sv, kv,
+        x1, qx, kt, vt, wk, qt, kbuf, vbuf, turned, sems,
+    ):
+        @pl.when(info[0] > 0)
+        def _():
+            wcopy = pltpu.make_async_copy(w.at[:, D : 2 * D], wk, sems.at[0])
+            wcopy.start()
+            projected = jnp.dot(hid[...], wq[...], preferred_element_type=f32).astype(bf16)
+            turn(projected, 0, D - low1, qt)
+            gain = gains[0:HD, :]
+            first = chunks[1][0]
+            for h in range(first, heads):
+                part = normed(qt[HD * h - low1 : HD * (h + 1) - low1, :], gain)
+                if h < asked:
+                    i = h - first
+                    x1[QR * i : QR * (i + 1), :] = pieces([part])
+                else:
+                    i = h - asked
+                    qx[HP * i : HP * (i + 1), :] = padded(part, 0.0)
+            wcopy.wait()
+
+        @pl.when(info[0] == 0)
+        def _():
+            width = ceil_to(HD * asked, LANES)
+            kcopy = pltpu.make_async_copy(sk.at[:, 0:width], kbuf.at[:, 0:width], sems.at[0])
+            vcopy = pltpu.make_async_copy(sv.at[:, 0:width], vbuf.at[:, 0:width], sems.at[1])
+            kcopy.start()
+            vcopy.start()
+            x1[...] = kv[...]
+            gain = gains[HD : 2 * HD, :]
+            kcopy.wait()
+            turn(kbuf, 0, width, turned)
+            for h in range(asked):
+                kt[HP * h : HP * (h + 1), :] = padded(normed(turned[HD * h : HD * (h + 1), :], gain), 0.0)
+            vcopy.wait()
+            turn(vbuf, 0, width, turned)
+            for h in range(asked):
+                vt[HP * h : HP * (h + 1), :] = padded(turned[HD * h : HD * (h + 1), :], 1.0)
+
+    x1, qx, kt_far, vt_far, wk = call(
+        second,
+        [
+            near(QR * len(chunks[1]), LANES, bf16),
+            near(HP * len(shipped), R, bf16),
+            near(HP * asked, N, bf16),
+            near(HP * asked, N, bf16),
+            near(D, D, bf16),
+        ],
+        [VM] * 5,
+        [info, gains, hidden, wq, *map(far, (projection_weight, stale_keys, stale_values)), here(kv)],
+        [SM, VM, VM, VM, ANY, ANY, ANY, VM],
+        [vm((D - low1, R), f32), vm((N, D), bf16), vm((N, D), bf16), vm((D, N), f32), DMA((2,))],
+    )
+    qx, kt_far, vt_far, wk = map(here, (qx, kt_far, vt_far, wk))
+    send(x1)
+    sent = [here(x0), here(x1)]
+
+    def third(
+        info, gains, hid, wk, w, sk, sv, so,
+        kt, vt, out, new, mix, wv, vmix, held, turned, sems,
+    ):
+        @pl.when(info[0] > 0)
+        def _():
+            kcopy = pltpu.make_async_copy(sk, mix, sems.at[0])
+            kcopy.start()
+            wcopy = pltpu.make_async_copy(w.at[:, 2 * D : 3 * D], wv, sems.at[1])
+            wcopy.start()
+            vcopy = pltpu.make_async_copy(sv, vmix, sems.at[2])
+            vcopy.start()
+            icopy = pltpu.make_async_copy(so, held, sems.at[3])
+            icopy.start()
+            ocopy = pltpu.make_async_copy(held, out, sems.at[4])
+            new[...] = jnp.dot(hid[...], wk[...], preferred_element_type=f32).astype(bf16)
+            kcopy.wait()
+            settle(info, new, mix)
+            turn(mix, 0, D, turned)
+            gain = gains[HD : 2 * HD, :]
+            for h in range(heads):
+                kt[HP * h : HP * (h + 1), :] = padded(normed(turned[HD * h : HD * (h + 1), :], gain), 0.0)
+            icopy.wait()
+            ocopy.start()
+            wcopy.wait()
+            new[...] = jnp.dot(hid[...], wv[...], preferred_element_type=f32).astype(bf16)
+            vcopy.wait()
+            settle(info, new, vmix)
+            turn(vmix, 0, D, turned)
+            for h in range(heads):
+                vt[HP * h : HP * (h + 1), :] = padded(turned[HD * h : HD * (h + 1), :], 1.0)
+            ocopy.wait()
+
+    kt, vt, out = call(
+        third,
+        [near(HP * heads, N, bf16), near(HP * heads, N, bf16), jax.ShapeDtypeStruct((N, D), bf16)],
+        [VM, VM, ANY],
+        [
+            info, gains, hidden, wk,
+            *map(far, (projection_weight, stale_keys, stale_values, stale_output)),
+        ],
+        [SM, VM, VM, VM, ANY, ANY, ANY, ANY],
+        [
+            vm((R, D), bf16),
+            vm((N, D), bf16),
+            vm((D, D), bf16),
+            vm((N, D), bf16),
+            vm((N, D), bf16),
+            vm((D, N), f32),
+            DMA((5,)),
+        ],
+    )
+    kt, vt = here(kt), here(vt)
+
+    own, told = [], []
+
+    for a, (c, qs) in enumerate(answers):
+        group = groups[a - SENDS + 1] if SENDS - 1 <= a < SENDS + 1 else ()
+
+        def reply(info, xr, ktf, vtf, *rest, skip=qs[0] - chunks[c][0], qs=qs, group=group):
+            if group:
+                kt, vt, qx, *sent, x, terms = rest
+            else:
+                (x,) = rest
+
+            @pl.when(info[0] == 0)
+            def _():
+                answer(xr, skip, ktf, vtf, qs, x)
+
+            if group:
+
+                @pl.when(info[0] > 0)
+                def _():
+                    for i, h in enumerate(group):
+                        q = own_query(h, sent, qx)
+                        terms[HP * i : HP * (i + 1), :] = score(q, head_of(kt, h), head_of(vt, h))
+
+        ins = [info, here(got[c]), kt_far, vt_far]
+        outs = [near(QR * len(qs) + tail_rows(len(qs)), LANES, bf16)]
+        if group:
+            ins += [kt, vt, qx, *sent]
+            outs += [near(HP * len(group), R, f32)]
+        res = call(reply, outs, [VM] * len(outs), ins, [SM] + [VM] * (len(ins) - 1))
+        send(res[0])
+        told.append(here(got[-1]))
+        if group:
+            own.append(here(res[1]))
+
+    open_low = [HD * qs[0] // LANES * LANES for _, qs in answers]
+    open_high = ceil_to(HD * (answers[-1][1][-1] + 1), LANES)
+
+    def flush(info, turned, at, rows, out, ranges, sems):
+        for low, high in ranges:
+            for j in range(low, high, LANES):
+                turn_back(turned, at, rows, j)
+        for k, (low, high) in enumerate(ranges):
+            write_rows(info, rows, out, low, high, sems.at[k])
+
+    def settle_rows(rows, out, ranges, sems):
+        for k, (low, high) in enumerate(ranges):
+            wait_rows(rows, out, low, high, sems.at[k])
+
+    def rest_of(info, so, kt, vt, qx, *rest):
+        kvs, rest = rest[:SENDS], rest[SENDS:]
+        theirs, rest = rest[: len(answers) - 2], rest[len(answers) - 2 :]
+        first, second_, _, keep, out, turned, rows, held, sems = rest
+        own = (first, second_)
+        low = open_low[-2]
+
+        @pl.when(info[0] == 0)
+        def _():
+            icopy = pltpu.make_async_copy(so, held, sems.at[0])
+            ocopy = pltpu.make_async_copy(held, out, sems.at[1])
+            icopy.start()
+            icopy.wait()
+            ocopy.start()
+            ocopy.wait()
+
+        @pl.when(info[0] > 0)
+        def _():
+            for c, ks in enumerate(parcels):
+                for i, h in enumerate(ks):
+                    block = kvs[c][block_rows * i : block_rows * (i + 1), :].astype(f32)
+                    value = own_terms(own, h) + score(
+                        qx[HP * (h - asked) : HP * (h - asked + 1), :],
+                        padded(widen(block, 0, KB), 0.0),
+                        padded(widen(block, KB, KB), 1.0),
+                    )
+                    turned[HD * h : HD * (h + 1), :] = value[:HD] / value[HD : HD + 1]
+            for x, (_, qs) in zip(theirs, answers):
+                merge(lambda h: own_terms(own, h), x, qs, turned, 0)
+            ranges = [(0, low), (open_high, D)]
+            flush(info, turned, 0, rows, out, ranges, sems)
+            keep[...] = turned[low:open_high, :]
+            settle_rows(rows, out, ranges, sems)
+
+    ins = [info, far(stale_output), kt, vt, qx, *map(here, got[:SENDS]), *told[:-2], *own, out]
+    keep, out = call(
+        rest_of,
+        [near(open_high - open_low[-2], R, f32), jax.ShapeDtypeStruct((N, D), bf16)],
+        [VM, ANY],
+        ins,
+        [SM, ANY] + [VM] * (len(ins) - 3) + [ANY],
+        [vm((D, R), f32), vm((R, D), bf16), vm((N, D), bf16), DMA((2,))],
+        {len(ins) - 1: 1},
+    )
+
+    def join(info, keep, first, second_, theirs, _, left, out, turned, rows, sems):
+        low, high = open_low[-2], open_low[-1]
+
+        @pl.when(info[0] > 0)
+        def _():
+            turned[...] = keep[...]
+            merge(lambda h: own_terms((first, second_), h), theirs, answers[-2][1], turned, low)
+            flush(info, turned, low, rows, out, [(low, high)], sems)
+            left[...] = turned[high - low :, :]
+            settle_rows(rows, out, [(low, high)], sems)
+
+    left, out = call(
+        join,
+        [near(open_high - open_low[-1], R, f32), jax.ShapeDtypeStruct((N, D), bf16)],
+        [VM, ANY],
+        [info, here(keep), *own, told[-2], out],
+        [SM, VM, VM, VM, VM, ANY],
+        [vm((open_high - open_low[-2], R), f32), vm((R, D), bf16), DMA((1,))],
+        {5: 1},
+    )
+
+    def last(info, left, first, second_, theirs, _, out, turned, rows, sems):
+        low = open_low[-1]
+
+        @pl.when(info[0] > 0)
+        def _():
+            turned[...] = left[...]
+            merge(lambda h: own_terms((first, second_), h), theirs, answers[-1][1], turned, low)
+            flush(info, turned, low, rows, out, [(low, open_high)], sems)
+            settle_rows(rows, out, [(low, open_high)], sems)
+
+    return call(
+        last,
+        [jax.ShapeDtypeStruct((N, D), bf16)],
+        [ANY],
+        [info, here(left), *own, told[-1], out],
+        [SM, VM, VM, VM, VM, ANY],
+        [vm((open_high - open_low[-1], R), f32), vm((R, D), bf16), DMA((1,))],
+        {5: 0},
+    )[0]
+
+
+def pick_plan(mesh, token_count, model_width):
+    patch = mesh.shape["patch"]
+    own_rows = token_count // (mesh.shape["grp"] * patch)
+    own_tiles = own_rows // TILE
+    fresh_tiles = own_tiles * patch // 3
+    if patch != 2 or fresh_tiles > own_tiles:
+        return None
+    return pair_plan(H, model_width, own_rows, fresh_tiles * TILE)
+
+
 def solution(mesh):
     in_specs = (
         P(("grp", "patch"), None),
@@ -163,4 +754,19 @@
         P("grp"),
     )
     out_specs = P(("grp", "patch"), None)
-    return jax.shard_map(body, mesh=mesh, in_specs=in_specs, out_specs=out_specs, check_vma=False)
+
+    def whole(*arrays):
+        plan = pick_plan(mesh, *arrays[0].shape)
+        if plan is None:
+            inner = body
+        else:
+
+            def inner(*blocks):
+                return pair_body(plan, *blocks)
+
+        step = jax.shard_map(
+            inner, mesh=mesh, in_specs=in_specs, out_specs=out_specs, check_vma=False
+        )
+        return step(*arrays)
+
+    return whole

time: 104 us -> 26.8 us (0.26)
  waiting for transfers between devices: 28.5 us -> 5.12 us
  local copies, waits for them, and re-layouts: 23.2 us -> 0 us
  matrix products: 23 us -> 0 us
  other arithmetic: 14.6 us -> 0 us
  Pallas kernels: 0 us -> 14.3 us
  between operations: 13.3 us -> 0.07 us
  starting transfers between devices: 0.27 us -> 7.1 us
    reduce_scatter x2 -> x0, waiting for transfers between devices: 24.7 us -> none  [the longest x1 23.4 us: attend(): lax.psum_scatter(numerator.astype(jnp.bfloat16), 'patch', scatter_dimensi...]
    dot_general x3 -> x0, matrix products: 23 us -> none  [the longest x1 8.67 us: partial_terms(): jnp.einsum('qhd,khd->hqk', query_heads, key_heads, preferred_element_type...]
    pallas_call x0 -> x9, Pallas kernels: none -> 14.3 us  [call(): pl.pallas_call(kernel, out_shape=tuple(outs), in_specs=list(in_specs), ou...]
    gather x5 -> x0, local copies, waits for them, and re-layouts: 8.27 us -> none  [the longest x2 6.26 us: body(): value_new[position]]
    ppermute x0 -> x5, starting transfers between devices: none -> 7.1 us  [send(): got.append(lax.ppermute(array, 'patch', [(0, 1), (1, 0)]))]
    select_n x5 -> x0, other arithmetic: 5.37 us -> none  [the longest x1 3.29 us: body(): jnp.where(fresh_tile, value_new[position], stale_values.reshape(own_tiles...]
    ppermute x0 -> x5, waiting for transfers between devices: none -> 5.12 us  [send(): got.append(lax.ppermute(array, 'patch', [(0, 1), (1, 0)]))]
    reshape x3 -> x0, local copies, waits for them, and re-layouts: 4.97 us -> none  [the longest x1 2.19 us: head_norm(): row_block.astype(jnp.float32).reshape(row_block.shape[0], head_count, -1)]
  transfers between devices with their start and end apart: 3 -> 5, of which waited for: 3 -> 2; matrix products, arithmetic and copies ran while one was open for 29% -> 0% of each run, Pallas kernels for 0% -> 41%
where the time goes in v3:
time: 26.8 us; the launch traced here: 26.6 us
  Pallas kernels  14.3 us (53%)
  starting transfers between devices  7.1 us (26%)
  waiting for transfers between devices  5.12 us (19%)
    pallas_call x9, Pallas kernels, call(): pl.pallas_call(kernel, out_shape=tuple(outs), in_specs=list(in_specs), ou...  14.3 us
    ppermute x5, starting transfers between devices, send(): got.append(lax.ppermute(array, 'patch', [(0, 1), (1, 0)]))  7.1 us
    ppermute x5, waiting for transfers between devices, send(): got.append(lax.ppermute(array, 'patch', [(0, 1), (1, 0)]))  5.12 us
  transfers between devices with their start and end apart: 5, of which 2 were waited for; matrix products, arithmetic and copies ran while one was open for 0% of the time, Pallas kernels for 41%

profile of v3, /device:TPU:0, one launch (start us, length us, event | category | flops | bytes accessed | tf_op | source)
XLA Modules:
  0.0 26.6 jit_solution(9509543017649438039)
XLA Ops:
  0.0 2.6 %shard_map.100 = (s32[18]{0:T(128)S(4)}, f32[144,128]{1,0:T(8,128)S(1)}, bf16[256,1152]{1,0:T(8,128)(2,1)S(1)}, bf16[1152,768]{1,0:T(8,128)(2,1)S(1)}, bf16[864,...) custom-call(s32[48]{0:T(128)} %flags.1, bf16[384,1152]{1,0:T(8,128)(2,1)} %tok.1, bf16[1152,3456]{1,0:T(8,128)(2,1)} %w.5, ...), custom_call_target="tpu_custom_call" | custom-call | tf_op jit(solution)/shard_map/pallas_call | solution.py:226
  2.6 2.3 %collective-permute-start = (bf16[864,128]{1,0:T(8,128)(2,1)S(1)}, bf16[864,128]{1,0:T(8,128)(2,1)S(1)}, u32[]{:S(2)}, u32[]{:S(2)}) collective-permute-start(bf16[864,128]{1,0:T(8,128)(2,1)S(1)} %get-tuple-element.36.rest_3_), channel_id=1, source_target_pairs={{0,1},{1,0},{2,3},{3,2},{4,5},{5,4},{6,7},{7,6},{8,9},{9,8},{10,11... | collective-permute-start | bytes 663560 | tf_op jit(solution)/shard_map/ppermute | solution.py:482
  4.9 1.8 %shard_map.101 = (bf16[864,128]{1,0:T(8,128)(2,1)S(1)}, bf16[320,256]{1,0:T(8,128)(2,1)S(1)}, bf16[960,384]{1,0:T(8,128)(2,1)S(1)}, bf16[960,384]{1,0:T(8,128)(2,1)S(1)}, bf16[1152,1152]{1,0:T(8,128)(2,1)S(1)}) custom-call(s32[18]{0:T(128)S(4)} %get-tuple-element.27.info, f32[144,128]{1,0:T(8,128)S(1)} %get-tuple-element.28.gains, ...), custom_call_target="tpu_custom_call" | custom-call | tf_op jit(solution)/shard_map/pallas_call | solution.py:226
  6.7 0.1 collective-permute-start.1
  6.9 4.4 %collective-permute-done.xr.rest_0_ = bf16[864,128]{1,0:T(8,128)(2,1)S(1)} collective-permute-done((bf16[864,128]{1,0:T(8,128)(2,1)S(1)}, bf16[864,128]{1,0:T(8,128)(2,1)S(1)}, u32[]{:S(2)}, u32[]{:S(2)}) %collective-permute-start) | collective-permute-done | bytes 221216 | tf_op jit(solution)/shard_map/ppermute | solution.py:482
  11.2 3.2 %collective-permute-start.2 = (bf16[896,128]{1,0:T(8,128)(2,1)S(1)}, bf16[896,128]{1,0:T(8,128)(2,1)S(1)}, u32[]{:S(2)}, u32[]{:S(2)}) collective-permute-start(bf16[896,128]{1,0:T(8,128)(2,1)S(1)} %shard_map.103), channel_id=1, source_target_pairs={{0,1},{1,0},{2,3},{3,2},{4,5},{5,4},{6,7},{7,6},{8,9},{9,8},{10,11... | collective-permute-start | bytes 688136 | tf_op jit(solution)/shard_map/ppermute | solution.py:482
  14.4 4.0 %shard_map.102 = (bf16[1280,384]{1,0:T(8,128)(2,1)S(1)}, bf16[1280,384]{1,0:T(8,128)(2,1)S(1)}, bf16[384,1152]{1,0:T(8,128)(2,1)}) custom-call(s32[18]{0:T(128)S(4)} %get-tuple-element.27.info, f32[144,128]{1,0:T(8,128)S(1)} %get-tuple-element.28.gains, bf16[256,1152]{1,0:T(8,128)(2,1)S(1)} %get-tuple-element.29.hid, ...), custom_call_target="tpu_custom_call" | custom-call | tf_op jit(solution)/shard_map/pallas_call | solution.py:226
  18.4 0.0 collective-permute-done.1.xr.rest_1_
  18.4 1.3 %shard_map.104 = (bf16[592,128]{1,0:T(8,128)(2,1)S(1)}, f32[640,256]{1,0:T(8,128)S(1)}) custom-call(s32[18]{0:T(128)S(4)} %get-tuple-element.27.info, bf16[864,128]{1,0:T(8,128)(2,1)S(1)} %collective-permute-done.1.xr.rest_1_, bf16[960,384]{1,0:T(8,128)(2,1)S(1)} %get-tuple-element.38.ktf, bf16[960,384]{1,0:T(8,128)(2,1)S(1)} %get-tuple-element.39.vtf, ...), custom_call_target="tpu_custom_call" | custom-call | tf_op jit(solution)/shard_map/pallas_call | solution.py:226
  19.7 0.1 collective-permute-start.3
  19.8 1.3 %shard_map.105 = (bf16[304,128]{1,0:T(8,128)(2,1)S(1)}, f32[640,256]{1,0:T(8,128)S(1)}) custom-call(s32[18]{0:T(128)S(4)} %get-tuple-element.27.info, bf16[864,128]{1,0:T(8,128)(2,1)S(1)} %collective-permute-done.1.xr.rest_1_, bf16[960,384]{1,0:T(8,128)(2,1)S(1)} %get-tuple-element.38.ktf, bf16[960,384]{1,0:T(8,128)(2,1)S(1)} %get-tuple-element.39.vtf, ...), custom_call_target="tpu_custom_call" | custom-call | tf_op jit(solution)/shard_map/pallas_call | solution.py:226
  21.1 1.4 %collective-permute-start.4 = (bf16[304,128]{1,0:T(8,128)(2,1)S(1)}, bf16[304,128]{1,0:T(8,128)(2,1)S(1)}, u32[]{:S(2)}, u32[]{:S(2)}) collective-permute-start(bf16[304,128]{1,0:T(8,128)(2,1)S(1)} %get-tuple-element.47), channel_id=1, source_target_pairs={{0,1},{1,0},{2,3},{3,2},{4,5},{5,4},{6,7},{7,6},{8,9},{9,8},{10,11... | collective-permute-start | bytes 233480 | tf_op jit(solution)/shard_map/ppermute | solution.py:482
  22.6 0.0 collective-permute-done.2.rest_2_
  22.6 1.7 %shard_map.106 = (f32[512,256]{1,0:T(8,128)S(1)}, bf16[384,1152]{1,0:T(8,128)(2,1)}) custom-call(s32[18]{0:T(128)S(4)} %get-tuple-element.27.info, bf16[384,1152]{1,0:T(8,128)(2,1)} %so.3, bf16[1280,384]{1,0:T(8,128)(2,1)S(1)} %get-tuple-element.33.rest_0_.kt, bf16[1280,384]{1,0:T(8,128)(2,1)S(1)} %get-tuple-element.34.rest_1_.vt, ...), custom_call_target="tpu_custom_call", output_to_operand_aliasing={{1}: (10, {})} | custom-call | tf_op jit(solution)/shard_map/pallas_call | solution.py:226
  24.3 0.7 %collective-permute-done.3.theirs = bf16[592,128]{1,0:T(8,128)(2,1)S(1)} collective-permute-done((bf16[592,128]{1,0:T(8,128)(2,1)S(1)}, bf16[592,128]{1,0:T(8,128)(2,1)S(1)}, u32[]{:S(2)}, u32[]{:S(2)}) %collective-permute-start.3) | collective-permute-done | bytes 151584 | tf_op jit(solution)/shard_map/ppermute | solution.py:482
  25.0 0.8 %shard_map.107 = (f32[256,256]{1,0:T(8,128)S(1)}, bf16[384,1152]{1,0:T(8,128)(2,1)}) custom-call(s32[18]{0:T(128)S(4)} %get-tuple-element.27.info, f32[512,256]{1,0:T(8,128)S(1)} %get-tuple-element.43.keep, f32[640,256]{1,0:T(8,128)S(1)} %get-tuple-element.40.rest_3_.first, ...), custom_call_target="tpu_custom_call", output_to_operand_aliasing={{1}: (5, {})} | custom-call | tf_op jit(solution)/shard_map/pallas_call | solution.py:226
  25.8 0.0 collective-permute-done.4.theirs
  25.8 0.8 %shard_map.108 = bf16[384,1152]{1,0:T(8,128)(2,1)} custom-call(s32[18]{0:T(128)S(4)} %get-tuple-element.27.info, f32[256,256]{1,0:T(8,128)S(1)} %get-tuple-element.46.left, f32[640,256]{1,0:T(8,128)S(1)} %get-tuple-element.40.rest_3_.first, f32[640,256]{1,0:T(8,128)S(1)} %get-tuple-element.41.rest_4_.second_, ...), custom_call_target="tpu_custom_call", output_to_operand_aliasing={{}: (5, {})} | custom-call | tf_op jit(solution)/shard_map/pallas_call | solution.py:226
  (1 shorter events, 0.0 us)
Async XLA Ops:
  2.6 8.6 %collective-permute-start = (bf16[864,128]{1,0:T(8,128)(2,1)S(1)}, bf16[864,128]{1,0:T(8,128)(2,1)S(1)}, u32[]{:S(2)}, u32[]{:S(2)}) collective-permute-start(bf16[864,128]{1,0:T(8,128)(2,1)S(1)} %get-tuple-element.36.rest_3_), channel_id=1, source_target_pairs={{0,1},{1,0},{2,3},{3,2},{4,5},{5,4},{6,7},{7,6},{8,9},{9,8},{10,11... | collective-permute-start | bytes 663560 | tf_op jit(solution)/shard_map/ppermute | solution.py:482
  6.7 11.6 %collective-permute-start.1 = (bf16[864,128]{1,0:T(8,128)(2,1)S(1)}, bf16[864,128]{1,0:T(8,128)(2,1)S(1)}, u32[]{:S(2)}, u32[]{:S(2)}) collective-permute-start(bf16[864,128]{1,0:T(8,128)(2,1)S(1)} %get-tuple-element.37.rest_4_), channel_id=1, source_target_pairs={{0,1},{1,0},{2,3},{3,2},{4,5},{5,4},{6,7},{7,6},{8,9},{9,8},{10,11... | collective-permute-start | bytes 663560 | tf_op jit(solution)/shard_map/ppermute | solution.py:482
  11.2 11.3 %collective-permute-start.2 = (bf16[896,128]{1,0:T(8,128)(2,1)S(1)}, bf16[896,128]{1,0:T(8,128)(2,1)S(1)}, u32[]{:S(2)}, u32[]{:S(2)}) collective-permute-start(bf16[896,128]{1,0:T(8,128)(2,1)S(1)} %shard_map.103), channel_id=1, source_target_pairs={{0,1},{1,0},{2,3},{3,2},{4,5},{5,4},{6,7},{7,6},{8,9},{9,8},{10,11... | collective-permute-start | bytes 688136 | tf_op jit(solution)/shard_map/ppermute | solution.py:482
  19.7 5.3 %collective-permute-start.3 = (bf16[592,128]{1,0:T(8,128)(2,1)S(1)}, bf16[592,128]{1,0:T(8,128)(2,1)S(1)}, u32[]{:S(2)}, u32[]{:S(2)}) collective-permute-start(bf16[592,128]{1,0:T(8,128)(2,1)S(1)} %get-tuple-element.44), channel_id=1, source_target_pairs={{0,1},{1,0},{2,3},{3,2},{4,5},{5,4},{6,7},{7,6},{8,9},{9,8},{10,11... | collective-permute-start | bytes 454664 | tf_op jit(solution)/shard_map/ppermute | solution.py:482
  21.1 4.7 %collective-permute-start.4 = (bf16[304,128]{1,0:T(8,128)(2,1)S(1)}, bf16[304,128]{1,0:T(8,128)(2,1)S(1)}, u32[]{:S(2)}, u32[]{:S(2)}) collective-permute-start(bf16[304,128]{1,0:T(8,128)(2,1)S(1)} %get-tuple-element.47), channel_id=1, source_target_pairs={{0,1},{1,0},{2,3},{3,2},{4,5},{5,4},{6,7},{7,6},{8,9},{9,8},{10,11... | collective-permute-start | bytes 233480 | tf_op jit(solution)/shard_map/ppermute | solution.py:482

commit v4 on v3

--- a/solution.py
+++ b/solution.py
@@ -153,7 +153,7 @@
 
 
 LANES = 128
-SENDS = 2
+LAG = 3
 
 
 def ceil_to(amount, unit):
@@ -165,18 +165,15 @@
     ratio = 2 * own_rows // fresh_rows
     if 2 * own_rows % fresh_rows or own_rows % LANES or fresh_rows % LANES:
         return None
-    if head_count % (SENDS * (1 + ratio)):
-        return None
     if head_size % 8 or fresh_rows // LANES * head_size % 16 or 2 * own_rows // LANES * head_size % 16:
         return None
-    parts = head_count // (SENDS * (1 + ratio))
-    asked = SENDS * parts * ratio
-    chunks = [tuple(range(h, h + parts * ratio)) for h in range(0, asked, parts * ratio)]
-    shipped = [tuple(range(h, h + parts)) for h in range(asked, head_count, parts)]
-    cut = -(-2 * len(chunks[-1]) // 3)
-    answers = [(c, qs) for c, qs in enumerate(chunks[:-1])]
-    answers += [(SENDS - 1, chunks[-1][:cut]), (SENDS - 1, chunks[-1][cut:])]
-    return chunks, shipped, answers
+    asked = head_count - LAG
+    late = -(-(asked - LAG * ratio) // (LAG - 1))
+    if not 0 < late <= ratio:
+        return None
+    chunks = [tuple(range(h, h + ratio)) for h in range(0, LAG * ratio, ratio)]
+    chunks += [tuple(range(h, min(h + late, asked))) for h in range(LAG * ratio, asked, late)]
+    return chunks, tuple(range(asked, head_count))
 
 
 def pair_body(
@@ -192,8 +189,7 @@
     stale_output,
     refreshed,
 ):
-    chunks, parcels, answers = plan
-    shipped = [h for ks in parcels for h in ks]
+    chunks, shipped = plan
     N, D = tokens.shape
     HD = query_gain.shape[0]
     heads = D // HD
@@ -236,6 +232,12 @@
     def tail_rows(n):
         return ceil_to(2 * QB * n, 16)
 
+    def step_rows(s):
+        rows = [QR * len(chunks[s])] if s < len(chunks) else []
+        if s >= LAG:
+            rows.append(QR * len(chunks[s - LAG]) + tail_rows(len(chunks[s - LAG])))
+        return max(rows)
+
     def wide(column, width):
         return jnp.concatenate([column] * (width // LANES), axis=1)
 
@@ -277,16 +279,17 @@
         return ref[HP * h : HP * (h + 1), :]
 
     high0 = ceil_to(HD * (chunks[0][-1] + 1), LANES)
-    low1 = HD * chunks[1][0] // LANES * LANES
+    low1, high1 = HD * chunks[1][0] // LANES * LANES, ceil_to(HD * (chunks[1][-1] + 1), LANES)
+    low2 = HD * chunks[2][0] // LANES * LANES
     lows = HD * shipped[0] // LANES * LANES
 
-    def answer(x, skip, kt, vt, qs, target):
+    def answer(x, kt, vt, qs, target):
         n = len(qs)
         count = tail_rows(n)
         place = lax.broadcasted_iota(jnp.int32, (count, LANES), 0)
         tail = jnp.zeros((count, LANES), f32)
         for i, h in enumerate(qs):
-            terms = score(query_of(x, skip + i), head_of(kt, h), head_of(vt, h))
+            terms = score(query_of(x, i), head_of(kt, h), head_of(vt, h))
             target[QR * i : QR * (i + 1), :] = pieces([terms[:HD]])
             total = terms[HD : HD + 1]
             top = total.astype(bf16).astype(f32)
@@ -304,18 +307,21 @@
         ]
         return jnp.concatenate(parts, axis=1)
 
-    groups = [tuple(range(heads // 2)), tuple(range(heads // 2, heads))]
+    bounds = (0, 3 * heads // 8, 5 * heads // 8, 7 * heads // 8, heads)
+    groups = [tuple(range(a, b)) for a, b in zip(bounds, bounds[1:])]
 
     def own_terms(own, h):
-        g = 0 if h in groups[0] else 1
+        g = [h in group for group in groups].index(True)
         i = h - groups[g][0]
         return own[g][HP * i : HP * (i + 1), :]
 
-    def own_query(h, sent, qx):
+    def own_query(h, sent, stash, qx):
         if h >= asked:
             return qx[HP * (h - asked) : HP * (h - asked + 1), :]
         c = [h in qs for qs in chunks].index(True)
-        return query_of(sent[c], h - chunks[c][0])
+        if c < LAG:
+            return query_of(sent[c], h - chunks[c][0])
+        return query_of(stash, h - chunks[LAG][0])
 
     def settle(info, new, mix):
         for i in range(fresh_tiles):
@@ -353,7 +359,7 @@
     def front(
         flags, tok, w, shift, scale, gq, gk, sk, sv,
         info, gains, hid, wq, x0, kv,
-        fl, sh, sc, g0, g1, tbuf, wbuf, kbuf, vbuf, qt, st, sems,
+        fl, sh, sc, g0, g1, tbuf, kbuf, vbuf, qt, st, sems,
     ):
         def load(source, target, k):
             copy = pltpu.make_async_copy(source, target, sems.at[k])
@@ -368,7 +374,7 @@
         ctok = load(tok, tbuf, 5)
         cshift = load(shift, sh, 6)
         cscale = load(scale, sc, 7)
-        cw = load(w.at[:, 0:high0], wbuf, 8)
+        cw = load(w.at[:, 0:high0], wq.at[:, 0:high0], 8)
         cflags.wait()
         me = lax.axis_index("patch")
         base = me * tiles
@@ -379,7 +385,7 @@
 
         count = lax.fori_loop(0, tiles, note, 0)
         info[0] = count
-        rest = pltpu.make_async_copy(w.at[:, low1:D], wq, sems.at[9])
+        rest = pltpu.make_async_copy(w.at[:, high0:high1], wq.at[:, high0:high1], sems.at[9])
 
         @pl.when(count > 0)
         def _():
@@ -402,15 +408,13 @@
             turn(kbuf, 0, D - lows, st.at[0])
             turn(vbuf, 0, D - lows, st.at[1])
             gain = gains[HD : 2 * HD, :]
-            for c, ks in enumerate(parcels):
-                for i, h in enumerate(ks):
-                    at = HD * h - lows
-                    block = pieces([normed(st[0, at : at + HD, :], gain), st[1, at : at + HD, :]])
-                    if c == 0:
-                        x0[block_rows * i : block_rows * (i + 1), :] = block
-                    else:
-                        row = block_rows * ((c - 1) * len(ks) + i)
-                        kv[row : row + block_rows, :] = block
+            for i, h in enumerate(shipped):
+                at = HD * h - lows
+                block = pieces([normed(st[0, at : at + HD, :], gain), st[1, at : at + HD, :]])
+                if i == 0:
+                    x0[...] = block
+                else:
+                    kv[block_rows * (i - 1) : block_rows * i, :] = block
 
         cshift.wait()
         cscale.wait()
@@ -432,7 +436,7 @@
 
         @pl.when(count > 0)
         def _():
-            projected = jnp.dot(hid[...], wbuf[...], preferred_element_type=f32).astype(bf16)
+            projected = jnp.dot(hid[...], wq[:, 0:high0], preferred_element_type=f32).astype(bf16)
             turn(projected, 0, high0, qt)
             gain = gains[0:HD, :]
             for i, h in enumerate(chunks[0]):
@@ -445,9 +449,9 @@
             pltpu.SMEM((fresh_tiles + 2,), jnp.int32),
             near(2 * HD, LANES, f32),
             near(R, D, bf16),
-            near(D, D - low1, bf16),
+            near(D, high1, bf16),
             near(QR * len(chunks[0]), LANES, bf16),
-            near(block_rows * (len(shipped) - len(parcels[0])), LANES, bf16),
+            near(block_rows * (LAG - 1), LANES, bf16),
         ],
         [SM] + [VM] * 5,
         [
@@ -465,7 +469,6 @@
             vm(query_gain.shape, f32),
             vm(key_gain.shape, f32),
             vm((N, D), bf16),
-            vm((D, high0), bf16),
             vm((N, D - lows), bf16),
             vm((N, D - lows), bf16),
             vm((high0, R), f32),
@@ -474,6 +477,7 @@
         ],
     )
 
+    late_weight = here(lax.optimization_barrier((projection_weight, x0))[0])
     info = pltpu.with_memory_space_constraint(info, pltpu.SMEM)
     gains, hidden, wq = here(gains), here(hidden), here(wq)
     got = []
@@ -483,27 +487,17 @@
 
     send(x0)
 
-    def second(
-        info, gains, hid, wq, w, sk, sv, kv,
-        x1, qx, kt, vt, wk, qt, kbuf, vbuf, turned, sems,
+    def following(
+        info, gains, hid, wq, sk, sv, kv, x1, kt, vbuf, qt, kbuf, turned, sems
     ):
         @pl.when(info[0] > 0)
         def _():
-            wcopy = pltpu.make_async_copy(w.at[:, D : 2 * D], wk, sems.at[0])
-            wcopy.start()
-            projected = jnp.dot(hid[...], wq[...], preferred_element_type=f32).astype(bf16)
-            turn(projected, 0, D - low1, qt)
+            projected = jnp.dot(hid[...], wq[:, low1:high1], preferred_element_type=f32).astype(bf16)
+            turn(projected, 0, high1 - low1, qt)
             gain = gains[0:HD, :]
-            first = chunks[1][0]
-            for h in range(first, heads):
+            for i, h in enumerate(chunks[1]):
                 part = normed(qt[HD * h - low1 : HD * (h + 1) - low1, :], gain)
-                if h < asked:
-                    i = h - first
-                    x1[QR * i : QR * (i + 1), :] = pieces([part])
-                else:
-                    i = h - asked
-                    qx[HP * i : HP * (i + 1), :] = padded(part, 0.0)
-            wcopy.wait()
+                x1[QR * i : QR * (i + 1), :] = pieces([part])
 
         @pl.when(info[0] == 0)
         def _():
@@ -512,125 +506,178 @@
             vcopy = pltpu.make_async_copy(sv.at[:, 0:width], vbuf.at[:, 0:width], sems.at[1])
             kcopy.start()
             vcopy.start()
-            x1[...] = kv[...]
+            x1[...] = kv[0:block_rows, :]
             gain = gains[HD : 2 * HD, :]
             kcopy.wait()
             turn(kbuf, 0, width, turned)
             for h in range(asked):
                 kt[HP * h : HP * (h + 1), :] = padded(normed(turned[HD * h : HD * (h + 1), :], gain), 0.0)
             vcopy.wait()
-            turn(vbuf, 0, width, turned)
+
+    kv = here(kv)
+    x1, kt_far, v_far = call(
+        following,
+        [near(step_rows(1), LANES, bf16), near(HP * asked, N, bf16), near(N, D, bf16)],
+        [VM] * 3,
+        [info, gains, hidden, wq, far(stale_keys), far(stale_values), kv],
+        [SM, VM, VM, VM, ANY, ANY, VM],
+        [vm((high1 - low1, R), f32), vm((N, D), bf16), vm((D, N), f32), DMA((2,))],
+    )
+    kt_far, v_far = here(kt_far), here(v_far)
+    send(x1)
+
+    def second(info, gains, hid, w, kv, v_far, x2, stash, qx, vt, qt, turned):
+        @pl.when(info[0] > 0)
+        def _():
+            projected = jnp.dot(hid[...], w[:, low2:D], preferred_element_type=f32).astype(bf16)
+            turn(projected, 0, D - low2, qt)
+            gain = gains[0:HD, :]
+            for h in range(chunks[2][0], heads):
+                part = normed(qt[HD * h - low2 : HD * (h + 1) - low2, :], gain)
+                if h in chunks[2]:
+                    i = h - chunks[2][0]
+                    x2[QR * i : QR * (i + 1), :] = pieces([part])
+                elif h < asked:
+                    i = h - chunks[LAG][0]
+                    stash[QR * i : QR * (i + 1), :] = pieces([part])
+                else:
+                    i = h - asked
+                    qx[HP * i : HP * (i + 1), :] = padded(part, 0.0)
+
+        @pl.when(info[0] == 0)
+        def _():
+            x2[...] = kv[block_rows : 2 * block_rows, :]
+            turn(v_far, 0, ceil_to(HD * asked, LANES), turned)
             for h in range(asked):
                 vt[HP * h : HP * (h + 1), :] = padded(turned[HD * h : HD * (h + 1), :], 1.0)
 
-    x1, qx, kt_far, vt_far, wk = call(
+    x2, stash, qx, vt_far = call(
         second,
         [
-            near(QR * len(chunks[1]), LANES, bf16),
+            near(step_rows(2), LANES, bf16),
+            near(QR * (asked - chunks[LAG][0]), LANES, bf16),
             near(HP * len(shipped), R, bf16),
             near(HP * asked, N, bf16),
-            near(HP * asked, N, bf16),
-            near(D, D, bf16),
         ],
-        [VM] * 5,
-        [info, gains, hidden, wq, *map(far, (projection_weight, stale_keys, stale_values)), here(kv)],
-        [SM, VM, VM, VM, ANY, ANY, ANY, VM],
-        [vm((D - low1, R), f32), vm((N, D), bf16), vm((N, D), bf16), vm((D, N), f32), DMA((2,))],
-    )
-    qx, kt_far, vt_far, wk = map(here, (qx, kt_far, vt_far, wk))
-    send(x1)
-    sent = [here(x0), here(x1)]
-
-    def third(
-        info, gains, hid, wk, w, sk, sv, so,
-        kt, vt, out, new, mix, wv, vmix, held, turned, sems,
-    ):
+        [VM] * 4,
+        [info, gains, hidden, late_weight, kv, v_far],
+        [SM] + [VM] * 5,
+        [vm((D - low2, R), f32), vm((D, N), f32)],
+    )
+    stash, qx, vt_far = here(stash), here(qx), here(vt_far)
+    send(x2)
+    sent = [here(x0), here(x1), here(x2)]
+
+    def third(info, hid, w, sk, turned, new, mix, sem):
         @pl.when(info[0] > 0)
         def _():
-            kcopy = pltpu.make_async_copy(sk, mix, sems.at[0])
+            kcopy = pltpu.make_async_copy(sk, mix, sem)
             kcopy.start()
-            wcopy = pltpu.make_async_copy(w.at[:, 2 * D : 3 * D], wv, sems.at[1])
-            wcopy.start()
-            vcopy = pltpu.make_async_copy(sv, vmix, sems.at[2])
-            vcopy.start()
-            icopy = pltpu.make_async_copy(so, held, sems.at[3])
-            icopy.start()
-            ocopy = pltpu.make_async_copy(held, out, sems.at[4])
-            new[...] = jnp.dot(hid[...], wk[...], preferred_element_type=f32).astype(bf16)
+            new[...] = jnp.dot(hid[...], w[:, D : 2 * D], preferred_element_type=f32).astype(bf16)
             kcopy.wait()
             settle(info, new, mix)
             turn(mix, 0, D, turned)
-            gain = gains[HD : 2 * HD, :]
-            for h in range(heads):
-                kt[HP * h : HP * (h + 1), :] = padded(normed(turned[HD * h : HD * (h + 1), :], gain), 0.0)
-            icopy.wait()
-            ocopy.start()
-            wcopy.wait()
-            new[...] = jnp.dot(hid[...], wv[...], preferred_element_type=f32).astype(bf16)
-            vcopy.wait()
-            settle(info, new, vmix)
-            turn(vmix, 0, D, turned)
-            for h in range(heads):
-                vt[HP * h : HP * (h + 1), :] = padded(turned[HD * h : HD * (h + 1), :], 1.0)
-            ocopy.wait()
-
-    kt, vt, out = call(
+
+    (keys_turned,) = call(
         third,
-        [near(HP * heads, N, bf16), near(HP * heads, N, bf16), jax.ShapeDtypeStruct((N, D), bf16)],
-        [VM, VM, ANY],
-        [
-            info, gains, hidden, wk,
-            *map(far, (projection_weight, stale_keys, stale_values, stale_output)),
-        ],
-        [SM, VM, VM, VM, ANY, ANY, ANY, ANY],
-        [
-            vm((R, D), bf16),
-            vm((N, D), bf16),
-            vm((D, D), bf16),
-            vm((N, D), bf16),
-            vm((N, D), bf16),
-            vm((D, N), f32),
-            DMA((5,)),
-        ],
-    )
-    kt, vt = here(kt), here(vt)
+        [near(D, N, f32)],
+        [VM],
+        [info, hidden, late_weight, far(stale_keys)],
+        [SM, VM, VM, ANY],
+        [vm((R, D), bf16), vm((N, D), bf16), DMA],
+    )
+    keys_turned = here(keys_turned)
 
     own, told = [], []
-
-    for a, (c, qs) in enumerate(answers):
-        group = groups[a - SENDS + 1] if SENDS - 1 <= a < SENDS + 1 else ()
-
-        def reply(info, xr, ktf, vtf, *rest, skip=qs[0] - chunks[c][0], qs=qs, group=group):
-            if group:
+    kt = vt = vnew = vall = held = out = None
+    project_at, turn_at = 1, 2
+
+    for c, qs in enumerate(chunks):
+        s = c + LAG
+        after = chunks[s] if s < len(chunks) else ()
+        group = groups[c - turn_at] if c >= turn_at else ()
+
+        def reply(info, xr, ktf, vtf, stash, *rest, c=c, qs=qs, after=after, group=group):
+            if c == project_at:
+                gains, keys_turned, hid, w, sv, so, x, vnew, kt, vall, held, sems = rest
+            elif c == turn_at:
+                kt, qx, *sent, vnew, vall, held, x, terms, vt, out, mix, turned, sem = rest
+            elif group:
                 kt, vt, qx, *sent, x, terms = rest
             else:
                 (x,) = rest
 
             @pl.when(info[0] == 0)
             def _():
-                answer(xr, skip, ktf, vtf, qs, x)
-
-            if group:
-
-                @pl.when(info[0] > 0)
-                def _():
-                    for i, h in enumerate(group):
-                        q = own_query(h, sent, qx)
-                        terms[HP * i : HP * (i + 1), :] = score(q, head_of(kt, h), head_of(vt, h))
-
-        ins = [info, here(got[c]), kt_far, vt_far]
-        outs = [near(QR * len(qs) + tail_rows(len(qs)), LANES, bf16)]
-        if group:
+                answer(xr, ktf, vtf, qs, x)
+
+            @pl.when(info[0] > 0)
+            def _():
+                if after:
+                    at = QR * (after[0] - chunks[LAG][0])
+                    x[0 : QR * len(after), :] = stash[at : at + QR * len(after), :]
+                if c == project_at:
+                    vcopy = pltpu.make_async_copy(sv, vall, sems.at[0])
+                    vcopy.start()
+                    ocopy = pltpu.make_async_copy(so, held, sems.at[1])
+                    ocopy.start()
+                    vnew[...] = jnp.dot(hid[...], w[:, 2 * D :], preferred_element_type=f32).astype(bf16)
+                    gain = gains[HD : 2 * HD, :]
+                    for h in range(heads):
+                        part = normed(keys_turned[HD * h : HD * (h + 1), :], gain)
+                        kt[HP * h : HP * (h + 1), :] = padded(part, 0.0)
+                    vcopy.wait()
+                    ocopy.wait()
+                if c == turn_at:
+                    ocopy = pltpu.make_async_copy(held, out, sem)
+                    ocopy.start()
+                    mix[...] = vall[...]
+                    settle(info, vnew, mix)
+                    turn(mix, 0, D, turned)
+                    for h in range(heads):
+                        vt[HP * h : HP * (h + 1), :] = padded(turned[HD * h : HD * (h + 1), :], 1.0)
+                for i, h in enumerate(group):
+                    q = own_query(h, sent, stash, qx)
+                    terms[HP * i : HP * (i + 1), :] = score(q, head_of(kt, h), head_of(vt, h))
+                if c == turn_at:
+                    ocopy.wait()
+
+        ins = [info, here(got[c]), kt_far, vt_far, stash]
+        outs = [near(step_rows(s), LANES, bf16)]
+        given = [VM] * len(ins[1:])
+        spaces = [VM]
+        scratch = []
+        if c == project_at:
+            ins += [gains, keys_turned, hidden, late_weight, far(stale_values), far(stale_output)]
+            given += [VM] * 4 + [ANY] * 2
+            outs += [near(R, D, bf16), near(HP * heads, N, bf16), near(N, D, bf16), near(N, D, bf16)]
+            spaces += [VM] * 4
+            scratch = [DMA((2,))]
+        elif c == turn_at:
+            ins += [kt, qx, *sent, vnew, vall, held]
+            given += [VM] * (5 + len(sent))
+            outs += [near(HP * len(group), R, f32), near(HP * heads, N, bf16), jax.ShapeDtypeStruct((N, D), bf16)]
+            spaces += [VM, VM, ANY]
+            scratch = [vm((N, D), bf16), vm((D, N), f32), DMA]
+        elif group:
             ins += [kt, vt, qx, *sent]
+            given += [VM] * (3 + len(sent))
             outs += [near(HP * len(group), R, f32)]
-        res = call(reply, outs, [VM] * len(outs), ins, [SM] + [VM] * (len(ins) - 1))
+            spaces += [VM]
+        res = call(reply, outs, spaces, ins, [SM] + given, scratch)
         send(res[0])
         told.append(here(got[-1]))
-        if group:
+        if c == project_at:
+            vnew, kt, vall, held = map(here, res[1:])
+        elif group:
             own.append(here(res[1]))
-
-    open_low = [HD * qs[0] // LANES * LANES for _, qs in answers]
-    open_high = ceil_to(HD * (answers[-1][1][-1] + 1), LANES)
+            if c == turn_at:
+                vt, out = here(res[2]), res[3]
+
+    answers = chunks
+
+    open_low = [HD * qs[0] // LANES * LANES for qs in answers]
+    open_high = ceil_to(HD * (answers[-1][-1] + 1), LANES)
 
     def flush(info, turned, at, rows, out, ranges, sems):
         for low, high in ranges:
@@ -643,11 +690,13 @@
         for k, (low, high) in enumerate(ranges):
             wait_rows(rows, out, low, high, sems.at[k])
 
-    def rest_of(info, so, kt, vt, qx, *rest):
-        kvs, rest = rest[:SENDS], rest[SENDS:]
+    def rest_of(info, so, kt, vt, qx, stash, *rest):
+        sent, rest = rest[:LAG], rest[LAG:]
+        kvs, rest = rest[:LAG], rest[LAG:]
         theirs, rest = rest[: len(answers) - 2], rest[len(answers) - 2 :]
-        first, second_, _, keep, out, turned, rows, held, sems = rest
-        own = (first, second_)
+        early, rest = rest[: len(groups) - 1], rest[len(groups) - 1 :]
+        _, terms, keep, out, turned, rows, held, sems = rest
+        own = (*early, terms)
         low = open_low[-2]
 
         @pl.when(info[0] == 0)
@@ -661,40 +710,51 @@
 
         @pl.when(info[0] > 0)
         def _():
-            for c, ks in enumerate(parcels):
-                for i, h in enumerate(ks):
-                    block = kvs[c][block_rows * i : block_rows * (i + 1), :].astype(f32)
-                    value = own_terms(own, h) + score(
-                        qx[HP * (h - asked) : HP * (h - asked + 1), :],
-                        padded(widen(block, 0, KB), 0.0),
-                        padded(widen(block, KB, KB), 1.0),
-                    )
-                    turned[HD * h : HD * (h + 1), :] = value[:HD] / value[HD : HD + 1]
-            for x, (_, qs) in zip(theirs, answers):
+            for i, h in enumerate(groups[-1]):
+                q = own_query(h, sent, stash, qx)
+                terms[HP * i : HP * (i + 1), :] = score(q, head_of(kt, h), head_of(vt, h))
+            for i, h in enumerate(shipped):
+                block = kvs[i][...].astype(f32)
+                value = own_terms(own, h) + score(
+                    qx[HP * i : HP * (i + 1), :],
+                    padded(widen(block, 0, KB), 0.0),
+                    padded(widen(block, KB, KB), 1.0),
+                )
+                turned[HD * h : HD * (h + 1), :] = value[:HD] / value[HD : HD + 1]
+            for x, qs in zip(theirs, answers):
                 merge(lambda h: own_terms(own, h), x, qs, turned, 0)
             ranges = [(0, low), (open_high, D)]
             flush(info, turned, 0, rows, out, ranges, sems)
             keep[...] = turned[low:open_high, :]
             settle_rows(rows, out, ranges, sems)
 
-    ins = [info, far(stale_output), kt, vt, qx, *map(here, got[:SENDS]), *told[:-2], *own, out]
-    keep, out = call(
+    ins = [
+        info, far(stale_output), kt, vt, qx, stash, *sent,
+        *map(here, got[:LAG]), *told[:-2], *own, out,
+    ]
+    terms, keep, out = call(
         rest_of,
-        [near(open_high - open_low[-2], R, f32), jax.ShapeDtypeStruct((N, D), bf16)],
-        [VM, ANY],
+        [
+            near(HP * len(groups[-1]), R, f32),
+            near(open_high - open_low[-2], R, f32),
+            jax.ShapeDtypeStruct((N, D), bf16),
+        ],
+        [VM, VM, ANY],
         ins,
         [SM, ANY] + [VM] * (len(ins) - 3) + [ANY],
         [vm((D, R), f32), vm((R, D), bf16), vm((N, D), bf16), DMA((2,))],
-        {len(ins) - 1: 1},
-    )
-
-    def join(info, keep, first, second_, theirs, _, left, out, turned, rows, sems):
+        {len(ins) - 1: 2},
+    )
+    own.append(here(terms))
+
+    def join(info, keep, theirs, *rest):
+        own, (_, left, out, turned, rows, sems) = rest[: len(groups)], rest[len(groups) :]
         low, high = open_low[-2], open_low[-1]
 
         @pl.when(info[0] > 0)
         def _():
             turned[...] = keep[...]
-            merge(lambda h: own_terms((first, second_), h), theirs, answers[-2][1], turned, low)
+            merge(lambda h: own_terms(own, h), theirs, answers[-2], turned, low)
             flush(info, turned, low, rows, out, [(low, high)], sems)
             left[...] = turned[high - low :, :]
             settle_rows(rows, out, [(low, high)], sems)
@@ -703,19 +763,20 @@
         join,
         [near(open_high - open_low[-1], R, f32), jax.ShapeDtypeStruct((N, D), bf16)],
         [VM, ANY],
-        [info, here(keep), *own, told[-2], out],
-        [SM, VM, VM, VM, VM, ANY],
+        [info, here(keep), told[-2], *own, out],
+        [SM, VM, VM] + [VM] * len(own) + [ANY],
         [vm((open_high - open_low[-2], R), f32), vm((R, D), bf16), DMA((1,))],
-        {5: 1},
-    )
-
-    def last(info, left, first, second_, theirs, _, out, turned, rows, sems):
+        {3 + len(own): 1},
+    )
+
+    def last(info, left, theirs, *rest):
+        own, (_, out, turned, rows, sems) = rest[: len(groups)], rest[len(groups) :]
         low = open_low[-1]
 
         @pl.when(info[0] > 0)
         def _():
             turned[...] = left[...]
-            merge(lambda h: own_terms((first, second_), h), theirs, answers[-1][1], turned, low)
+            merge(lambda h: own_terms(own, h), theirs, answers[-1], turned, low)
             flush(info, turned, low, rows, out, [(low, open_high)], sems)
             settle_rows(rows, out, [(low, open_high)], sems)
 
@@ -723,10 +784,10 @@
         last,
         [jax.ShapeDtypeStruct((N, D), bf16)],
         [ANY],
-        [info, here(left), *own, told[-1], out],
-        [SM, VM, VM, VM, VM, ANY],
+        [info, here(left), told[-1], *own, out],
+        [SM, VM, VM] + [VM] * len(own) + [ANY],
         [vm((open_high - open_low[-1], R), f32), vm((R, D), bf16), DMA((1,))],
-        {5: 0},
+        {3 + len(own): 0},
     )[0]
 
 

time: 26.8 us -> 26.8 us (level)
  starting transfers between devices: 7.1 us -> 8.71 us
  waiting for transfers between devices: 5.12 us -> 3.58 us
    ppermute x5 -> x8, starting transfers between devices: 7.1 us -> 8.71 us  [send(): got.append(lax.ppermute(array, 'patch', [(0, 1), (1, 0)]))]
    ppermute x5 -> x8, waiting for transfers between devices: 5.12 us -> 3.58 us  [send(): got.append(lax.ppermute(array, 'patch', [(0, 1), (1, 0)]))]
    pallas_call x9 -> x12, Pallas kernels: 14.3 us -> 14.2 us  [call(): pl.pallas_call(kernel, out_shape=tuple(outs), in_specs=list(in_specs), ou...]
  transfers between devices with their start and end apart: 5 -> 8, of which waited for: 2 -> 4; matrix products, arithmetic and copies ran while one was open for 0% -> 0% of each run, Pallas kernels for 41% -> 41%
where the time goes in v4:
time: 26.8 us; the launch traced here: 26.6 us
  Pallas kernels  14.2 us (53%)
  starting transfers between devices  8.71 us (32%)
  waiting for transfers between devices  3.58 us (13%)
    pallas_call x12, Pallas kernels, call(): pl.pallas_call(kernel, out_shape=tuple(outs), in_specs=list(in_specs), ou...  14.2 us
    ppermute x8, starting transfers between devices, send(): got.append(lax.ppermute(array, 'patch', [(0, 1), (1, 0)]))  8.71 us
    ppermute x8, waiting for transfers between devices, send(): got.append(lax.ppermute(array, 'patch', [(0, 1), (1, 0)]))  3.58 us
  transfers between devices with their start and end apart: 8, of which 4 were waited for; matrix products, arithmetic and copies ran while one was open for 0% of the time, Pallas kernels for 41%

profile of v4, /device:TPU:0, one launch (start us, length us, event | category | flops | bytes accessed | tf_op | source)
XLA Modules:
  0.0 26.6 jit_solution(2913862707298635596)
XLA Ops:
  0.0 0.0 copy-start
  0.0 2.5 %shard_map.100 = (s32[18]{0:T(128)S(4)}, f32[144,128]{1,0:T(8,128)S(1)}, bf16[256,1152]{1,0:T(8,128)(2,1)S(1)}, bf16[1152,512]{1,0:T(8,128)(2,1)S(1)}, bf16[432,...) custom-call(s32[48]{0:T(128)} %flags.1, bf16[384,1152]{1,0:T(8,128)(2,1)} %tok.1, bf16[1152,3456]{1,0:T(8,128)(2,1)} %rest_3_, ...), custom_call_target="tpu_custom_call" | custom-call | tf_op jit(solution)/shard_map/pallas_call | solution.py:222
  2.5 2.4 %collective-permute-start.2 = (bf16[432,128]{1,0:T(8,128)(2,1)S(1)}, bf16[432,128]{1,0:T(8,128)(2,1)S(1)}, u32[]{:S(2)}, u32[]{:S(2)}) collective-permute-start(bf16[432,128]{1,0:T(8,128)(2,1)S(1)} %get-tuple-element.44.rest_2_.rest_3_.rest_0_), channel_id=1, source_target_pairs={{0,1},{1,0},{2,3},{3,2},{4,5},{5,4},{6,7},{7,6},{8,9},{9,8},{10,11... | collective-permute-start | bytes 331784 | tf_op jit(solution)/shard_map/ppermute | solution.py:486
  4.9 0.6 %shard_map.101 = (bf16[432,128]{1,0:T(8,128)(2,1)S(1)}, bf16[1040,384]{1,0:T(8,128)(2,1)S(1)}, bf16[384,1152]{1,0:T(8,128)(2,1)S(1)}) custom-call(s32[18]{0:T(128)S(4)} %get-tuple-element.37.info, f32[144,128]{1,0:T(8,128)S(1)} %get-tuple-element.38.gains.rest_0_, bf16[256,1152]{1,0:T(8,128)(2,1)S(1)} %get-tuple-element.39.hid.rest_2_, ...), custom_call_target="tpu_custom_call" | custom-call | tf_op jit(solution)/shard_map/pallas_call | solution.py:222
  5.5 1.4 %collective-permute-start = (bf16[432,128]{1,0:T(8,128)(2,1)S(1)}, bf16[432,128]{1,0:T(8,128)(2,1)S(1)}, u32[]{:S(2)}, u32[]{:S(2)}) collective-permute-start(bf16[432,128]{1,0:T(8,128)(2,1)S(1)} %get-tuple-element.42.rest_3_.rest_4_.rest_1_), channel_id=1, source_target_pairs={{0,1},{1,0},{2,3},{3,2},{4,5},{5,4},{6,7},{7,6},{8,9},{9,8},{10,11... | collective-permute-start | bytes 331784 | tf_op jit(solution)/shard_map/ppermute | solution.py:486
  6.9 0.0 copy-done
  6.9 0.9 %shard_map.102 = (bf16[432,128]{1,0:T(8,128)(2,1)S(1)}, bf16[576,128]{1,0:T(8,128)(2,1)S(1)}, bf16[240,256]{1,0:T(8,128)(2,1)S(1)}, bf16[1040,384]{1,0:T(8,128)(2,1)S(1)}) custom-call(s32[18]{0:T(128)S(4)} %get-tuple-element.37.info, f32[144,128]{1,0:T(8,128)S(1)} %get-tuple-element.38.gains.rest_0_, bf16[256,1152]{1,0:T(8,128)(2,1)S(1)} %get-tuple-element.39.hid.rest_2_, ...), custom_call_target="tpu_custom_call" | custom-call | tf_op jit(solution)/shard_map/pallas_call | solution.py:222
  7.8 0.2 collective-permute-start.1
  8.0 0.3 collective-permute-done.2.xr.rest_3_
  8.2 2.6 %collective-permute-start.3 = (bf16[448,128]{1,0:T(8,128)(2,1)S(1)}, bf16[448,128]{1,0:T(8,128)(2,1)S(1)}, u32[]{:S(2)}, u32[]{:S(2)}) collective-permute-start(bf16[448,128]{1,0:T(8,128)(2,1)S(1)} %shard_map.106), channel_id=1, source_target_pairs={{0,1},{1,0},{2,3},{3,2},{4,5},{5,4},{6,7},{7,6},{8,9},{9,8},{10,11... | collective-permute-start | bytes 344072 | tf_op jit(solution)/shard_map/ppermute | solution.py:486
  10.9 2.4 %shard_map.103.rest_1_ = f32[1152,384]{1,0:T(8,128)S(1)} custom-call(s32[18]{0:T(128)S(4)} %get-tuple-element.37.info, bf16[256,1152]{1,0:T(8,128)(2,1)S(1)} %get-tuple-element.39.hid.rest_2_, bf16[1152,3456]{1,0:T(8,128)(2,1)S(1)} %copy-done, bf16[384,1152]{1,0:T(8,128)(2,1)} %sk.5), custom_call_target="tpu_custom_call" | custom-call | tf_op jit(solution)/shard_map/pallas_call | solution.py:222
  13.3 0.0 collective-permute-done.xr.rest_4_
  13.3 1.5 %shard_map.104 = (bf16[448,128]{1,0:T(8,128)(2,1)S(1)}, bf16[256,1152]{1,0:T(8,128)(2,1)S(1)}, bf16[1280,384]{1,0:T(8,128)(2,1)S(1)}, bf16[384,1152]{1,0:T(8,128)(2,1)S(1)}, bf16[384,1152]{1,0:T(8,128)(2,1)S(1)}) custom-call(s32[18]{0:T(128)S(4)} %get-tuple-element.37.info, bf16[432,128]{1,0:T(8,128)(2,1)S(1)} %collective-permute-done.xr.rest_4_, ...), custom_call_target="tpu_custom_call" | custom-call | tf_op jit(solution)/shard_map/pallas_call | solution.py:222
  14.8 0.1 collective-permute-start.4
  14.9 0.0 collective-permute-done.1.xr.rest_5_
  14.9 1.2 %shard_map.105 = (bf16[448,128]{1,0:T(8,128)(2,1)S(1)}, f32[480,256]{1,0:T(8,128)S(1)}, bf16[1280,384]{1,0:T(8,128)(2,1)S(1)}, bf16[384,1152]{1,0:T(8,128)(2,1)}) custom-call(s32[18]{0:T(128)S(4)} %get-tuple-element.37.info, bf16[432,128]{1,0:T(8,128)(2,1)S(1)} %collective-permute-done.1.xr.rest_5_, bf16[1040,384]{1,0:T(8,128)(2,1)S(1)} %get-tuple-element.43.ktf, ...), custom_call_target="tpu_custom_call" | custom-call | tf_op jit(solution)/shard_map/pallas_call | solution.py:222
  16.1 1.7 %collective-permute-start.5 = (bf16[448,128]{1,0:T(8,128)(2,1)S(1)}, bf16[448,128]{1,0:T(8,128)(2,1)S(1)}, u32[]{:S(2)}, u32[]{:S(2)}) collective-permute-start(bf16[448,128]{1,0:T(8,128)(2,1)S(1)} %get-tuple-element.57), channel_id=1, source_target_pairs={{0,1},{1,0},{2,3},{3,2},{4,5},{5,4},{6,7},{7,6},{8,9},{9,8},{10,11... | collective-permute-start | bytes 344072 | tf_op jit(solution)/shard_map/ppermute | solution.py:486
  17.8 0.0 collective-permute-done.3.xr.rest_6_
  17.8 0.9 %shard_map.107 = (bf16[304,128]{1,0:T(8,128)(2,1)S(1)}, f32[320,256]{1,0:T(8,128)S(1)}) custom-call(s32[18]{0:T(128)S(4)} %get-tuple-element.37.info, bf16[448,128]{1,0:T(8,128)(2,1)S(1)} %collective-permute-done.3.xr.rest_6_, bf16[1040,384]{1,0:T(8,128)(2,1)S(1)} %get-tuple-element.43.ktf, bf16[1040,384]{1,0:T(8,128)(2,1)S(1)} %get-tuple-element.47.vtf, ...), custom_call_target="tpu_custom_call" | custom-call | tf_op jit(solution)/shard_map/pallas_call | solution.py:222
  18.6 0.3 collective-permute-start.6
  18.9 1.6 %collective-permute-done.4.xr.rest_7_ = bf16[448,128]{1,0:T(8,128)(2,1)S(1)} collective-permute-done((bf16[448,128]{1,0:T(8,128)(2,1)S(1)}, bf16[448,128]{1,0:T(8,128)(2,1)S(1)}, u32[]{:S(2)}, u32[]{:S(2)}) %collective-permute-start.4) | collective-permute-done | bytes 114720 | tf_op jit(solution)/shard_map/ppermute | solution.py:486
  20.5 0.9 %shard_map.108 = (bf16[304,128]{1,0:T(8,128)(2,1)S(1)}, f32[320,256]{1,0:T(8,128)S(1)}) custom-call(s32[18]{0:T(128)S(4)} %get-tuple-element.37.info, bf16[448,128]{1,0:T(8,128)(2,1)S(1)} %collective-permute-done.4.xr.rest_7_, bf16[1040,384]{1,0:T(8,128)(2,1)S(1)} %get-tuple-element.43.ktf, bf16[1040,384]{1,0:T(8,128)(2,1)S(1)} %get-tuple-element.47.vtf, ...), custom_call_target="tpu_custom_call" | custom-call | tf_op jit(solution)/shard_map/pallas_call | solution.py:222
  21.4 0.1 collective-permute-start.7
  21.5 1.5 %collective-permute-done.5.rest_8_ = bf16[448,128]{1,0:T(8,128)(2,1)S(1)} collective-permute-done((bf16[448,128]{1,0:T(8,128)(2,1)S(1)}, bf16[448,128]{1,0:T(8,128)(2,1)S(1)}, u32[]{:S(2)}, u32[]{:S(2)}) %collective-permute-start.5) | collective-permute-done | bytes 114720 | tf_op jit(solution)/shard_map/ppermute | solution.py:486
  23.0 1.9 %shard_map.109 = (f32[160,256]{1,0:T(8,128)S(1)}, f32[384,256]{1,0:T(8,128)S(1)}, bf16[384,1152]{1,0:T(8,128)(2,1)}) custom-call(s32[18]{0:T(128)S(4)} %get-tuple-element.37.info, bf16[384,1152]{1,0:T(8,128)(2,1)} %so.1, bf16[1280,384]{1,0:T(8,128)(2,1)S(1)} %get-tuple-element.49.rest_0_.kt, ...), custom_call_target="tpu_custom_call", output_to_operand_aliasing={{2}: (18, {})} | custom-call | tf_op jit(solution)/shard_map/pallas_call | solution.py:222
  24.8 0.0 collective-permute-done.6.theirs
  24.9 0.8 %shard_map.110 = (f32[256,256]{1,0:T(8,128)S(1)}, bf16[384,1152]{1,0:T(8,128)(2,1)}) custom-call(s32[18]{0:T(128)S(4)} %get-tuple-element.37.info, f32[384,256]{1,0:T(8,128)S(1)} %get-tuple-element.62.keep, bf16[304,128]{1,0:T(8,128)(2,1)S(1)} %collective-permute-done.6.theirs, ...), custom_call_target="tpu_custom_call", output_to_operand_aliasing={{1}: (7, {})} | custom-call | tf_op jit(solution)/shard_map/pallas_call | solution.py:222
  25.7 0.2 collective-permute-done.7.theirs
  25.9 0.8 %shard_map.111 = bf16[384,1152]{1,0:T(8,128)(2,1)} custom-call(s32[18]{0:T(128)S(4)} %get-tuple-element.37.info, f32[256,256]{1,0:T(8,128)S(1)} %get-tuple-element.66.left, bf16[304,128]{1,0:T(8,128)(2,1)S(1)} %collective-permute-done.7.theirs, f32[480,256]{1,0:T(8,128)S(1)} %get-tuple-element.58.rest_9_.rest_0_, ...), custom_call_target="tpu_custom_call", output_to_operand_aliasing={{}: (7, {})} | custom-call | tf_op jit(solution)/shard_map/pallas_call | solution.py:222
  (1 shorter events, 0.0 us)
Async XLA Ops:
  0.0 6.9 %copy-start = (bf16[1152,3456]{1,0:T(8,128)(2,1)S(1)}, bf16[1152,3456]{1,0:T(8,128)(2,1)}, u32[]{:S(2)}) copy-start(bf16[1152,3456]{1,0:T(8,128)(2,1)} %rest_3_) | copy-start | bytes 23887876
  2.5 5.8 %collective-permute-start.2 = (bf16[432,128]{1,0:T(8,128)(2,1)S(1)}, bf16[432,128]{1,0:T(8,128)(2,1)S(1)}, u32[]{:S(2)}, u32[]{:S(2)}) collective-permute-start(bf16[432,128]{1,0:T(8,128)(2,1)S(1)} %get-tuple-element.44.rest_2_.rest_3_.rest_0_), channel_id=1, source_target_pairs={{0,1},{1,0},{2,3},{3,2},{4,5},{5,4},{6,7},{7,6},{8,9},{9,8},{10,11... | collective-permute-start | bytes 331784 | tf_op jit(solution)/shard_map/ppermute | solution.py:486
  5.5 7.8 %collective-permute-start = (bf16[432,128]{1,0:T(8,128)(2,1)S(1)}, bf16[432,128]{1,0:T(8,128)(2,1)S(1)}, u32[]{:S(2)}, u32[]{:S(2)}) collective-permute-start(bf16[432,128]{1,0:T(8,128)(2,1)S(1)} %get-tuple-element.42.rest_3_.rest_4_.rest_1_), channel_id=1, source_target_pairs={{0,1},{1,0},{2,3},{3,2},{4,5},{5,4},{6,7},{7,6},{8,9},{9,8},{10,11... | collective-permute-start | bytes 331784 | tf_op jit(solution)/shard_map/ppermute | solution.py:486
  7.8 7.1 %collective-permute-start.1 = (bf16[432,128]{1,0:T(8,128)(2,1)S(1)}, bf16[432,128]{1,0:T(8,128)(2,1)S(1)}, u32[]{:S(2)}, u32[]{:S(2)}) collective-permute-start(bf16[432,128]{1,0:T(8,128)(2,1)S(1)} %get-tuple-element.50.rest_4_.rest_5_.rest_2_), channel_id=1, source_target_pairs={{0,1},{1,0},{2,3},{3,2},{4,5},{5,4},{6,7},{7,6},{8,9},{9,8},{10,11... | collective-permute-start | bytes 331784 | tf_op jit(solution)/shard_map/ppermute | solution.py:486
  8.2 9.5 %collective-permute-start.3 = (bf16[448,128]{1,0:T(8,128)(2,1)S(1)}, bf16[448,128]{1,0:T(8,128)(2,1)S(1)}, u32[]{:S(2)}, u32[]{:S(2)}) collective-permute-start(bf16[448,128]{1,0:T(8,128)(2,1)S(1)} %shard_map.106), channel_id=1, source_target_pairs={{0,1},{1,0},{2,3},{3,2},{4,5},{5,4},{6,7},{7,6},{8,9},{9,8},{10,11... | collective-permute-start | bytes 344072 | tf_op jit(solution)/shard_map/ppermute | solution.py:486
  14.8 5.7 %collective-permute-start.4 = (bf16[448,128]{1,0:T(8,128)(2,1)S(1)}, bf16[448,128]{1,0:T(8,128)(2,1)S(1)}, u32[]{:S(2)}, u32[]{:S(2)}) collective-permute-start(bf16[448,128]{1,0:T(8,128)(2,1)S(1)} %get-tuple-element.56), channel_id=1, source_target_pairs={{0,1},{1,0},{2,3},{3,2},{4,5},{5,4},{6,7},{7,6},{8,9},{9,8},{10,11... | collective-permute-start | bytes 344072 | tf_op jit(solution)/shard_map/ppermute | solution.py:486
  16.1 6.9 %collective-permute-start.5 = (bf16[448,128]{1,0:T(8,128)(2,1)S(1)}, bf16[448,128]{1,0:T(8,128)(2,1)S(1)}, u32[]{:S(2)}, u32[]{:S(2)}) collective-permute-start(bf16[448,128]{1,0:T(8,128)(2,1)S(1)} %get-tuple-element.57), channel_id=1, source_target_pairs={{0,1},{1,0},{2,3},{3,2},{4,5},{5,4},{6,7},{7,6},{8,9},{9,8},{10,11... | collective-permute-start | bytes 344072 | tf_op jit(solution)/shard_map/ppermute | solution.py:486
  18.6 6.2 %collective-permute-start.6 = (bf16[304,128]{1,0:T(8,128)(2,1)S(1)}, bf16[304,128]{1,0:T(8,128)(2,1)S(1)}, u32[]{:S(2)}, u32[]{:S(2)}) collective-permute-start(bf16[304,128]{1,0:T(8,128)(2,1)S(1)} %get-tuple-element.63), channel_id=1, source_target_pairs={{0,1},{1,0},{2,3},{3,2},{4,5},{5,4},{6,7},{7,6},{8,9},{9,8},{10,11... | collective-permute-start | bytes 233480 | tf_op jit(solution)/shard_map/ppermute | solution.py:486
  21.4 4.5 %collective-permute-start.7 = (bf16[304,128]{1,0:T(8,128)(2,1)S(1)}, bf16[304,128]{1,0:T(8,128)(2,1)S(1)}, u32[]{:S(2)}, u32[]{:S(2)}) collective-permute-start(bf16[304,128]{1,0:T(8,128)(2,1)S(1)} %get-tuple-element.67), channel_id=1, source_target_pairs={{0,1},{1,0},{2,3},{3,2},{4,5},{5,4},{6,7},{7,6},{8,9},{9,8},{10,11... | collective-permute-start | bytes 233480 | tf_op jit(solution)/shard_map/ppermute | solution.py:486

commit v5 on v4

--- a/solution.py
+++ b/solution.py
@@ -168,7 +168,7 @@
     if head_size % 8 or fresh_rows // LANES * head_size % 16 or 2 * own_rows // LANES * head_size % 16:
         return None
     asked = head_count - LAG
-    late = -(-(asked - LAG * ratio) // (LAG - 1))
+    late = min(ratio, asked - LAG * ratio - 1)
     if not 0 < late <= ratio:
         return None
     chunks = [tuple(range(h, h + ratio)) for h in range(0, LAG * ratio, ratio)]
@@ -230,7 +230,7 @@
         )(*ins)
 
     def tail_rows(n):
-        return ceil_to(2 * QB * n, 16)
+        return ceil_to(QB * n, 8)
 
     def step_rows(s):
         rows = [QR * len(chunks[s])] if s < len(chunks) else []
@@ -292,22 +292,14 @@
             terms = score(query_of(x, i), head_of(kt, h), head_of(vt, h))
             target[QR * i : QR * (i + 1), :] = pieces([terms[:HD]])
             total = terms[HD : HD + 1]
-            top = total.astype(bf16).astype(f32)
-            for k, piece in enumerate((top, total - top)):
-                for b in range(QB):
-                    row = (2 * i + k) * QB + b
-                    tail = jnp.where(place == row, piece[:, LANES * b : LANES * (b + 1)], tail)
+            for b in range(QB):
+                tail = jnp.where(place == QB * i + b, total[:, LANES * b : LANES * (b + 1)], tail)
         target[QR * n : QR * n + count, :] = tail.astype(bf16)
 
     def total_of(tail, i):
-        parts = [
-            tail[(2 * i) * QB + b : (2 * i) * QB + b + 1, :]
-            + tail[(2 * i + 1) * QB + b : (2 * i + 1) * QB + b + 1, :]
-            for b in range(QB)
-        ]
-        return jnp.concatenate(parts, axis=1)
-
-    bounds = (0, 3 * heads // 8, 5 * heads // 8, 7 * heads // 8, heads)
+        return jnp.concatenate([tail[QB * i + b : QB * i + b + 1, :] for b in range(QB)], axis=1)
+
+    bounds = (0, 7 * heads // 16, 3 * heads // 4, 7 * heads // 8, heads)
     groups = [tuple(range(a, b)) for a, b in zip(bounds, bounds[1:])]
 
     def own_terms(own, h):
@@ -599,9 +591,9 @@
 
         def reply(info, xr, ktf, vtf, stash, *rest, c=c, qs=qs, after=after, group=group):
             if c == project_at:
-                gains, keys_turned, hid, w, sv, so, x, vnew, kt, vall, held, sems = rest
+                hid, w, sv, so, x, vnew, vall, held, sems = rest
             elif c == turn_at:
-                kt, qx, *sent, vnew, vall, held, x, terms, vt, out, mix, turned, sem = rest
+                gains, keys_turned, qx, *sent, vnew, vall, held, x, terms, kt, vt, out, mix, turned, sem = rest
             elif group:
                 kt, vt, qx, *sent, x, terms = rest
             else:
@@ -622,15 +614,15 @@
                     ocopy = pltpu.make_async_copy(so, held, sems.at[1])
                     ocopy.start()
                     vnew[...] = jnp.dot(hid[...], w[:, 2 * D :], preferred_element_type=f32).astype(bf16)
-                    gain = gains[HD : 2 * HD, :]
-                    for h in range(heads):
-                        part = normed(keys_turned[HD * h : HD * (h + 1), :], gain)
-                        kt[HP * h : HP * (h + 1), :] = padded(part, 0.0)
                     vcopy.wait()
                     ocopy.wait()
                 if c == turn_at:
                     ocopy = pltpu.make_async_copy(held, out, sem)
                     ocopy.start()
+                    gain = gains[HD : 2 * HD, :]
+                    for h in range(heads):
+                        part = normed(keys_turned[HD * h : HD * (h + 1), :], gain)
+                        kt[HP * h : HP * (h + 1), :] = padded(part, 0.0)
                     mix[...] = vall[...]
                     settle(info, vnew, mix)
                     turn(mix, 0, D, turned)
@@ -648,16 +640,17 @@
         spaces = [VM]
         scratch = []
         if c == project_at:
-            ins += [gains, keys_turned, hidden, late_weight, far(stale_values), far(stale_output)]
-            given += [VM] * 4 + [ANY] * 2
-            outs += [near(R, D, bf16), near(HP * heads, N, bf16), near(N, D, bf16), near(N, D, bf16)]
-            spaces += [VM] * 4
+            ins += [hidden, late_weight, far(stale_values), far(stale_output)]
+            given += [VM] * 2 + [ANY] * 2
+            outs += [near(R, D, bf16), near(N, D, bf16), near(N, D, bf16)]
+            spaces += [VM] * 3
             scratch = [DMA((2,))]
         elif c == turn_at:
-            ins += [kt, qx, *sent, vnew, vall, held]
-            given += [VM] * (5 + len(sent))
-            outs += [near(HP * len(group), R, f32), near(HP * heads, N, bf16), jax.ShapeDtypeStruct((N, D), bf16)]
-            spaces += [VM, VM, ANY]
+            ins += [gains, keys_turned, qx, *sent, vnew, vall, held]
+            given += [VM] * (6 + len(sent))
+            outs += [near(HP * len(group), R, f32)] + [near(HP * heads, N, bf16)] * 2
+            outs += [jax.ShapeDtypeStruct((N, D), bf16)]
+            spaces += [VM] * 3 + [ANY]
             scratch = [vm((N, D), bf16), vm((D, N), f32), DMA]
         elif group:
             ins += [kt, vt, qx, *sent]
@@ -668,11 +661,11 @@
         send(res[0])
         told.append(here(got[-1]))
         if c == project_at:
-            vnew, kt, vall, held = map(here, res[1:])
+            vnew, vall, held = map(here, res[1:])
         elif group:
             own.append(here(res[1]))
             if c == turn_at:
-                vt, out = here(res[2]), res[3]
+                kt, vt, out = here(res[2]), here(res[3]), res[4]
 
     answers = chunks
 
@@ -747,36 +740,15 @@
     )
     own.append(here(terms))
 
-    def join(info, keep, theirs, *rest):
-        own, (_, left, out, turned, rows, sems) = rest[: len(groups)], rest[len(groups) :]
-        low, high = open_low[-2], open_low[-1]
+    def last(info, keep, theirs, latest, *rest):
+        own, (_, out, turned, rows, sems) = rest[: len(groups)], rest[len(groups) :]
+        low = open_low[-2]
 
         @pl.when(info[0] > 0)
         def _():
             turned[...] = keep[...]
             merge(lambda h: own_terms(own, h), theirs, answers[-2], turned, low)
-            flush(info, turned, low, rows, out, [(low, high)], sems)
-            left[...] = turned[high - low :, :]
-            settle_rows(rows, out, [(low, high)], sems)
-
-    left, out = call(
-        join,
-        [near(open_high - open_low[-1], R, f32), jax.ShapeDtypeStruct((N, D), bf16)],
-        [VM, ANY],
-        [info, here(keep), told[-2], *own, out],
-        [SM, VM, VM] + [VM] * len(own) + [ANY],
-        [vm((open_high - open_low[-2], R), f32), vm((R, D), bf16), DMA((1,))],
-        {3 + len(own): 1},
-    )
-
-    def last(info, left, theirs, *rest):
-        own, (_, out, turned, rows, sems) = rest[: len(groups)], rest[len(groups) :]
-        low = open_low[-1]
-
-        @pl.when(info[0] > 0)
-        def _():
-            turned[...] = left[...]
-            merge(lambda h: own_terms(own, h), theirs, answers[-1], turned, low)
+            merge(lambda h: own_terms(own, h), latest, answers[-1], turned, low)
             flush(info, turned, low, rows, out, [(low, open_high)], sems)
             settle_rows(rows, out, [(low, open_high)], sems)
 
@@ -784,10 +756,10 @@
         last,
         [jax.ShapeDtypeStruct((N, D), bf16)],
         [ANY],
-        [info, here(left), told[-1], *own, out],
-        [SM, VM, VM] + [VM] * len(own) + [ANY],
-        [vm((open_high - open_low[-1], R), f32), vm((R, D), bf16), DMA((1,))],
-        {3 + len(own): 0},
+        [info, here(keep), *told[-2:], *own, out],
+        [SM, VM, VM, VM] + [VM] * len(own) + [ANY],
+        [vm((open_high - open_low[-2], R), f32), vm((R, D), bf16), DMA((1,))],
+        {4 + len(own): 0},
     )[0]
 
 

time: 26.8 us -> 26.7 us (level)
  starting transfers between devices: 8.71 us -> 10.6 us
  waiting for transfers between devices: 3.58 us -> 2.21 us
  Pallas kernels: 14.2 us -> 13.6 us
    ppermute x8, starting transfers between devices: 8.71 us -> 10.6 us  [send(): got.append(lax.ppermute(array, 'patch', [(0, 1), (1, 0)]))]
    ppermute x8, waiting for transfers between devices: 3.58 us -> 2.21 us  [send(): got.append(lax.ppermute(array, 'patch', [(0, 1), (1, 0)]))]
    pallas_call x12 -> x11, Pallas kernels: 14.2 us -> 13.6 us  [call(): pl.pallas_call(kernel, out_shape=tuple(outs), in_specs=list(in_specs), ou...]
  transfers between devices with their start and end apart: 8 -> 8, of which waited for: 4 -> 4; matrix products, arithmetic and copies ran while one was open for 0% -> 0% of each run, Pallas kernels for 41% -> 39%
where the time goes in v5:
time: 26.7 us; the launch traced here: 26.5 us
  Pallas kernels  13.6 us (51%)
  starting transfers between devices  10.6 us (40%)
  waiting for transfers between devices  2.21 us (8%)
    pallas_call x11, Pallas kernels, call(): pl.pallas_call(kernel, out_shape=tuple(outs), in_specs=list(in_specs), ou...  13.6 us
    ppermute x8, starting transfers between devices, send(): got.append(lax.ppermute(array, 'patch', [(0, 1), (1, 0)]))  10.6 us
    ppermute x8, waiting for transfers between devices, send(): got.append(lax.ppermute(array, 'patch', [(0, 1), (1, 0)]))  2.21 us
  transfers between devices with their start and end apart: 8, of which 4 were waited for; matrix products, arithmetic and copies ran while one was open for 0% of the time, Pallas kernels for 39%

profile of v5, /device:TPU:0, one launch (start us, length us, event | category | flops | bytes accessed | tf_op | source)
XLA Modules:
  0.0 26.5 jit_solution(3898275903663426269)
XLA Ops:
  0.0 0.0 copy-start
  0.0 2.5 %shard_map.100 = (s32[18]{0:T(128)S(4)}, f32[144,128]{1,0:T(8,128)S(1)}, bf16[256,1152]{1,0:T(8,128)(2,1)S(1)}, bf16[1152,512]{1,0:T(8,128)(2,1)S(1)}, bf16[432,...) custom-call(s32[48]{0:T(128)} %flags.1, bf16[384,1152]{1,0:T(8,128)(2,1)} %tok.1, bf16[1152,3456]{1,0:T(8,128)(2,1)} %rest_1_, ...), custom_call_target="tpu_custom_call" | custom-call | tf_op jit(solution)/shard_map/pallas_call | solution.py:222
  2.5 2.4 %collective-permute-start.2 = (bf16[432,128]{1,0:T(8,128)(2,1)S(1)}, bf16[432,128]{1,0:T(8,128)(2,1)S(1)}, u32[]{:S(2)}, u32[]{:S(2)}) collective-permute-start(bf16[432,128]{1,0:T(8,128)(2,1)S(1)} %get-tuple-element.38.rest_3_.rest_0_), channel_id=1, source_target_pairs={{0,1},{1,0},{2,3},{3,2},{4,5},{5,4},{6,7},{7,6},{8,9},{9,8},{10,11... | collective-permute-start | bytes 331784 | tf_op jit(solution)/shard_map/ppermute | solution.py:478
  4.9 0.6 %shard_map.101 = (bf16[432,128]{1,0:T(8,128)(2,1)S(1)}, bf16[1040,384]{1,0:T(8,128)(2,1)S(1)}, bf16[384,1152]{1,0:T(8,128)(2,1)S(1)}) custom-call(s32[18]{0:T(128)S(4)} %get-tuple-element.35.info, f32[144,128]{1,0:T(8,128)S(1)} %get-tuple-element.36.gains.rest_0_, bf16[256,1152]{1,0:T(8,128)(2,1)S(1)} %get-tuple-element.37.hid.rest_0_, ...), custom_call_target="tpu_custom_call" | custom-call | tf_op jit(solution)/shard_map/pallas_call | solution.py:222
  5.5 1.4 %collective-permute-start.1 = (bf16[432,128]{1,0:T(8,128)(2,1)S(1)}, bf16[432,128]{1,0:T(8,128)(2,1)S(1)}, u32[]{:S(2)}, u32[]{:S(2)}) collective-permute-start(bf16[432,128]{1,0:T(8,128)(2,1)S(1)} %get-tuple-element.48.rest_4_.rest_1_), channel_id=1, source_target_pairs={{0,1},{1,0},{2,3},{3,2},{4,5},{5,4},{6,7},{7,6},{8,9},{9,8},{10,11... | collective-permute-start | bytes 331784 | tf_op jit(solution)/shard_map/ppermute | solution.py:478
  6.9 0.0 copy-done
  6.9 0.9 %shard_map.102 = (bf16[432,128]{1,0:T(8,128)(2,1)S(1)}, bf16[576,128]{1,0:T(8,128)(2,1)S(1)}, bf16[240,256]{1,0:T(8,128)(2,1)S(1)}, bf16[1040,384]{1,0:T(8,128)(2,1)S(1)}) custom-call(s32[18]{0:T(128)S(4)} %get-tuple-element.35.info, f32[144,128]{1,0:T(8,128)S(1)} %get-tuple-element.36.gains.rest_0_, bf16[256,1152]{1,0:T(8,128)(2,1)S(1)} %get-tuple-element.37.hid.rest_0_, ...), custom_call_target="tpu_custom_call" | custom-call | tf_op jit(solution)/shard_map/pallas_call | solution.py:222
  7.8 0.4 %collective-permute-done.2.xr.rest_3_ = bf16[432,128]{1,0:T(8,128)(2,1)S(1)} collective-permute-done((bf16[432,128]{1,0:T(8,128)(2,1)S(1)}, bf16[432,128]{1,0:T(8,128)(2,1)S(1)}, u32[]{:S(2)}, u32[]{:S(2)}) %collective-permute-start.2) | collective-permute-done | bytes 110624 | tf_op jit(solution)/shard_map/ppermute | solution.py:478
  8.3 2.6 %collective-permute-start.3 = (bf16[440,128]{1,0:T(8,128)(2,1)S(1)}, bf16[440,128]{1,0:T(8,128)(2,1)S(1)}, u32[]{:S(2)}, u32[]{:S(2)}) collective-permute-start(bf16[440,128]{1,0:T(8,128)(2,1)S(1)} %shard_map.106), channel_id=1, source_target_pairs={{0,1},{1,0},{2,3},{3,2},{4,5},{5,4},{6,7},{7,6},{8,9},{9,8},{10,11... | collective-permute-start | bytes 337928 | tf_op jit(solution)/shard_map/ppermute | solution.py:478
  10.9 0.1 collective-permute-start
  10.9 0.0 collective-permute-done.1.xr.rest_4_
  10.9 1.5 %shard_map.104 = (bf16[440,128]{1,0:T(8,128)(2,1)S(1)}, bf16[256,1152]{1,0:T(8,128)(2,1)S(1)}, bf16[384,1152]{1,0:T(8,128)(2,1)S(1)}, bf16[384,1152]{1,0:T(8,128)(2,1)S(1)}) custom-call(s32[18]{0:T(128)S(4)} %get-tuple-element.35.info, bf16[432,128]{1,0:T(8,128)(2,1)S(1)} %collective-permute-done.1.xr.rest_4_, bf16[1040,384]{1,0:T(8,128)(2,1)S(1)} %get-tuple-element.44.ktf, ...), custom_call_target="tpu_custom_call" | custom-call | tf_op jit(solution)/shard_map/pallas_call | solution.py:222
  12.4 1.3 %collective-permute-start.4 = (bf16[440,128]{1,0:T(8,128)(2,1)S(1)}, bf16[440,128]{1,0:T(8,128)(2,1)S(1)}, u32[]{:S(2)}, u32[]{:S(2)}) collective-permute-start(bf16[440,128]{1,0:T(8,128)(2,1)S(1)} %get-tuple-element.54), channel_id=1, source_target_pairs={{0,1},{1,0},{2,3},{3,2},{4,5},{5,4},{6,7},{7,6},{8,9},{9,8},{10,11... | collective-permute-start | bytes 337928 | tf_op jit(solution)/shard_map/ppermute | solution.py:478
  13.8 2.4 %shard_map.103.rest_1_ = f32[1152,384]{1,0:T(8,128)S(1)} custom-call(s32[18]{0:T(128)S(4)} %get-tuple-element.35.info, bf16[256,1152]{1,0:T(8,128)(2,1)S(1)} %get-tuple-element.37.hid.rest_0_, bf16[1152,3456]{1,0:T(8,128)(2,1)S(1)} %copy-done, bf16[384,1152]{1,0:T(8,128)(2,1)} %sk.5), custom_call_target="tpu_custom_call" | custom-call | tf_op jit(solution)/shard_map/pallas_call | solution.py:222
  16.2 0.4 %collective-permute-done.xr.rest_5_ = bf16[432,128]{1,0:T(8,128)(2,1)S(1)} collective-permute-done((bf16[432,128]{1,0:T(8,128)(2,1)S(1)}, bf16[432,128]{1,0:T(8,128)(2,1)S(1)}, u32[]{:S(2)}, u32[]{:S(2)}) %collective-permute-start) | collective-permute-done | bytes 110624 | tf_op jit(solution)/shard_map/ppermute | solution.py:478
  16.6 1.4 %shard_map.105 = (bf16[440,128]{1,0:T(8,128)(2,1)S(1)}, f32[560,256]{1,0:T(8,128)S(1)}, bf16[1280,384]{1,0:T(8,128)(2,1)S(1)}, bf16[1280,384]{1,0:T(8,128)(2,1)S(1)}, bf16[384,1152]{1,0:T(8,128)(2,1)}) custom-call(s32[18]{0:T(128)S(4)} %get-tuple-element.35.info, bf16[432,128]{1,0:T(8,128)(2,1)S(1)} %collective-permute-done.xr.rest_5_, ...), custom_call_target="tpu_custom_call" | custom-call | tf_op jit(solution)/shard_map/pallas_call | solution.py:222
  18.1 0.9 %collective-permute-start.5 = (bf16[440,128]{1,0:T(8,128)(2,1)S(1)}, bf16[440,128]{1,0:T(8,128)(2,1)S(1)}, u32[]{:S(2)}, u32[]{:S(2)}) collective-permute-start(bf16[440,128]{1,0:T(8,128)(2,1)S(1)} %get-tuple-element.55), channel_id=1, source_target_pairs={{0,1},{1,0},{2,3},{3,2},{4,5},{5,4},{6,7},{7,6},{8,9},{9,8},{10,11... | collective-permute-start | bytes 337928 | tf_op jit(solution)/shard_map/ppermute | solution.py:478
  19.0 0.0 collective-permute-done.3.xr.rest_6_
  19.0 1.0 %shard_map.107 = (bf16[440,128]{1,0:T(8,128)(2,1)S(1)}, f32[400,256]{1,0:T(8,128)S(1)}) custom-call(s32[18]{0:T(128)S(4)} %get-tuple-element.35.info, bf16[440,128]{1,0:T(8,128)(2,1)S(1)} %collective-permute-done.3.xr.rest_6_, bf16[1040,384]{1,0:T(8,128)(2,1)S(1)} %get-tuple-element.44.ktf, bf16[1040,384]{1,0:T(8,128)(2,1)S(1)} %get-tuple-element.45.vtf, ...), custom_call_target="tpu_custom_call" | custom-call | tf_op jit(solution)/shard_map/pallas_call | solution.py:222
  20.0 1.1 %collective-permute-start.6 = (bf16[440,128]{1,0:T(8,128)(2,1)S(1)}, bf16[440,128]{1,0:T(8,128)(2,1)S(1)}, u32[]{:S(2)}, u32[]{:S(2)}) collective-permute-start(bf16[440,128]{1,0:T(8,128)(2,1)S(1)} %get-tuple-element.61), channel_id=1, source_target_pairs={{0,1},{1,0},{2,3},{3,2},{4,5},{5,4},{6,7},{7,6},{8,9},{9,8},{10,11... | collective-permute-start | bytes 337928 | tf_op jit(solution)/shard_map/ppermute | solution.py:478
  21.0 0.0 collective-permute-done.4.xr.rest_7_
  21.0 0.7 %shard_map.108 = (bf16[152,128]{1,0:T(8,128)(2,1)S(1)}, f32[160,256]{1,0:T(8,128)S(1)}) custom-call(s32[18]{0:T(128)S(4)} %get-tuple-element.35.info, bf16[440,128]{1,0:T(8,128)(2,1)S(1)} %collective-permute-done.4.xr.rest_7_, bf16[1040,384]{1,0:T(8,128)(2,1)S(1)} %get-tuple-element.44.ktf, bf16[1040,384]{1,0:T(8,128)(2,1)S(1)} %get-tuple-element.45.vtf, ...), custom_call_target="tpu_custom_call" | custom-call | tf_op jit(solution)/shard_map/pallas_call | solution.py:222
  21.7 0.9 %collective-permute-start.7 = (bf16[152,128]{1,0:T(8,128)(2,1)S(1)}, bf16[152,128]{1,0:T(8,128)(2,1)S(1)}, u32[]{:S(2)}, u32[]{:S(2)}) collective-permute-start(bf16[152,128]{1,0:T(8,128)(2,1)S(1)} %get-tuple-element.62), channel_id=1, source_target_pairs={{0,1},{1,0},{2,3},{3,2},{4,5},{5,4},{6,7},{7,6},{8,9},{9,8},{10,11... | collective-permute-start | bytes 116744 | tf_op jit(solution)/shard_map/ppermute | solution.py:478
  22.5 0.7 %collective-permute-done.5.rest_8_ = bf16[440,128]{1,0:T(8,128)(2,1)S(1)} collective-permute-done((bf16[440,128]{1,0:T(8,128)(2,1)S(1)}, bf16[440,128]{1,0:T(8,128)(2,1)S(1)}, u32[]{:S(2)}, u32[]{:S(2)}) %collective-permute-start.5) | collective-permute-done | bytes 112672 | tf_op jit(solution)/shard_map/ppermute | solution.py:478
  23.2 1.9 %shard_map.109 = (f32[160,256]{1,0:T(8,128)S(1)}, f32[384,256]{1,0:T(8,128)S(1)}, bf16[384,1152]{1,0:T(8,128)(2,1)}) custom-call(s32[18]{0:T(128)S(4)} %get-tuple-element.35.info, bf16[384,1152]{1,0:T(8,128)(2,1)} %so.1, bf16[1280,384]{1,0:T(8,128)(2,1)S(1)} %get-tuple-element.52.rest_0_.kt, ...), custom_call_target="tpu_custom_call", output_to_operand_aliasing={{2}: (18, {})} | custom-call | tf_op jit(solution)/shard_map/pallas_call | solution.py:222
  25.1 0.6 %collective-permute-done.7.latest = bf16[152,128]{1,0:T(8,128)(2,1)S(1)} collective-permute-done((bf16[152,128]{1,0:T(8,128)(2,1)S(1)}, bf16[152,128]{1,0:T(8,128)(2,1)S(1)}, u32[]{:S(2)}, u32[]{:S(2)}) %collective-permute-start.7) | collective-permute-done | bytes 38944 | tf_op jit(solution)/shard_map/ppermute | solution.py:478
  25.7 0.0 collective-permute-done.6.theirs
  25.7 0.8 %shard_map.110 = bf16[384,1152]{1,0:T(8,128)(2,1)} custom-call(s32[18]{0:T(128)S(4)} %get-tuple-element.35.info, f32[384,256]{1,0:T(8,128)S(1)} %get-tuple-element.60.keep, bf16[440,128]{1,0:T(8,128)(2,1)S(1)} %collective-permute-done.6.theirs, bf16[152,128]{1,0:T(8,128)(2,1)S(1)} %collective-permute-done.7.latest, ...), custom_call_target="tpu_custom_call", output_to_operand_aliasing={{}: (8, {})} | custom-call | tf_op jit(solution)/shard_map/pallas_call | solution.py:222
  (1 shorter events, 0.0 us)
Async XLA Ops:
  0.0 6.9 %copy-start = (bf16[1152,3456]{1,0:T(8,128)(2,1)S(1)}, bf16[1152,3456]{1,0:T(8,128)(2,1)}, u32[]{:S(2)}) copy-start(bf16[1152,3456]{1,0:T(8,128)(2,1)} %rest_1_) | copy-start | bytes 23887876
  2.5 5.8 %collective-permute-start.2 = (bf16[432,128]{1,0:T(8,128)(2,1)S(1)}, bf16[432,128]{1,0:T(8,128)(2,1)S(1)}, u32[]{:S(2)}, u32[]{:S(2)}) collective-permute-start(bf16[432,128]{1,0:T(8,128)(2,1)S(1)} %get-tuple-element.38.rest_3_.rest_0_), channel_id=1, source_target_pairs={{0,1},{1,0},{2,3},{3,2},{4,5},{5,4},{6,7},{7,6},{8,9},{9,8},{10,11... | collective-permute-start | bytes 331784 | tf_op jit(solution)/shard_map/ppermute | solution.py:478
  5.5 5.4 %collective-permute-start.1 = (bf16[432,128]{1,0:T(8,128)(2,1)S(1)}, bf16[432,128]{1,0:T(8,128)(2,1)S(1)}, u32[]{:S(2)}, u32[]{:S(2)}) collective-permute-start(bf16[432,128]{1,0:T(8,128)(2,1)S(1)} %get-tuple-element.48.rest_4_.rest_1_), channel_id=1, source_target_pairs={{0,1},{1,0},{2,3},{3,2},{4,5},{5,4},{6,7},{7,6},{8,9},{9,8},{10,11... | collective-permute-start | bytes 331784 | tf_op jit(solution)/shard_map/ppermute | solution.py:478
  8.3 10.7 %collective-permute-start.3 = (bf16[440,128]{1,0:T(8,128)(2,1)S(1)}, bf16[440,128]{1,0:T(8,128)(2,1)S(1)}, u32[]{:S(2)}, u32[]{:S(2)}) collective-permute-start(bf16[440,128]{1,0:T(8,128)(2,1)S(1)} %shard_map.106), channel_id=1, source_target_pairs={{0,1},{1,0},{2,3},{3,2},{4,5},{5,4},{6,7},{7,6},{8,9},{9,8},{10,11... | collective-permute-start | bytes 337928 | tf_op jit(solution)/shard_map/ppermute | solution.py:478
  10.9 5.8 %collective-permute-start = (bf16[432,128]{1,0:T(8,128)(2,1)S(1)}, bf16[432,128]{1,0:T(8,128)(2,1)S(1)}, u32[]{:S(2)}, u32[]{:S(2)}) collective-permute-start(bf16[432,128]{1,0:T(8,128)(2,1)S(1)} %get-tuple-element.43.rest_5_.rest_2_), channel_id=1, source_target_pairs={{0,1},{1,0},{2,3},{3,2},{4,5},{5,4},{6,7},{7,6},{8,9},{9,8},{10,11... | collective-permute-start | bytes 331784 | tf_op jit(solution)/shard_map/ppermute | solution.py:478
  12.4 8.6 %collective-permute-start.4 = (bf16[440,128]{1,0:T(8,128)(2,1)S(1)}, bf16[440,128]{1,0:T(8,128)(2,1)S(1)}, u32[]{:S(2)}, u32[]{:S(2)}) collective-permute-start(bf16[440,128]{1,0:T(8,128)(2,1)S(1)} %get-tuple-element.54), channel_id=1, source_target_pairs={{0,1},{1,0},{2,3},{3,2},{4,5},{5,4},{6,7},{7,6},{8,9},{9,8},{10,11... | collective-permute-start | bytes 337928 | tf_op jit(solution)/shard_map/ppermute | solution.py:478
  18.1 5.2 %collective-permute-start.5 = (bf16[440,128]{1,0:T(8,128)(2,1)S(1)}, bf16[440,128]{1,0:T(8,128)(2,1)S(1)}, u32[]{:S(2)}, u32[]{:S(2)}) collective-permute-start(bf16[440,128]{1,0:T(8,128)(2,1)S(1)} %get-tuple-element.55), channel_id=1, source_target_pairs={{0,1},{1,0},{2,3},{3,2},{4,5},{5,4},{6,7},{7,6},{8,9},{9,8},{10,11... | collective-permute-start | bytes 337928 | tf_op jit(solution)/shard_map/ppermute | solution.py:478
  20.0 5.8 %collective-permute-start.6 = (bf16[440,128]{1,0:T(8,128)(2,1)S(1)}, bf16[440,128]{1,0:T(8,128)(2,1)S(1)}, u32[]{:S(2)}, u32[]{:S(2)}) collective-permute-start(bf16[440,128]{1,0:T(8,128)(2,1)S(1)} %get-tuple-element.61), channel_id=1, source_target_pairs={{0,1},{1,0},{2,3},{3,2},{4,5},{5,4},{6,7},{7,6},{8,9},{9,8},{10,11... | collective-permute-start | bytes 337928 | tf_op jit(solution)/shard_map/ppermute | solution.py:478
  21.7 4.0 %collective-permute-start.7 = (bf16[152,128]{1,0:T(8,128)(2,1)S(1)}, bf16[152,128]{1,0:T(8,128)(2,1)S(1)}, u32[]{:S(2)}, u32[]{:S(2)}) collective-permute-start(bf16[152,128]{1,0:T(8,128)(2,1)S(1)} %get-tuple-element.62), channel_id=1, source_target_pairs={{0,1},{1,0},{2,3},{3,2},{4,5},{5,4},{6,7},{7,6},{8,9},{9,8},{10,11... | collective-permute-start | bytes 116744 | tf_op jit(solution)/shard_map/ppermute | solution.py:478

commit v6 on v5

--- a/solution.py
+++ b/solution.py
@@ -346,12 +346,15 @@
     def turn_back(turned, low, rows, j):
         rows[:, j : j + LANES] = turned[j - low : j - low + LANES, :].T.astype(bf16)
 
-    block_rows = 2 * KB * HD
+    def parcel(st, gains, i):
+        at = HD * shipped[i] - lows
+        key = normed(st[0, at : at + HD, :], gains[HD : 2 * HD, :])
+        return pieces([key, st[1, at : at + HD, :]])
 
     def front(
         flags, tok, w, shift, scale, gq, gk, sk, sv,
-        info, gains, hid, wq, x0, kv,
-        fl, sh, sc, g0, g1, tbuf, kbuf, vbuf, qt, st, sems,
+        info, gains, hid, wq, x0, st,
+        fl, sh, sc, g0, g1, tbuf, kbuf, vbuf, qt, sems,
     ):
         def load(source, target, k):
             copy = pltpu.make_async_copy(source, target, sems.at[k])
@@ -399,14 +402,7 @@
         def _():
             turn(kbuf, 0, D - lows, st.at[0])
             turn(vbuf, 0, D - lows, st.at[1])
-            gain = gains[HD : 2 * HD, :]
-            for i, h in enumerate(shipped):
-                at = HD * h - lows
-                block = pieces([normed(st[0, at : at + HD, :], gain), st[1, at : at + HD, :]])
-                if i == 0:
-                    x0[...] = block
-                else:
-                    kv[block_rows * (i - 1) : block_rows * i, :] = block
+            x0[...] = parcel(st, gains, 0)
 
         cshift.wait()
         cscale.wait()
@@ -443,7 +439,7 @@
             near(R, D, bf16),
             near(D, high1, bf16),
             near(QR * len(chunks[0]), LANES, bf16),
-            near(block_rows * (LAG - 1), LANES, bf16),
+            pltpu.VMEM((2, D - lows, N), f32),
         ],
         [SM] + [VM] * 5,
         [
@@ -464,7 +460,6 @@
             vm((N, D - lows), bf16),
             vm((N, D - lows), bf16),
             vm((high0, R), f32),
-            vm((2, D - lows, N), f32),
             DMA((10,)),
         ],
     )
@@ -498,7 +493,7 @@
             vcopy = pltpu.make_async_copy(sv.at[:, 0:width], vbuf.at[:, 0:width], sems.at[1])
             kcopy.start()
             vcopy.start()
-            x1[...] = kv[0:block_rows, :]
+            x1[...] = parcel(kv, gains, 1)
             gain = gains[HD : 2 * HD, :]
             kcopy.wait()
             turn(kbuf, 0, width, turned)
@@ -538,7 +533,7 @@
 
         @pl.when(info[0] == 0)
         def _():
-            x2[...] = kv[block_rows : 2 * block_rows, :]
+            x2[...] = parcel(kv, gains, 2)
             turn(v_far, 0, ceil_to(HD * asked, LANES), turned)
             for h in range(asked):
                 vt[HP * h : HP * (h + 1), :] = padded(turned[HD * h : HD * (h + 1), :], 1.0)

time: 26.7 us -> 26.7 us (level)
  no operation moved by 1% of the time
where the time goes in v6:
time: 26.7 us; the launch traced here: 26.5 us
  Pallas kernels  13.6 us (51%)
  starting transfers between devices  10.6 us (40%)
  waiting for transfers between devices  2.21 us (8%)
    pallas_call x11, Pallas kernels, call(): pl.pallas_call(kernel, out_shape=tuple(outs), in_specs=list(in_specs), ou...  13.6 us
    ppermute x8, starting transfers between devices, send(): got.append(lax.ppermute(array, 'patch', [(0, 1), (1, 0)]))  10.6 us
    ppermute x8, waiting for transfers between devices, send(): got.append(lax.ppermute(array, 'patch', [(0, 1), (1, 0)]))  2.21 us
  transfers between devices with their start and end apart: 8, of which 4 were waited for; matrix products, arithmetic and copies ran while one was open for 0% of the time, Pallas kernels for 39%

profile of v6, /device:TPU:0, one launch (start us, length us, event | category | flops | bytes accessed | tf_op | source)
XLA Modules:
  0.0 26.5 jit_solution(5742414856198085307)
XLA Ops:
  0.0 0.0 copy-start
  0.0 2.5 %shard_map.100 = (s32[18]{0:T(128)S(4)}, f32[144,128]{1,0:T(8,128)S(1)}, bf16[256,1152]{1,0:T(8,128)(2,1)S(1)}, bf16[1152,512]{1,0:T(8,128)(2,1)S(1)}, bf16[432,...) custom-call(s32[48]{0:T(128)} %flags.1, bf16[384,1152]{1,0:T(8,128)(2,1)} %tok.1, bf16[1152,3456]{1,0:T(8,128)(2,1)} %rest_1_, ...), custom_call_target="tpu_custom_call" | custom-call | tf_op jit(solution)/shard_map/pallas_call | solution.py:222
  2.5 2.4 %collective-permute-start.2 = (bf16[432,128]{1,0:T(8,128)(2,1)S(1)}, bf16[432,128]{1,0:T(8,128)(2,1)S(1)}, u32[]{:S(2)}, u32[]{:S(2)}) collective-permute-start(bf16[432,128]{1,0:T(8,128)(2,1)S(1)} %get-tuple-element.38.rest_3_.rest_0_), channel_id=1, source_target_pairs={{0,1},{1,0},{2,3},{3,2},{4,5},{5,4},{6,7},{7,6},{8,9},{9,8},{10,11... | collective-permute-start | bytes 331784 | tf_op jit(solution)/shard_map/ppermute | solution.py:473
  4.9 0.6 %shard_map.101 = (bf16[432,128]{1,0:T(8,128)(2,1)S(1)}, bf16[1040,384]{1,0:T(8,128)(2,1)S(1)}, bf16[384,1152]{1,0:T(8,128)(2,1)S(1)}) custom-call(s32[18]{0:T(128)S(4)} %get-tuple-element.35.info, f32[144,128]{1,0:T(8,128)S(1)} %get-tuple-element.36.gains.rest_0_, bf16[256,1152]{1,0:T(8,128)(2,1)S(1)} %get-tuple-element.37.hid.rest_0_, ...), custom_call_target="tpu_custom_call" | custom-call | tf_op jit(solution)/shard_map/pallas_call | solution.py:222
  5.5 1.4 %collective-permute-start.1 = (bf16[432,128]{1,0:T(8,128)(2,1)S(1)}, bf16[432,128]{1,0:T(8,128)(2,1)S(1)}, u32[]{:S(2)}, u32[]{:S(2)}) collective-permute-start(bf16[432,128]{1,0:T(8,128)(2,1)S(1)} %get-tuple-element.48.rest_4_.rest_1_), channel_id=1, source_target_pairs={{0,1},{1,0},{2,3},{3,2},{4,5},{5,4},{6,7},{7,6},{8,9},{9,8},{10,11... | collective-permute-start | bytes 331784 | tf_op jit(solution)/shard_map/ppermute | solution.py:473
  6.9 0.0 copy-done
  6.9 0.9 %shard_map.102 = (bf16[432,128]{1,0:T(8,128)(2,1)S(1)}, bf16[576,128]{1,0:T(8,128)(2,1)S(1)}, bf16[240,256]{1,0:T(8,128)(2,1)S(1)}, bf16[1040,384]{1,0:T(8,128)(2,1)S(1)}) custom-call(s32[18]{0:T(128)S(4)} %get-tuple-element.35.info, f32[144,128]{1,0:T(8,128)S(1)} %get-tuple-element.36.gains.rest_0_, bf16[256,1152]{1,0:T(8,128)(2,1)S(1)} %get-tuple-element.37.hid.rest_0_, ...), custom_call_target="tpu_custom_call" | custom-call | tf_op jit(solution)/shard_map/pallas_call | solution.py:222
  7.8 0.4 %collective-permute-done.2.xr.rest_3_ = bf16[432,128]{1,0:T(8,128)(2,1)S(1)} collective-permute-done((bf16[432,128]{1,0:T(8,128)(2,1)S(1)}, bf16[432,128]{1,0:T(8,128)(2,1)S(1)}, u32[]{:S(2)}, u32[]{:S(2)}) %collective-permute-start.2) | collective-permute-done | bytes 110624 | tf_op jit(solution)/shard_map/ppermute | solution.py:473
  8.3 2.6 %collective-permute-start.3 = (bf16[440,128]{1,0:T(8,128)(2,1)S(1)}, bf16[440,128]{1,0:T(8,128)(2,1)S(1)}, u32[]{:S(2)}, u32[]{:S(2)}) collective-permute-start(bf16[440,128]{1,0:T(8,128)(2,1)S(1)} %shard_map.106), channel_id=1, source_target_pairs={{0,1},{1,0},{2,3},{3,2},{4,5},{5,4},{6,7},{7,6},{8,9},{9,8},{10,11... | collective-permute-start | bytes 337928 | tf_op jit(solution)/shard_map/ppermute | solution.py:473
  10.9 0.1 collective-permute-start
  10.9 0.0 collective-permute-done.1.xr.rest_4_
  10.9 1.5 %shard_map.104 = (bf16[440,128]{1,0:T(8,128)(2,1)S(1)}, bf16[256,1152]{1,0:T(8,128)(2,1)S(1)}, bf16[384,1152]{1,0:T(8,128)(2,1)S(1)}, bf16[384,1152]{1,0:T(8,128)(2,1)S(1)}) custom-call(s32[18]{0:T(128)S(4)} %get-tuple-element.35.info, bf16[432,128]{1,0:T(8,128)(2,1)S(1)} %collective-permute-done.1.xr.rest_4_, bf16[1040,384]{1,0:T(8,128)(2,1)S(1)} %get-tuple-element.44.ktf, ...), custom_call_target="tpu_custom_call" | custom-call | tf_op jit(solution)/shard_map/pallas_call | solution.py:222
  12.4 1.3 %collective-permute-start.4 = (bf16[440,128]{1,0:T(8,128)(2,1)S(1)}, bf16[440,128]{1,0:T(8,128)(2,1)S(1)}, u32[]{:S(2)}, u32[]{:S(2)}) collective-permute-start(bf16[440,128]{1,0:T(8,128)(2,1)S(1)} %get-tuple-element.54), channel_id=1, source_target_pairs={{0,1},{1,0},{2,3},{3,2},{4,5},{5,4},{6,7},{7,6},{8,9},{9,8},{10,11... | collective-permute-start | bytes 337928 | tf_op jit(solution)/shard_map/ppermute | solution.py:473
  13.8 2.4 %shard_map.103.rest_1_ = f32[1152,384]{1,0:T(8,128)S(1)} custom-call(s32[18]{0:T(128)S(4)} %get-tuple-element.35.info, bf16[256,1152]{1,0:T(8,128)(2,1)S(1)} %get-tuple-element.37.hid.rest_0_, bf16[1152,3456]{1,0:T(8,128)(2,1)S(1)} %copy-done, bf16[384,1152]{1,0:T(8,128)(2,1)} %sk.5), custom_call_target="tpu_custom_call" | custom-call | tf_op jit(solution)/shard_map/pallas_call | solution.py:222
  16.2 0.4 %collective-permute-done.xr.rest_5_ = bf16[432,128]{1,0:T(8,128)(2,1)S(1)} collective-permute-done((bf16[432,128]{1,0:T(8,128)(2,1)S(1)}, bf16[432,128]{1,0:T(8,128)(2,1)S(1)}, u32[]{:S(2)}, u32[]{:S(2)}) %collective-permute-start) | collective-permute-done | bytes 110624 | tf_op jit(solution)/shard_map/ppermute | solution.py:473
  16.6 1.4 %shard_map.105 = (bf16[440,128]{1,0:T(8,128)(2,1)S(1)}, f32[560,256]{1,0:T(8,128)S(1)}, bf16[1280,384]{1,0:T(8,128)(2,1)S(1)}, bf16[1280,384]{1,0:T(8,128)(2,1)S(1)}, bf16[384,1152]{1,0:T(8,128)(2,1)}) custom-call(s32[18]{0:T(128)S(4)} %get-tuple-element.35.info, bf16[432,128]{1,0:T(8,128)(2,1)S(1)} %collective-permute-done.xr.rest_5_, ...), custom_call_target="tpu_custom_call" | custom-call | tf_op jit(solution)/shard_map/pallas_call | solution.py:222
  18.1 0.9 %collective-permute-start.5 = (bf16[440,128]{1,0:T(8,128)(2,1)S(1)}, bf16[440,128]{1,0:T(8,128)(2,1)S(1)}, u32[]{:S(2)}, u32[]{:S(2)}) collective-permute-start(bf16[440,128]{1,0:T(8,128)(2,1)S(1)} %get-tuple-element.55), channel_id=1, source_target_pairs={{0,1},{1,0},{2,3},{3,2},{4,5},{5,4},{6,7},{7,6},{8,9},{9,8},{10,11... | collective-permute-start | bytes 337928 | tf_op jit(solution)/shard_map/ppermute | solution.py:473
  19.0 0.0 collective-permute-done.3.xr.rest_6_
  19.0 1.0 %shard_map.107 = (bf16[440,128]{1,0:T(8,128)(2,1)S(1)}, f32[400,256]{1,0:T(8,128)S(1)}) custom-call(s32[18]{0:T(128)S(4)} %get-tuple-element.35.info, bf16[440,128]{1,0:T(8,128)(2,1)S(1)} %collective-permute-done.3.xr.rest_6_, bf16[1040,384]{1,0:T(8,128)(2,1)S(1)} %get-tuple-element.44.ktf, bf16[1040,384]{1,0:T(8,128)(2,1)S(1)} %get-tuple-element.45.vtf, ...), custom_call_target="tpu_custom_call" | custom-call | tf_op jit(solution)/shard_map/pallas_call | solution.py:222
  19.9 1.1 %collective-permute-start.6 = (bf16[440,128]{1,0:T(8,128)(2,1)S(1)}, bf16[440,128]{1,0:T(8,128)(2,1)S(1)}, u32[]{:S(2)}, u32[]{:S(2)}) collective-permute-start(bf16[440,128]{1,0:T(8,128)(2,1)S(1)} %get-tuple-element.61), channel_id=1, source_target_pairs={{0,1},{1,0},{2,3},{3,2},{4,5},{5,4},{6,7},{7,6},{8,9},{9,8},{10,11... | collective-permute-start | bytes 337928 | tf_op jit(solution)/shard_map/ppermute | solution.py:473
  21.0 0.0 collective-permute-done.4.xr.rest_7_
  21.0 0.7 %shard_map.108 = (bf16[152,128]{1,0:T(8,128)(2,1)S(1)}, f32[160,256]{1,0:T(8,128)S(1)}) custom-call(s32[18]{0:T(128)S(4)} %get-tuple-element.35.info, bf16[440,128]{1,0:T(8,128)(2,1)S(1)} %collective-permute-done.4.xr.rest_7_, bf16[1040,384]{1,0:T(8,128)(2,1)S(1)} %get-tuple-element.44.ktf, bf16[1040,384]{1,0:T(8,128)(2,1)S(1)} %get-tuple-element.45.vtf, ...), custom_call_target="tpu_custom_call" | custom-call | tf_op jit(solution)/shard_map/pallas_call | solution.py:222
  21.7 0.8 %collective-permute-start.7 = (bf16[152,128]{1,0:T(8,128)(2,1)S(1)}, bf16[152,128]{1,0:T(8,128)(2,1)S(1)}, u32[]{:S(2)}, u32[]{:S(2)}) collective-permute-start(bf16[152,128]{1,0:T(8,128)(2,1)S(1)} %get-tuple-element.62), channel_id=1, source_target_pairs={{0,1},{1,0},{2,3},{3,2},{4,5},{5,4},{6,7},{7,6},{8,9},{9,8},{10,11... | collective-permute-start | bytes 116744 | tf_op jit(solution)/shard_map/ppermute | solution.py:473
  22.5 0.7 %collective-permute-done.5.rest_8_ = bf16[440,128]{1,0:T(8,128)(2,1)S(1)} collective-permute-done((bf16[440,128]{1,0:T(8,128)(2,1)S(1)}, bf16[440,128]{1,0:T(8,128)(2,1)S(1)}, u32[]{:S(2)}, u32[]{:S(2)}) %collective-permute-start.5) | collective-permute-done | bytes 112672 | tf_op jit(solution)/shard_map/ppermute | solution.py:473
  23.2 1.9 %shard_map.109 = (f32[160,256]{1,0:T(8,128)S(1)}, f32[384,256]{1,0:T(8,128)S(1)}, bf16[384,1152]{1,0:T(8,128)(2,1)}) custom-call(s32[18]{0:T(128)S(4)} %get-tuple-element.35.info, bf16[384,1152]{1,0:T(8,128)(2,1)} %so.1, bf16[1280,384]{1,0:T(8,128)(2,1)S(1)} %get-tuple-element.52.rest_0_.kt, ...), custom_call_target="tpu_custom_call", output_to_operand_aliasing={{2}: (18, {})} | custom-call | tf_op jit(solution)/shard_map/pallas_call | solution.py:222
  25.1 0.6 %collective-permute-done.7.latest = bf16[152,128]{1,0:T(8,128)(2,1)S(1)} collective-permute-done((bf16[152,128]{1,0:T(8,128)(2,1)S(1)}, bf16[152,128]{1,0:T(8,128)(2,1)S(1)}, u32[]{:S(2)}, u32[]{:S(2)}) %collective-permute-start.7) | collective-permute-done | bytes 38944 | tf_op jit(solution)/shard_map/ppermute | solution.py:473
  25.7 0.0 collective-permute-done.6.theirs
  25.7 0.8 %shard_map.110 = bf16[384,1152]{1,0:T(8,128)(2,1)} custom-call(s32[18]{0:T(128)S(4)} %get-tuple-element.35.info, f32[384,256]{1,0:T(8,128)S(1)} %get-tuple-element.60.keep, bf16[440,128]{1,0:T(8,128)(2,1)S(1)} %collective-permute-done.6.theirs, bf16[152,128]{1,0:T(8,128)(2,1)S(1)} %collective-permute-done.7.latest, ...), custom_call_target="tpu_custom_call", output_to_operand_aliasing={{}: (8, {})} | custom-call | tf_op jit(solution)/shard_map/pallas_call | solution.py:222
  (1 shorter events, 0.0 us)
Async XLA Ops:
  0.0 6.9 %copy-start = (bf16[1152,3456]{1,0:T(8,128)(2,1)S(1)}, bf16[1152,3456]{1,0:T(8,128)(2,1)}, u32[]{:S(2)}) copy-start(bf16[1152,3456]{1,0:T(8,128)(2,1)} %rest_1_) | copy-start | bytes 23887876
  2.5 5.8 %collective-permute-start.2 = (bf16[432,128]{1,0:T(8,128)(2,1)S(1)}, bf16[432,128]{1,0:T(8,128)(2,1)S(1)}, u32[]{:S(2)}, u32[]{:S(2)}) collective-permute-start(bf16[432,128]{1,0:T(8,128)(2,1)S(1)} %get-tuple-element.38.rest_3_.rest_0_), channel_id=1, source_target_pairs={{0,1},{1,0},{2,3},{3,2},{4,5},{5,4},{6,7},{7,6},{8,9},{9,8},{10,11... | collective-permute-start | bytes 331784 | tf_op jit(solution)/shard_map/ppermute | solution.py:473
  5.5 5.4 %collective-permute-start.1 = (bf16[432,128]{1,0:T(8,128)(2,1)S(1)}, bf16[432,128]{1,0:T(8,128)(2,1)S(1)}, u32[]{:S(2)}, u32[]{:S(2)}) collective-permute-start(bf16[432,128]{1,0:T(8,128)(2,1)S(1)} %get-tuple-element.48.rest_4_.rest_1_), channel_id=1, source_target_pairs={{0,1},{1,0},{2,3},{3,2},{4,5},{5,4},{6,7},{7,6},{8,9},{9,8},{10,11... | collective-permute-start | bytes 331784 | tf_op jit(solution)/shard_map/ppermute | solution.py:473
  8.3 10.7 %collective-permute-start.3 = (bf16[440,128]{1,0:T(8,128)(2,1)S(1)}, bf16[440,128]{1,0:T(8,128)(2,1)S(1)}, u32[]{:S(2)}, u32[]{:S(2)}) collective-permute-start(bf16[440,128]{1,0:T(8,128)(2,1)S(1)} %shard_map.106), channel_id=1, source_target_pairs={{0,1},{1,0},{2,3},{3,2},{4,5},{5,4},{6,7},{7,6},{8,9},{9,8},{10,11... | collective-permute-start | bytes 337928 | tf_op jit(solution)/shard_map/ppermute | solution.py:473
  10.9 5.8 %collective-permute-start = (bf16[432,128]{1,0:T(8,128)(2,1)S(1)}, bf16[432,128]{1,0:T(8,128)(2,1)S(1)}, u32[]{:S(2)}, u32[]{:S(2)}) collective-permute-start(bf16[432,128]{1,0:T(8,128)(2,1)S(1)} %get-tuple-element.43.rest_5_.rest_2_), channel_id=1, source_target_pairs={{0,1},{1,0},{2,3},{3,2},{4,5},{5,4},{6,7},{7,6},{8,9},{9,8},{10,11... | collective-permute-start | bytes 331784 | tf_op jit(solution)/shard_map/ppermute | solution.py:473
  12.4 8.6 %collective-permute-start.4 = (bf16[440,128]{1,0:T(8,128)(2,1)S(1)}, bf16[440,128]{1,0:T(8,128)(2,1)S(1)}, u32[]{:S(2)}, u32[]{:S(2)}) collective-permute-start(bf16[440,128]{1,0:T(8,128)(2,1)S(1)} %get-tuple-element.54), channel_id=1, source_target_pairs={{0,1},{1,0},{2,3},{3,2},{4,5},{5,4},{6,7},{7,6},{8,9},{9,8},{10,11... | collective-permute-start | bytes 337928 | tf_op jit(solution)/shard_map/ppermute | solution.py:473
  18.1 5.2 %collective-permute-start.5 = (bf16[440,128]{1,0:T(8,128)(2,1)S(1)}, bf16[440,128]{1,0:T(8,128)(2,1)S(1)}, u32[]{:S(2)}, u32[]{:S(2)}) collective-permute-start(bf16[440,128]{1,0:T(8,128)(2,1)S(1)} %get-tuple-element.55), channel_id=1, source_target_pairs={{0,1},{1,0},{2,3},{3,2},{4,5},{5,4},{6,7},{7,6},{8,9},{9,8},{10,11... | collective-permute-start | bytes 337928 | tf_op jit(solution)/shard_map/ppermute | solution.py:473
  19.9 5.8 %collective-permute-start.6 = (bf16[440,128]{1,0:T(8,128)(2,1)S(1)}, bf16[440,128]{1,0:T(8,128)(2,1)S(1)}, u32[]{:S(2)}, u32[]{:S(2)}) collective-permute-start(bf16[440,128]{1,0:T(8,128)(2,1)S(1)} %get-tuple-element.61), channel_id=1, source_target_pairs={{0,1},{1,0},{2,3},{3,2},{4,5},{5,4},{6,7},{7,6},{8,9},{9,8},{10,11... | collective-permute-start | bytes 337928 | tf_op jit(solution)/shard_map/ppermute | solution.py:473
  21.7 4.0 %collective-permute-start.7 = (bf16[152,128]{1,0:T(8,128)(2,1)S(1)}, bf16[152,128]{1,0:T(8,128)(2,1)S(1)}, u32[]{:S(2)}, u32[]{:S(2)}) collective-permute-start(bf16[152,128]{1,0:T(8,128)(2,1)S(1)} %get-tuple-element.62), channel_id=1, source_target_pairs={{0,1},{1,0},{2,3},{3,2},{4,5},{5,4},{6,7},{7,6},{8,9},{9,8},{10,11... | collective-permute-start | bytes 116744 | tf_op jit(solution)/shard_map/ppermute | solution.py:473
